TPU v7x, 32 devices: a whole 2x2x4 slice. The times are simulated.
32 devices in a mesh: expert: 16 (over z, x, core), tensor: 2 (over y).
Axes of the slice: x: 2, y: 2, z: 4, core: 2. Of those that a mesh axis runs over, the one named last changes fastest.
Arguments:
- tokens: bfloat16 [2048, 2048], P('expert', 'tensor'), may hold values from -6 to 6
- cotangent: bfloat16 [2048, 2048], P('expert', 'tensor'), may hold values from -6 to 6
- route_ids: int32 [2048, 6], P('expert'), may hold values from 0 to 15, all different within a row
- route_weights: float32 [2048, 6], P('expert'), may hold values from 0.05 to 0.5
- shared_gate: bfloat16 [1408, 2048], P('tensor'), may hold values from -0.125 to 0.125
- shared_up: bfloat16 [1408, 2048], P('tensor'), may hold values from -0.125 to 0.125
- shared_down: bfloat16 [1408, 2048], P('tensor'), may hold values from -0.15625 to 0.15625
- expert_gate: bfloat16 [16, 1408, 2048], P('expert', 'tensor'), may hold values from -0.125 to 0.125
- expert_up: bfloat16 [16, 1408, 2048], P('expert', 'tensor'), may hold values from -0.125 to 0.125
- expert_down: bfloat16 [16, 1408, 2048], P('expert', 'tensor'), may hold values from -0.15625 to 0.15625
Outputs:
- layer_output: bfloat16 [2048, 2048], P('expert', 'tensor')
- input_grad: bfloat16 [2048, 2048], P('expert', 'tensor')
Inputs may be any that keep to these rules, and one draw needn't show every extreme that they name: `route_ids`: each row names 6 different experts.
All inputs are finite; a program needn't handle non-finite values.
Results may differ from a plain program's by a relative error of at most 0.0051.
Values may be sent and summed in bfloat16 or wider, within the bound.
No kernel may reach another device: no remote copies, remote signals or barrier semaphores. Data moves between devices by JAX's collectives and lax.ppermute only.
A program may use at most 64 MiB of HBM per device.

v0:
```python
import jax
import jax.numpy as jnp
from jax import lax
from jax.sharding import PartitionSpec as P


def silu_parts(pre_act):
    sigmoid_value = jax.nn.sigmoid(pre_act)
    return (pre_act * sigmoid_value, sigmoid_value * (1.0 + pre_act * (1.0 - sigmoid_value)))


def on_device(
    tokens,
    cotangent,
    route_ids,
    route_weights,
    shared_gate,
    shared_up,
    shared_down,
    expert_gate,
    expert_up,
    expert_down,
):
    expert_count = lax.axis_size("expert")
    tok_rows, top_count = route_ids.shape
    local_experts = expert_gate.shape[0]
    all_experts = local_experts * expert_count
    capacity = tok_rows * top_count // (2 * all_experts)
    slot_total = all_experts * capacity
    flat_ids = route_ids.reshape(-1)
    one_hot = (flat_ids[:, None] == jnp.arange(all_experts, dtype=jnp.int32)[None, :]).astype(
        jnp.int32
    )
    rank_in = jnp.sum((jnp.cumsum(one_hot, axis=0) - one_hot) * one_hot, axis=1)
    kept_mask = rank_in < capacity
    slot_index = jnp.where(kept_mask, flat_ids * capacity + rank_in, slot_total)
    slot_match = jnp.arange(slot_total, dtype=jnp.int32)[:, None] == slot_index[None, :]
    dispatch = jnp.any(slot_match.reshape(slot_total, tok_rows, top_count), axis=2).astype(
        jnp.bfloat16
    )
    gate_flat = route_weights.reshape(-1)
    slot_gate = jnp.sum(jnp.where(slot_match, gate_flat[None, :], 0.0), axis=1)
    gate_dispatch = dispatch.astype(jnp.float32) * slot_gate[:, None]
    x_full, c_full = (
        lax.all_gather(tokens, "tensor", axis=1, tiled=True),
        lax.all_gather(cotangent, "tensor", axis=1, tiled=True),
    )
    x_slots = jnp.dot(dispatch, tokens, preferred_element_type=jnp.float32).astype(jnp.bfloat16)
    g_slots = (
        slot_gate[:, None] * jnp.dot(dispatch, cotangent, preferred_element_type=jnp.float32)
    ).astype(jnp.bfloat16)
    x_part, g_part = (
        lax.all_to_all(x_slots, "expert", split_axis=0, concat_axis=0, tiled=True),
        lax.all_to_all(g_slots, "expert", split_axis=0, concat_axis=0, tiled=True),
    )
    x_recv, g_recv = (
        lax.all_gather(x_part, "tensor", axis=1, tiled=True),
        lax.all_gather(g_part, "tensor", axis=1, tiled=True),
    )

    def owner_layout(values):
        shaped = values.reshape(expert_count, local_experts, capacity, values.shape[-1])
        return shaped.transpose(1, 0, 2, 3).reshape(
            local_experts, expert_count * capacity, values.shape[-1]
        )

    def source_layout(values):
        shaped = values.reshape(local_experts, expert_count, capacity, values.shape[-1])
        return shaped.transpose(1, 0, 2, 3).reshape(slot_total, values.shape[-1])

    x_own = owner_layout(x_recv)
    g_own = owner_layout(g_recv)
    gate_pre = jnp.einsum("erd,efd->erf", x_own, expert_gate, preferred_element_type=jnp.float32)
    up_pre = jnp.einsum("erd,efd->erf", x_own, expert_up, preferred_element_type=jnp.float32)
    act_value, act_slope = silu_parts(gate_pre)
    hidden = (act_value * up_pre).astype(jnp.bfloat16)
    grad_hidden = jnp.einsum("erd,efd->erf", g_own, expert_down, preferred_element_type=jnp.float32)
    grad_gate = (grad_hidden * up_pre * act_slope).astype(jnp.bfloat16)
    grad_up = (grad_hidden * act_value).astype(jnp.bfloat16)
    value_part = source_layout(
        jnp.einsum("erf,efd->erd", hidden, expert_down, preferred_element_type=jnp.float32).astype(
            jnp.bfloat16
        )
    )
    grads_joined = jnp.concatenate((grad_gate, grad_up), axis=2)
    weights_joined = jnp.concatenate((expert_gate, expert_up), axis=1)
    input_term = jnp.einsum(
        "erf,efd->erd", grads_joined, weights_joined, preferred_element_type=jnp.float32
    )
    input_part = source_layout(input_term.astype(jnp.bfloat16))
    shared_gate_pre = jnp.einsum(
        "td,fd->tf", x_full, shared_gate, preferred_element_type=jnp.float32
    )
    shared_up_pre = jnp.einsum("td,fd->tf", x_full, shared_up, preferred_element_type=jnp.float32)
    shared_act, shared_slope = silu_parts(shared_gate_pre)
    shared_hidden = (shared_act * shared_up_pre).astype(jnp.bfloat16)
    shared_value = jnp.dot(shared_hidden, shared_down, preferred_element_type=jnp.float32)
    shared_grad_hidden = jnp.einsum(
        "td,fd->tf", c_full, shared_down, preferred_element_type=jnp.float32
    )
    shared_grad_gate = (shared_grad_hidden * shared_up_pre * shared_slope).astype(jnp.bfloat16)
    shared_grad_up = (shared_grad_hidden * shared_act).astype(jnp.bfloat16)
    shared_input = jnp.dot(shared_grad_gate, shared_gate, preferred_element_type=jnp.float32)
    shared_input = shared_input + jnp.dot(
        shared_grad_up, shared_up, preferred_element_type=jnp.float32
    )
    value_back, input_back = (
        lax.all_to_all(value_part, "expert", split_axis=0, concat_axis=0, tiled=True),
        lax.all_to_all(input_part, "expert", split_axis=0, concat_axis=0, tiled=True),
    )
    early_value = shared_value + jnp.einsum(
        "st,sd->td",
        gate_dispatch,
        value_back.astype(jnp.float32),
        precision=lax.Precision.HIGHEST,
        preferred_element_type=jnp.float32,
    )
    early_input = shared_input + jnp.einsum(
        "st,sd->td",
        dispatch,
        input_back,
        precision=lax.Precision.HIGHEST,
        preferred_element_type=jnp.float32,
    )
    value_total, input_total = (
        lax.psum_scatter(early_value, "tensor", scatter_dimension=1, tiled=True),
        lax.psum_scatter(early_input, "tensor", scatter_dimension=1, tiled=True),
    )
    return (value_total.astype(jnp.bfloat16), input_total.astype(jnp.bfloat16))


def solution(mesh):
    in_specs = (
        P("expert", "tensor"),
        P("expert", "tensor"),
        P("expert", None),
        P("expert", None),
        P("tensor", None),
        P("tensor", None),
        P("tensor", None),
        P("expert", "tensor", None),
        P("expert", "tensor", None),
        P("expert", "tensor", None),
    )
    out_specs = (P("expert", "tensor"), P("expert", "tensor"))
    return jax.shard_map(
        on_device, mesh=mesh, in_specs=in_specs, out_specs=out_specs, check_vma=False
    )
```

profile of v0, /device:TPU:0, one launch (start us, length us, event | category | flops | bytes accessed | tf_op | source)
XLA Modules:
  0.0 222.2 jit_solution(5177407489219410796)
XLA Ops:
  7.2 0.9 copy.19
  8.1 0.1 eq.50
  8.3 0.1 eq.46
  8.4 0.7 broadcast_multiply_fusion
  9.1 1.7 reduce-window.6
  10.8 0.3 slice_reduce_fusion
  11.1 0.1 fusion.35
  11.2 0.1 reduce_sum.21
  11.4 0.1 copy.23
  11.5 0.1 copy.24
  11.5 0.2 fusion.16
  11.7 2.3 %convolution_convert_fusion = bf16[384,1024]{1,0:T(8,128)(2,1)} fusion(pred[384,128]{1,0:T(8,128)(4,1)S(1)} %fusion.16, bf16[128,1024]{1,0:T(8,128)(2,1)} %param.10), kind=kOutput, calls=%fused_computation.18 | convolution fusion | flops 101056512 | bytes 1097728 | tf_op jit(solution)/shard_map/dot_general | solution.py:48
  14.0 7.4 %all-to-all-start = ((bf16[16,24,1024]{2,1,0:T(8,128)(2,1)}), bf16[16,24,1024]{2,1,0:T(8,128)(2,1)}, u32[]{:S(2)}, u32[]{:S(2)}) async-start(bf16[16,24,1024]{2,1,0:T(8,128)(2,1)} %bitcast.74), calls=%async_computation | async-start | bytes 1572864 | tf_op jit(solution)/shard_map/all_to_all | solution.py:53
  21.4 0.0 all-gather.3.cloned.1.call-start
  21.5 0.1 copy.25
  21.6 0.1 broadcast_in_dim.27
  21.7 0.2 select_reduce_fusion
  21.9 18.2 %all-to-all-done = bf16[16,24,1024]{2,1,0:T(8,128)(2,1)} async-done(((bf16[16,24,1024]{2,1,0:T(8,128)(2,1)}), bf16[16,24,1024]{2,1,0:T(8,128)(2,1)}, u32[]{:S(2)}, u32[]{:S(2)}) %all-to-all-start) | async-done | bytes 786464 | tf_op jit(solution)/shard_map/all_to_all | solution.py:53
  40.2 0.0 all-gather.5.cloned.1.call-start
  40.2 0.4 multiply_convert_fusion
  40.6 25.4 %all_to_all.48 = bf16[16,24,1024]{2,1,0:T(8,128)(2,1)} all-to-all(bf16[16,24,1024]{2,1,0:T(8,128)(2,1)S(1)} %bitcast.76), channel_id=1, replica_groups=mesh['expert'=16,'tensor'=2] {'expert'}, dimensions={0} | all-to-all | bytes 1572864 | tf_op jit(solution)/shard_map/all_to_all | solution.py:54
  66.0 2.2 %all-gather.3.cloned.1.call-done = bf16[384,2048]{1,0:T(8,128)(2,1)} async-done(((bf16[384,1024]{1,0:T(8,128)(2,1)}), bf16[384,2048]{1,0:T(8,128)(2,1)}) %all-gather.3.cloned.1.call-update) | async-done | bytes 1572880 | tf_op jit(solution)/shard_map/all_gather | solution.py:57
  68.3 5.1 %fusion.7 = f32[384,704]{0,1:T(8,128)} fusion(bf16[384,2048]{1,0:T(8,128)(2,1)} %all-gather.3.cloned.1.call-done, bf16[1,704,2048]{2,1,0:T(8,128)(2,1)} %param.18), kind=kOutput, calls=%fused_computation.8 | convolution fusion | flops 1107296256 | bytes 5537792 | tf_op jit(solution)/shard_map/erd,efd->erf/dot_general | solution.py:74
  73.4 2.7 %fusion.9 = f32[384,704]{0,1:T(8,128)} fusion(bf16[384,2048]{1,0:T(8,128)(2,1)S(1)} %copy-done.15, bf16[1,704,2048]{2,1,0:T(8,128)(2,1)S(1)} %copy-done.13), kind=kOutput, calls=%fused_computation.10 | convolution fusion | flops 1107296256 | bytes 5537792 | tf_op jit(solution)/shard_map/erd,efd->erf/dot_general | solution.py:73
  76.0 21.0 %all-gather.5.cloned.1.call-done = bf16[384,2048]{1,0:T(8,128)(2,1)} async-done(((bf16[384,1024]{1,0:T(8,128)(2,1)}), bf16[384,2048]{1,0:T(8,128)(2,1)}) %all-gather.5.cloned.1.call-update) | async-done | bytes 1572880 | tf_op jit(solution)/shard_map/all_gather | solution.py:58
  97.0 4.1 %fusion.21 = (bf16[1,384,704]{1,2,0:T(8,128)(2,1)S(1)}, bf16[1,384,704]{1,2,0:T(8,128)(2,1)S(1)}) fusion(f32[384,704]{0,1:T(8,128)} %fusion.9, f32[384,704]{0,1:T(8,128)} %fusion.7, bf16[384,2048]{1,0:T(8,128)(2,1)} %all-gather.5.cloned.1.call-done, bf16[1,704,2048]{2,1,0:T(8,128)(2,1)S(1)} %copy-done), kind=kOutput, calls=%fused_computation.32 | convolution fusion | flops 1110810624 | bytes 7700480 | tf_op jit(solution)/shard_map/erd,efd->erf/dot_general | solution.py:77
  101.2 3.7 %fusion.14 = bf16[384,2048]{1,0:T(8,128)(2,1)} fusion(bf16[1,704,2048]{2,1,0:T(8,128)(2,1)S(1)} %copy-done.12, bf16[1,704,2048]{2,1,0:T(8,128)(2,1)S(1)} %copy-done.14, bf16[1,384,704]{1,2,0:T(8,128)(2,1)S(1)} %get-tuple-element.3, bf16[1,384,704]{1,2,0:T(8,128)(2,1)S(1)} %get-tuple-element.2), kind=kOutput, calls=%fused_computation.13 | convolution fusion | flops 2229075968 | bytes 8421376 | tf_op jit(solution)/shard_map/erf,efd->erd/dot_general | solution.py:87
  104.9 5.8 %all-to-all-start.3 = ((bf16[16,24,2048]{2,1,0:T(8,128)(2,1)}), bf16[16,24,2048]{2,1,0:T(8,128)(2,1)}, u32[]{:S(2)}, u32[]{:S(2)}) async-start(bf16[16,24,2048]{2,1,0:T(8,128)(2,1)} %bitcast.78), calls=%async_computation.4 | async-start | bytes 3145728 | tf_op jit(solution)/shard_map/all_to_all | solution.py:109
  110.7 9.2 %all_gather.12 = bf16[128,2048]{1,0:T(8,128)(2,1)S(1)} all-gather(bf16[128,1024]{1,0:T(8,128)(2,1)S(1)} %copy-done.7), channel_id=1, replica_groups=mesh['expert'=16,'tensor'=2] {'tensor'}, dimensions={1}, use_global_device_ids=true | all-gather | bytes 786432 | tf_op jit(solution)/shard_map/all_gather | solution.py:45
  120.0 0.8 copy-done.4
  120.8 2.9 %fusion.44 = f32[128,704]{0,1:T(8,128)S(1)} fusion(bf16[128,2048]{1,0:T(8,128)(2,1)S(1)} %all_gather.12, bf16[704,2048]{1,0:T(8,128)(2,1)} %param.14), kind=kOutput, calls=%fused_computation.62 | convolution fusion | flops 369098752 | bytes 3768320 | tf_op jit(solution)/shard_map/td,fd->tf/dot_general | solution.py:91
  123.7 2.7 %fusion.11 = bf16[384,2048]{1,0:T(8,128)(2,1)} fusion(bf16[1,704,2048]{2,1,0:T(8,128)(2,1)S(1)} %copy-done, f32[384,704]{0,1:T(8,128)S(1)} %copy-done.16, f32[384,704]{0,1:T(8,128)S(1)} %copy-done.17), kind=kOutput, calls=%fused_computation.12 | convolution fusion | flops 1109704704 | bytes 6619136 | tf_op jit(solution)/shard_map/erf,efd->erd/dot_general | solution.py:81
  126.4 16.3 %all-to-all-done.3 = bf16[16,24,2048]{2,1,0:T(8,128)(2,1)} async-done(((bf16[16,24,2048]{2,1,0:T(8,128)(2,1)}), bf16[16,24,2048]{2,1,0:T(8,128)(2,1)}, u32[]{:S(2)}, u32[]{:S(2)}) %all-to-all-start.3) | async-done | bytes 1572896 | tf_op jit(solution)/shard_map/all_to_all | solution.py:109
  142.6 9.2 %all-to-all-start.1 = ((bf16[16,24,2048]{2,1,0:T(8,128)(2,1)}), bf16[16,24,2048]{2,1,0:T(8,128)(2,1)}, u32[]{:S(2)}, u32[]{:S(2)}) async-start(bf16[16,24,2048]{2,1,0:T(8,128)(2,1)} %bitcast.77), calls=%async_computation.1 | async-start | bytes 3145728 | tf_op jit(solution)/shard_map/all_to_all | solution.py:108
  151.9 3.0 %fusion.45 = f32[128,704]{0,1:T(8,128)S(1)} fusion(bf16[128,2048]{1,0:T(8,128)(2,1)} %copy-done.4, bf16[704,2048]{1,0:T(8,128)(2,1)} %param.15), kind=kOutput, calls=%fused_computation.63 | convolution fusion | flops 369098752 | bytes 3768320 | tf_op jit(solution)/shard_map/td,fd->tf/dot_general | solution.py:94
  154.9 9.4 %all_gather.14 = bf16[128,2048]{1,0:T(8,128)(2,1)S(1)} all-gather(bf16[128,1024]{1,0:T(8,128)(2,1)S(1)} %copy-done.8), channel_id=1, replica_groups=mesh['expert'=16,'tensor'=2] {'tensor'}, dimensions={1}, use_global_device_ids=true | all-gather | bytes 786432 | tf_op jit(solution)/shard_map/all_gather | solution.py:46
  164.3 0.9 fusion.46
  165.3 0.9 copy-done.2
  166.2 0.7 fusion.27
  166.9 2.0 fusion.47
  168.9 1.6 fusion.15
  170.6 13.1 %all-to-all-done.1 = bf16[16,24,2048]{2,1,0:T(8,128)(2,1)} async-done(((bf16[16,24,2048]{2,1,0:T(8,128)(2,1)}), bf16[16,24,2048]{2,1,0:T(8,128)(2,1)}, u32[]{:S(2)}, u32[]{:S(2)}) %all-to-all-start.1) | async-done | bytes 1572896 | tf_op jit(solution)/shard_map/all_to_all | solution.py:108
  183.7 2.6 %fusion.23 = f32[128,2048]{1,0:T(8,128)S(1)} fusion(bf16[384,2048]{1,0:T(8,128)(2,1)} %bitcast.7, f32[384]{0:T(512)S(1)} %copy-done.10, pred[384,128]{1,0:T(8,128)(4,1)S(1)} %fusion.16), kind=kOutput, calls=%fused_computation.38 | convolution fusion | flops 1208107008 | bytes 2672128 | tf_op jit(solution)/shard_map/st,sd->td/dot_general | solution.py:111
  186.3 3.4 %convolution_add_fusion.1 = f32[128,2048]{1,0:T(8,128)} fusion(f32[128,2048]{1,0:T(8,128)S(1)} %fusion.23, bf16[704,2048]{1,0:T(8,128)(2,1)} %param.16, f32[128,704]{0,1:T(8,128)S(1)} %copy-done.6, f32[128,704]{0,1:T(8,128)S(1)} %fusion.44), kind=kOutput, calls=%fused_computation.15 | convolution fusion | flops 369901568 | bytes 5701632 | tf_op jit(solution)/shard_map/dot_general | solution.py:97
  189.7 1.5 reduce-scatter.5.cloned.1.call-done
  191.2 1.8 convert_element_type.76
  193.0 20.9 %reduce-scatter.3.cloned.1.call-done = f32[128,1024]{1,0:T(8,128)} async-done(((f32[128,2048]{1,0:T(8,128)}), f32[128,1024]{1,0:T(8,128)}) %reduce-scatter.3.cloned.1.call-update) | async-done | bytes 524304 | tf_op jit(solution)/shard_map/reduce_scatter | solution.py:126
  213.9 1.8 convert_element_type.67
  (44 shorter events, 0.3 us)
Async XLA Ops:
  7.2 89.9 %copy-start = (bf16[1,704,2048]{2,1,0:T(8,128)(2,1)S(1)}, bf16[1,704,2048]{2,1,0:T(8,128)(2,1)}, u32[]{:S(2)}) copy-start(bf16[1,704,2048]{2,1,0:T(8,128)(2,1)} %param.19) | copy-start | bytes 8650756
  11.2 10.3 %copy-start.11 = (f32[128,6]{0,1:T(8,128)S(1)}, f32[128,6]{0,1:T(8,128)}, u32[]{:S(2)}) copy-start(f32[128,6]{0,1:T(8,128)} %param.13) | copy-start | bytes 9220
  11.7 28.5 %copy-start.8 = (bf16[128,1024]{1,0:T(8,128)(2,1)S(1)}, bf16[128,1024]{1,0:T(8,128)(2,1)}, u32[]{:S(2)}) copy-start(bf16[128,1024]{1,0:T(8,128)(2,1)} %param.11) | copy-start | bytes 786436
  14.0 26.2 %all-to-all-start = ((bf16[16,24,1024]{2,1,0:T(8,128)(2,1)}), bf16[16,24,1024]{2,1,0:T(8,128)(2,1)}, u32[]{:S(2)}, u32[]{:S(2)}) async-start(bf16[16,24,1024]{2,1,0:T(8,128)(2,1)} %bitcast.74), calls=%async_computation | async-start | bytes 1572864 | tf_op jit(solution)/shard_map/all_to_all | solution.py:53
  21.4 46.9 %all-gather.3.cloned.1.call-start = ((), (), s32[]{:S(2)}) async-start(), calls=%async_computation.6 | async-start | bytes 2359296 | tf_op jit(solution)/shard_map/all_gather | solution.py:57
  21.9 44.1 %copy-start.9 = (f32[384]{0:T(512)}, f32[384]{0:T(512)S(1)}, u32[]{:S(2)}) copy-start(f32[384]{0:T(512)S(1)} %select_reduce_fusion) | copy-start | bytes 4612
  40.2 56.9 %all-gather.5.cloned.1.call-start = ((), (), s32[]{:S(2)}) async-start(), calls=%async_computation.8 | async-start | bytes 2359296 | tf_op jit(solution)/shard_map/all_gather | solution.py:58
  68.3 5.1 %copy-start.13 = (bf16[1,704,2048]{2,1,0:T(8,128)(2,1)S(1)}, bf16[1,704,2048]{2,1,0:T(8,128)(2,1)}, u32[]{:S(2)}) copy-start(bf16[1,704,2048]{2,1,0:T(8,128)(2,1)} %param.17) | copy-start | bytes 8650756
  68.3 5.1 %copy-start.15 = (bf16[384,2048]{1,0:T(8,128)(2,1)S(1)}, bf16[384,2048]{1,0:T(8,128)(2,1)}, u32[]{:S(2)}) copy-start(bf16[384,2048]{1,0:T(8,128)(2,1)} %all-gather.3.cloned.1.call-done) | copy-start | bytes 4718596
  97.0 4.1 %copy-start.12 = (bf16[1,704,2048]{2,1,0:T(8,128)(2,1)S(1)}, bf16[1,704,2048]{2,1,0:T(8,128)(2,1)}, u32[]{:S(2)}) copy-start(bf16[1,704,2048]{2,1,0:T(8,128)(2,1)} %param.18) | copy-start | bytes 8650756
  97.0 4.2 %copy-start.14 = (bf16[1,704,2048]{2,1,0:T(8,128)(2,1)S(1)}, bf16[1,704,2048]{2,1,0:T(8,128)(2,1)}, u32[]{:S(2)}) copy-start(bf16[1,704,2048]{2,1,0:T(8,128)(2,1)} %param.17) | copy-start | bytes 8650756
  104.9 5.8 %copy-start.7 = (bf16[128,1024]{1,0:T(8,128)(2,1)S(1)}, bf16[128,1024]{1,0:T(8,128)(2,1)}, u32[]{:S(2)}) copy-start(bf16[128,1024]{1,0:T(8,128)(2,1)} %param.10) | copy-start | bytes 786436
  104.9 37.7 %all-to-all-start.3 = ((bf16[16,24,2048]{2,1,0:T(8,128)(2,1)}), bf16[16,24,2048]{2,1,0:T(8,128)(2,1)}, u32[]{:S(2)}, u32[]{:S(2)}) async-start(bf16[16,24,2048]{2,1,0:T(8,128)(2,1)} %bitcast.78), calls=%async_computation.4 | async-start | bytes 3145728 | tf_op jit(solution)/shard_map/all_to_all | solution.py:109
  120.0 0.8 copy-start.4
  120.8 2.9 %copy-start.16 = (f32[384,704]{0,1:T(8,128)S(1)}, f32[384,704]{0,1:T(8,128)}, u32[]{:S(2)}) copy-start(f32[384,704]{0,1:T(8,128)} %fusion.7) | copy-start | bytes 3244036
  120.8 2.9 %copy-start.17 = (f32[384,704]{0,1:T(8,128)S(1)}, f32[384,704]{0,1:T(8,128)}, u32[]{:S(2)}) copy-start(f32[384,704]{0,1:T(8,128)} %fusion.9) | copy-start | bytes 3244036
  142.6 41.1 %all-to-all-start.1 = ((bf16[16,24,2048]{2,1,0:T(8,128)(2,1)}), bf16[16,24,2048]{2,1,0:T(8,128)(2,1)}, u32[]{:S(2)}, u32[]{:S(2)}) async-start(bf16[16,24,2048]{2,1,0:T(8,128)(2,1)} %bitcast.77), calls=%async_computation.1 | async-start | bytes 3145728 | tf_op jit(solution)/shard_map/all_to_all | solution.py:108
  151.8 39.4 %reduce-scatter.5.cloned.1.call-start = ((), (), s32[]{:S(2)}) async-start(), calls=%async_computation.9 | async-start | bytes 1572864 | tf_op jit(solution)/shard_map/reduce_scatter | solution.py:127
  151.8 12.5 %copy-start.3 = (bf16[704,2048]{1,0:T(8,128)(2,1)S(1)}, bf16[704,2048]{1,0:T(8,128)(2,1)}, u32[]{:S(2)}) copy-start(bf16[704,2048]{1,0:T(8,128)(2,1)} %param.16) | copy-start | bytes 8650756
  154.9 10.4 %copy-start.5 = (f32[128,704]{0,1:T(8,128)}, f32[128,704]{0,1:T(8,128)S(1)}, u32[]{:S(2)}) copy-start(f32[128,704]{0,1:T(8,128)S(1)} %fusion.45) | copy-start | bytes 1081348
  164.3 1.8 copy-start.2
  166.2 2.8 %copy-start.1 = (bf16[704,2048]{1,0:T(8,128)(2,1)S(1)}, bf16[704,2048]{1,0:T(8,128)(2,1)}, u32[]{:S(2)}) copy-start(bf16[704,2048]{1,0:T(8,128)(2,1)} %param.15) | copy-start | bytes 8650756
  168.9 14.8 %copy-start.10 = (f32[384]{0:T(512)S(1)}, f32[384]{0:T(512)}, u32[]{:S(2)}) copy-start(f32[384]{0:T(512)} %copy-done.9) | copy-start | bytes 4612
  170.6 43.3 %reduce-scatter.3.cloned.1.call-start = ((), (), s32[]{:S(2)}) async-start(), calls=%async_computation.7 | async-start | bytes 1572864 | tf_op jit(solution)/shard_map/reduce_scatter | solution.py:126
  183.7 2.6 %copy-start.6 = (f32[128,704]{0,1:T(8,128)S(1)}, f32[128,704]{0,1:T(8,128)}, u32[]{:S(2)}) copy-start(f32[128,704]{0,1:T(8,128)} %copy-done.5) | copy-start | bytes 1081348
Sparse Core Ops, SparseCore 0:
  40.3 27.9 all-gather.2
  69.8 27.1 all-gather.4
  170.7 20.4 reduce-scatter.4
  193.3 20.5 reduce-scatter.2
where the time goes:
time: 223 us; the launch traced here: 222 us
  waiting for transfers between devices  93.2 us (42%)
  blocking collectives  44.1 us (20%)
  matrix products  38.1 us (17%)
  starting transfers between devices  22.5 us (10%)
  between operations  14 us (6%)
  other arithmetic  6.47 us (3%)
  local copies, waits for them, and re-layouts  3.77 us (2%)
    all_to_all x1, blocking collectives, on_device(): lax.all_to_all(g_slots, 'expert', split_axis=0, concat_axis=0, tiled=True)  25.4 us
    all_gather x1, waiting for transfers between devices, on_device(): lax.all_gather(g_part, 'tensor', axis=1, tiled=True)  21 us
    reduce_scatter x1, waiting for transfers between devices, on_device(): lax.psum_scatter(early_value, 'tensor', scatter_dimension=1, tiled=True)  20.9 us
    all_to_all x1, waiting for transfers between devices, on_device(): lax.all_to_all(x_slots, 'expert', split_axis=0, concat_axis=0, tiled=True)  18.2 us
    all_to_all x1, waiting for transfers between devices, on_device(): lax.all_to_all(input_part, 'expert', split_axis=0, concat_axis=0, tiled=T...  16.3 us
    all_to_all x1, waiting for transfers between devices, on_device(): lax.all_to_all(value_part, 'expert', split_axis=0, concat_axis=0, tiled=T...  13.1 us
    all_gather x1, blocking collectives, on_device(): lax.all_gather(cotangent, 'tensor', axis=1, tiled=True)  9.42 us
    all_gather x1, blocking collectives, on_device(): lax.all_gather(tokens, 'tensor', axis=1, tiled=True)  9.24 us
  transfers between devices with their start and end apart: 7, of which 7 were waited for; matrix products, arithmetic and copies ran while one was open for 14% of the time, Pallas kernels for 0%

commit v1 on v0

--- a/solution.py
+++ b/solution.py
@@ -1,12 +1,426 @@
+import math
+
 import jax
 import jax.numpy as jnp
 from jax import lax
+from jax.experimental import pallas as pl
+from jax.experimental.pallas import tpu as pltpu
 from jax.sharding import PartitionSpec as P
+
+
+BF = jnp.bfloat16
+F32 = jnp.float32
+ROWS_BY_ROWS = (((1,), (1,)), ((), ()))
 
 
 def silu_parts(pre_act):
     sigmoid_value = jax.nn.sigmoid(pre_act)
     return (pre_act * sigmoid_value, sigmoid_value * (1.0 + pre_act * (1.0 - sigmoid_value)))
+
+
+def mm(a, b):
+    return jnp.dot(a, b, preferred_element_type=F32)
+
+
+def mmt(a, b):
+    return lax.dot_general(a, b, ROWS_BY_ROWS, preferred_element_type=F32)
+
+
+def local_call(body, scalars, arrays, outs, flops=0, staged=0, grant=20, keep=0):
+    count = len(arrays)
+
+    def kernel(*refs):
+        scalar_ref, ins = refs[0], refs[1 : count + 1]
+        out_refs = refs[count + 1 : count + 1 + len(outs)]
+        sem = refs[-1]
+        bufs = list(refs[count + 1 + len(outs) :][: staged - keep])
+        bufs += out_refs[len(outs) - keep :] if keep else ()
+        copies = [pltpu.make_async_copy(ins[i], bufs[i], sem.at[i]) for i in range(staged)]
+        for copy in copies:
+            copy.start()
+
+        def ready(*which):
+            for i in which:
+                copies[i].wait()
+
+        body(scalar_ref, bufs + list(ins[staged:]), out_refs, ready)
+
+    arrays = [
+        pltpu.with_memory_space_constraint(a, pltpu.HBM) if i < staged else a
+        for i, a in enumerate(arrays)
+    ]
+    moved = sum(math.prod(a.shape) * a.dtype.itemsize for a in arrays)
+    moved += sum(math.prod(o.shape) * o.dtype.itemsize for o in outs)
+    whole = pl.BlockSpec(memory_space=pltpu.VMEM)
+    return pl.pallas_call(
+        kernel,
+        out_shape=list(outs),
+        in_specs=[pl.BlockSpec(memory_space=pltpu.SMEM)]
+        + [pl.BlockSpec(memory_space=pltpu.HBM)] * staged
+        + [whole] * (count - staged),
+        out_specs=[whole] * len(outs),
+        scratch_shapes=[pltpu.VMEM(a.shape, a.dtype) for a in arrays[: staged - keep]]
+        + [pltpu.SemaphoreType.DMA((max(staged, 1),))],
+        compiler_params=pltpu.CompilerParams(vmem_limit_bytes=grant << 20),
+        cost_estimate=pl.CostEstimate(flops=flops, bytes_accessed=moved, transcendentals=0),
+    )(scalars, *arrays)
+
+
+def shaped(shape, dtype=BF):
+    return jax.ShapeDtypeStruct(shape, dtype)
+
+
+def prep(scalars, ids_t, wts_t, tokens, cotangent, experts, cap, near_chips):
+    tok_rows, half = tokens.shape
+    top_count = ids_t.shape[0]
+    slots = experts * cap
+    far = experts // 2 - near_chips
+
+    def body(scalar_ref, bufs, outs, ready):
+        ids_ref, wts_ref, tok_ref, cot_ref = bufs
+        core_out, dm_out, gm_out = outs[far : far + 3]
+        row = lax.broadcasted_iota(jnp.int32, (slots, 1), 0)
+        k = ((row.astype(F32) + 0.5) * (1.0 / cap)).astype(jnp.int32)
+        place = (row - k * cap).astype(F32)
+        expert = jnp.bitwise_xor(k, scalar_ref[0])
+        before = lax.broadcasted_iota(jnp.int32, (tok_rows, tok_rows), 0)
+        after = lax.broadcasted_iota(jnp.int32, (tok_rows, tok_rows), 1)
+        earlier = jnp.where(before < after, 1.0, 0.0).astype(BF)
+        ready(0, 1)
+        named = jnp.zeros((slots, tok_rows), F32)
+        gate = jnp.zeros((slots, tok_rows), F32)
+        for i in range(top_count):
+            hit = ids_ref[i : i + 1, :] == expert
+            named = jnp.where(hit, 1.0, named)
+            gate = jnp.where(hit, wts_ref[i : i + 1, :], gate)
+        rank = mm(named.astype(BF), earlier)
+        kept = (named > 0.5) & (rank == place)
+        dm = jnp.where(kept, 1.0, 0.0)
+        gm = jnp.where(kept, gate, 0.0)
+        dmb = dm.astype(BF)
+        slot_gate = jnp.sum(gm, axis=1, keepdims=True)
+        dm_out[...] = dm
+        gm_out[...] = gm
+        first = 2 * near_chips * cap
+        ready(2)
+        x_rows = mm(dmb[first:], tok_ref[...])
+        ready(3)
+        g_rows = slot_gate[first:] * mm(dmb[first:], cot_ref[...])
+        for q in range(far):
+            for b in range(2):
+                low = (2 * q + b) * cap
+                both = jnp.concatenate((x_rows[low : low + cap], g_rows[low : low + cap]), 0)
+                if b:
+                    core_out[2 * cap * q : 2 * cap * (q + 1), :] = both.astype(BF)
+                else:
+                    outs[q][...] = both.astype(BF)
+
+    outs = local_call(
+        body,
+        scalars,
+        (ids_t, wts_t, tokens, cotangent),
+        [shaped((2 * cap, half))] * far
+        + [
+            shaped((far * 2 * cap, half)),
+            shaped((slots, tok_rows), F32),
+            shaped((slots, tok_rows), F32),
+            shaped(tokens.shape),
+            shaped(cotangent.shape),
+        ],
+        flops=4 * slots * tok_rows * half,
+        staged=4,
+        grant=20,
+        keep=2,
+    )
+    return outs[:far], outs[far:]
+
+
+def gate_tables(scalars, dm, gm, cap, near_chips):
+    slots, tok_rows = dm.shape
+    near = 2 * near_chips * cap
+
+    def body(_, bufs, outs, ready):
+        blank = jnp.zeros((cap, tok_rows), F32)
+        for out, low, high in ((outs[0], 0, near), (outs[1], near, slots)):
+            gates, picks = [], []
+            for k in range(low, high, cap):
+                gates += [bufs[1][k : k + cap, :], blank]
+                picks += [blank, bufs[0][k : k + cap, :]]
+            gate = jnp.transpose(jnp.concatenate(gates, 0))
+            one = gate.astype(BF)
+            left = gate - one.astype(F32)
+            two = left.astype(BF)
+            out[0:tok_rows] = one
+            out[tok_rows : 2 * tok_rows] = two
+            out[2 * tok_rows : 3 * tok_rows] = (left - two.astype(F32)).astype(BF)
+            out[3 * tok_rows :] = jnp.transpose(jnp.concatenate(picks, 0)).astype(BF)
+
+    return local_call(
+        body,
+        scalars,
+        (dm, gm),
+        (shaped((4 * tok_rows, 2 * near)), shaped((4 * tok_rows, 2 * (slots - near)))),
+    )
+
+
+def near_rows(scalars, dm, gm, tokens, tokens_other, cotangent, cotangent_other, cap, chips):
+    tok_rows, half = tokens.shape
+    near = 2 * chips * cap
+
+    def body(_, bufs, outs, ready):
+        t_own, c_own, dm_ref, gm_ref, t_oth, c_oth = bufs
+        dmb = dm_ref[0:near, :].astype(BF)
+        slot_gate = jnp.sum(gm_ref[0:near, :], axis=1, keepdims=True)
+        for h, (t_ref, c_ref) in enumerate(((t_own, c_own), (t_oth, c_oth))):
+            x_rows = mm(dmb, t_ref[...])
+            g_rows = slot_gate * mm(dmb, c_ref[...])
+            for q in range(chips):
+                for b in range(2):
+                    low = (2 * q + b) * cap
+                    both = jnp.concatenate((x_rows[low : low + cap], g_rows[low : low + cap]), 0)
+                    outs[b][q, h] = both.astype(BF)
+
+    return local_call(
+        body,
+        scalars,
+        (tokens, cotangent, dm, gm, tokens_other, cotangent_other),
+        [shaped((chips, 2, 2 * cap, half))] * 2,
+        flops=8 * near * tok_rows * half,
+    )
+
+
+def ffn(scalar_ref, xs, gs, weight_refs):
+    half = xs[0].shape[1]
+    gate_w, up_w, down_w = (
+        [
+            w.at[:, pl.ds(pl.multiple_of(jnp.bitwise_xor(scalar_ref[1], i) * half, half), half)]
+            for i in range(2)
+        ]
+        for w in weight_refs
+    )
+    gate_pre = mmt(xs[0], gate_w[0][...]) + mmt(xs[1], gate_w[1][...])
+    up_pre = mmt(xs[0], up_w[0][...]) + mmt(xs[1], up_w[1][...])
+    act, slope = silu_parts(gate_pre)
+    hidden = (act * up_pre).astype(BF)
+    grad_hidden = mmt(gs[0], down_w[0][...]) + mmt(gs[1], down_w[1][...])
+    grad_gate = (grad_hidden * up_pre * slope).astype(BF)
+    grad_up = (grad_hidden * act).astype(BF)
+    values = [mm(hidden, down_w[i][...]) for i in range(2)]
+    inputs = [mm(grad_gate, gate_w[i][...]) + mm(grad_up, up_w[i][...]) for i in range(2)]
+    return values, inputs
+
+
+def ffn_flops(rows, weights):
+    return 12 * rows * weights[0].shape[0] * weights[0].shape[1]
+
+
+def routed_ffn(scalars, near, far, other, weights, cap):
+    arrays = list(near) + list(far) + ([other] if far else [])
+    count = len(near) + len(far)
+
+    def body(scalar_ref, bufs, outs, ready):
+        def views(refs):
+            pairs = [(r.at[0], r.at[1]) for r in refs[: len(near)]]
+            rest = refs[len(near) :]
+            return pairs + [(rest[i], rest[len(far)].at[i]) for i in range(len(far))]
+
+        def pick(h, part):
+            segments = []
+            for pair in views(bufs[: len(arrays)]):
+                block = pair[h][...].astype(F32)
+                for b in range(2):
+                    low = (2 * b + part) * cap
+                    segments.append(block[low : low + cap])
+            return jnp.concatenate(segments, 0).astype(BF)
+
+        xs = [pick(0, 0), pick(1, 0)]
+        gs = [pick(0, 1), pick(1, 1)]
+        values, inputs = ffn(scalar_ref, xs, gs, bufs[len(arrays) :])
+        for n, pair in enumerate(views(outs)):
+            for h in range(2):
+                segments = []
+                for b in range(2):
+                    low = (2 * n + b) * cap
+                    segments += [values[h][low : low + cap], inputs[h][low : low + cap]]
+                pair[h][...] = jnp.concatenate(segments, 0).astype(BF)
+
+    outs = local_call(
+        body,
+        scalars,
+        arrays + list(weights),
+        [shaped(a.shape) for a in arrays],
+        flops=ffn_flops(2 * cap * count, weights),
+    )
+    return outs if near else (outs[:-1], outs[-1])
+
+
+def shared_ffn(scalars, tokens, tokens_other, cotangent, cotangent_other, weights):
+    tok_rows, half = tokens.shape
+
+    def body(scalar_ref, bufs, outs, ready):
+        xs = [bufs[0][...], bufs[2][...]]
+        gs = [bufs[1][...], bufs[3][...]]
+        values, inputs = ffn(scalar_ref, xs, gs, bufs[4:])
+        for h in range(2):
+            outs[h][0] = values[h]
+            outs[h][1] = inputs[h]
+
+    return local_call(
+        body,
+        scalars,
+        (tokens, cotangent, tokens_other, cotangent_other, *weights),
+        [shaped((2, tok_rows, half), F32)] * 2,
+        flops=ffn_flops(tok_rows, weights),
+    )
+
+
+def combine(table, blocks):
+    tok_rows = table.shape[0] // 4
+    sums = mm(table[...], jnp.concatenate(blocks, 0))
+    parts = [sums[i * tok_rows : (i + 1) * tok_rows] for i in range(4)]
+    return parts[0] + parts[1] + parts[2], parts[3]
+
+
+def near_combine(scalars, table, own, core0, core, shared_own, shared_other, cap):
+    _, tok_rows, half = shared_own.shape
+    near = len(own)
+
+    def body(_, bufs, outs, ready):
+        table_ref, core0_ref, core_ref, s_own, s_oth = bufs[:5]
+        for h, shared in enumerate((s_own, s_oth)):
+            blocks = []
+            for q in range(near):
+                partner = core_ref[q - 1, h, 2 * cap :] if q else core0_ref[h, 2 * cap :]
+                blocks += [bufs[5 + q][h, : 2 * cap], partner]
+            value, grad = combine(table_ref, blocks)
+            outs[h][0] = (shared[0] + value).astype(outs[h].dtype)
+            outs[h][1] = (shared[1] + grad).astype(outs[h].dtype)
+
+    return local_call(
+        body,
+        scalars,
+        (table, core0, core, shared_own, shared_other, *own),
+        (shaped((2, tok_rows, half), F32), shaped((2, tok_rows, half))),
+        flops=64 * tok_rows * near * cap * half,
+    )
+
+
+def far_combine(scalars, table, base, partner, own, core, cap):
+    _, tok_rows, half = base.shape
+    far = len(own)
+
+    def body(_, bufs, outs, ready):
+        table_ref, base_ref, partner_ref = bufs[:3]
+        received = bufs[3:]
+        blocks = []
+        for q in range(far):
+            blocks += [received[q][: 2 * cap], received[far + q][2 * cap :]]
+        sums = combine(table_ref, blocks)
+        for i in range(2):
+            outs[i][...] = (base_ref[i] + partner_ref[i].astype(F32) + sums[i]).astype(BF)
+
+    return local_call(
+        body,
+        scalars,
+        (table, base, partner, *own, *core),
+        [shaped((tok_rows, half))] * 2,
+        flops=32 * tok_rows * far * cap * half,
+    )
+
+
+def paired(*args):
+    return paired_steps(*args)
+
+
+def paired_steps(
+    tokens,
+    cotangent,
+    route_ids,
+    route_weights,
+    shared_gate,
+    shared_up,
+    shared_down,
+    expert_gate,
+    expert_up,
+    expert_down,
+):
+    experts = lax.axis_size("expert")
+    tok_rows, top_count = route_ids.shape
+    cap = tok_rows * top_count // (2 * experts)
+    scalars = jnp.stack([lax.axis_index("expert"), lax.axis_index("tensor")]).astype(jnp.int32)
+    routed = (expert_gate[0], expert_up[0], expert_down[0])
+    shared = (shared_gate, shared_up, shared_down)
+
+    def across(values):
+        return lax.ppermute(values, "tensor", [(0, 1), (1, 0)])
+
+    def exchange(values, k):
+        return lax.ppermute(values, "expert", [(i, i ^ k) for i in range(experts)])
+
+    def joined(own, core):
+        return jnp.concatenate((own, core), axis=own.ndim - 2)
+
+    chips, near_chips = experts // 2, experts // 4
+    own_far, rest = prep(
+        scalars, route_ids.T, route_weights.T, tokens, cotangent, experts, cap, near_chips
+    )
+    core_far, dm, gm, tokens_here, cotangent_here = rest
+    tokens_other = across(tokens)
+    cotangent_other = across(cotangent)
+    core_back = exchange(core_far, 1)
+    arrived = {}
+    for q in range(near_chips, chips):
+        rows = slice((q - near_chips) * 2 * cap, (q - near_chips + 1) * 2 * cap)
+        arrived[q] = exchange(joined(own_far[q - near_chips], core_back[rows]), 2 * q)
+    near_own, near_out = near_rows(
+        scalars, dm, gm, tokens_here, tokens_other, cotangent_here, cotangent_other, cap, near_chips
+    )
+    near_back = exchange(near_out, 1)
+    near_table, far_table = gate_tables(scalars, dm, gm, cap, near_chips)
+    near = [joined(near_own[q], near_back[q]) for q in range(near_chips)]
+    near = near[:1] + [exchange(near[q], 2 * q) for q in range(1, near_chips)]
+    shared_own, shared_other = shared_ffn(
+        scalars, tokens_here, tokens_other, cotangent_here, cotangent_other, shared
+    )
+    out = routed_ffn(scalars, near, (), None, routed, cap)
+    home = list(out[:1]) + [exchange(out[q], 2 * q) for q in range(1, near_chips)]
+    core0 = exchange(home[0], 1)
+    joint = jnp.stack(home[1:])
+    core1 = exchange(joint, 1)
+    base, partial = near_combine(
+        scalars, near_table, home, core0, core1, shared_own, shared_other, cap
+    )
+    partner = across(partial)
+    returned = {}
+    for group in FAR_GROUPS:
+        rows = [arrived[q] for q in group]
+        both = jnp.stack(rows)
+        other = across(both)
+        own, rest = routed_ffn(scalars, (), rows, other, routed, cap)
+        rest = across(rest)
+        for n, q in enumerate(group):
+            total = (own[n].astype(F32) + rest[n].astype(F32)).astype(BF)
+            returned[q] = exchange(total, 2 * q)
+    own = [returned[q] for q in range(near_chips, chips)]
+    core = [exchange(returned[q], 1) for q in range(near_chips, chips)]
+    return far_combine(scalars, far_table, base, partner, own, core, cap)
+
+
+FAR_GROUPS = ((6,), (7,), (4, 5,))
+
+
+def serves(mesh_shape, args):
+    _, _, route_ids = args[:3]
+    experts, tensor = mesh_shape["expert"], mesh_shape["tensor"]
+    block, top_count = route_ids.shape[0] // experts, route_ids.shape[1]
+    cap = block * top_count // (2 * experts)
+    return (
+        tensor == 2
+        and args[7].shape[0] == experts
+        and experts == 16
+        and cap % 8 == 0
+        and block % 16 == 0
+    )
 
 
 def on_device(
@@ -143,6 +557,16 @@
         P("expert", "tensor", None),
     )
     out_specs = (P("expert", "tensor"), P("expert", "tensor"))
-    return jax.shard_map(
-        on_device, mesh=mesh, in_specs=in_specs, out_specs=out_specs, check_vma=False
-    )
+
+    def layer(*args):
+        fits = serves(dict(mesh.shape), args)
+        program = jax.shard_map(
+            paired if fits else on_device,
+            mesh=mesh,
+            in_specs=in_specs,
+            out_specs=out_specs,
+            check_vma=False,
+        )
+        return program(*args)
+
+    return layer

time: 223 us -> 155 us (0.70)
  blocking collectives: 44.1 us -> 0 us
  matrix products: 38.1 us -> 0 us
  Pallas kernels: 0 us -> 31.1 us
  starting transfers between devices: 22.5 us -> 45.6 us
  waiting for transfers between devices: 93.2 us -> 75.9 us
  between operations: 14 us -> 1.06 us
  other arithmetic: 6.47 us -> 0.64 us
  local copies, waits for them, and re-layouts: 3.77 us -> 0.16 us
    ppermute x0 -> x31, waiting for transfers between devices: none -> 75.9 us  [the longest x22 59 us: exchange(): return lax.ppermute(values, 'expert', [(i, i ^ k) for i in range(experts)])]
    all_to_all x3 -> x0, waiting for transfers between devices: 47.5 us -> none  [the longest x1 18.2 us: on_device(): lax.all_to_all(x_slots, 'expert', split_axis=0, concat_axis=0, tiled=True)]
    ppermute x0 -> x31, starting transfers between devices: none -> 45.6 us  [the longest x22 34.5 us: exchange(): return lax.ppermute(values, 'expert', [(i, i ^ k) for i in range(experts)])]
    dot_general x15 -> x0, matrix products: 38.1 us -> none  [the longest x1 5.11 us: on_device(): jnp.einsum('erd,efd->erf', x_own, expert_up, preferred_element_type=jnp.f...]
    pallas_call x0 -> x10, Pallas kernels: none -> 31.1 us  [local_call(): pl.pallas_call(kernel, out_shape=list(outs), in_specs=[pl.BlockSpec(memor...]
    all_to_all x1 -> x0, blocking collectives: 25.4 us -> none  [on_device(): lax.all_to_all(g_slots, 'expert', split_axis=0, concat_axis=0, tiled=True)]
    all_gather x2 -> x0, waiting for transfers between devices: 23.2 us -> none  [the longest x1 21 us: on_device(): lax.all_gather(g_part, 'tensor', axis=1, tiled=True)]
    all_to_all x3 -> x0, starting transfers between devices: 22.4 us -> none  [the longest x1 9.15 us: on_device(): lax.all_to_all(value_part, 'expert', split_axis=0, concat_axis=0, tiled=T...]
  transfers between devices with their start and end apart: 7 -> 31, of which waited for: 7 -> 15; matrix products, arithmetic and copies ran while one was open for 14% -> 0% of each run, Pallas kernels for 0% -> 15%
where the time goes in v1:
time: 155 us
  waiting for transfers between devices  75.9 us (49%)
  starting transfers between devices  45.6 us (29%)
  Pallas kernels  31.1 us (20%)
    ppermute x22, waiting for transfers between devices, exchange(): return lax.ppermute(values, 'expert', [(i, i ^ k) for i in range(experts)])  59 us
    ppermute x22, starting transfers between devices, exchange(): return lax.ppermute(values, 'expert', [(i, i ^ k) for i in range(experts)])  34.5 us
    pallas_call x10, Pallas kernels, local_call(): pl.pallas_call(kernel, out_shape=list(outs), in_specs=[pl.BlockSpec(memor...  31.1 us
    ppermute x9, waiting for transfers between devices, across(): return lax.ppermute(values, 'tensor', [(0, 1), (1, 0)])  17 us
    ppermute x9, starting transfers between devices, across(): return lax.ppermute(values, 'tensor', [(0, 1), (1, 0)])  11.1 us
  transfers between devices with their start and end apart: 31, of which 15 were waited for; matrix products, arithmetic and copies ran while one was open for 0% of the time, Pallas kernels for 15%

profile of v1, /device:TPU:0, one launch (start us, length us, event | category | flops | bytes accessed | tf_op | source)
XLA Modules:
  0.0 154.5 jit_solution(3285681636258006365)
XLA Ops:
  0.6 3.1 %collective-permute-start = (bf16[128,1024]{1,0:T(8,128)(2,1)}, bf16[128,1024]{1,0:T(8,128)(2,1)S(1)}, u32[]{:S(2)}, u32[]{:S(2)}) collective-permute-start(bf16[128,1024]{1,0:T(8,128)(2,1)} %refs_3_.1), channel_id=1, source_target_pairs={{0,1},{1,0},{2,3},{3,2},{4,5},{5,4},{6,7},{7,6},{8,9},{9,8},{10,11... | collective-permute-start | bytes 786440 | tf_op jit(solution)/shard_map/ppermute | solution.py:355
  3.8 2.4 %shard_map.113 = (bf16[48,1024]{1,0:T(8,128)(2,1)S(1)}, bf16[48,1024]{1,0:T(8,128)(2,1)S(1)}, bf16[48,1024]{1,0:T(8,128)(2,1)S(1)}, bf16[48,1024]{1,0:T(8,128)(2...) custom-call(s32[2]{0:T(128)S(1)} %pad_add_fusion.refs_0_, ...), custom_call_target="tpu_custom_call" | custom-call | flops 201326592 | bytes 2234368 | tf_op jit(solution)/shard_map/pallas_call | solution.py:55
  6.2 4.8 %collective-permute-done.refs_5_.refs_3_ = bf16[128,1024]{1,0:T(8,128)(2,1)S(1)} collective-permute-done((bf16[128,1024]{1,0:T(8,128)(2,1)}, bf16[128,1024]{1,0:T(8,128)(2,1)S(1)}, u32[]{:S(2)}, u32[]{:S(2)}) %collective-permute-start) | collective-permute-done | bytes 262176 | tf_op jit(solution)/shard_map/ppermute | solution.py:355
  11.1 4.8 %collective-permute-done.1.refs_6_.refs_4_ = bf16[128,1024]{1,0:T(8,128)(2,1)S(1)} collective-permute-done((bf16[128,1024]{1,0:T(8,128)(2,1)}, bf16[128,1024]{1,0:T(8,128)(2,1)S(1)}, u32[]{:S(2)}, u32[]{:S(2)}) %collective-permute-start.1) | collective-permute-done | bytes 262176 | tf_op jit(solution)/shard_map/ppermute | solution.py:355
  15.8 1.1 shard_map.115
  17.0 0.5 collective-permute-start.12
  17.6 1.7 %collective-permute-done.2 = bf16[4,2,48,1024]{3,2,1,0:T(8,128)(2,1)S(1)} collective-permute-done((bf16[4,2,48,1024]{3,2,1,0:T(8,128)(2,1)S(1)}, bf16[4,2,48,1024]{3,2,1,0:T(8,128)(2,1)S(1)}, u32[]{:S(2)}, u32[]{:S(2)}) %collective-permute-start.2) | collective-permute-done | bytes 786464 | tf_op jit(solution)/shard_map/ppermute | solution.py:358
  19.4 1.8 %collective-permute-start.3 = (bf16[2,96,1024]{2,1,0:T(8,128)(2,1)S(1)}, bf16[2,96,1024]{2,1,0:T(8,128)(2,1)S(1)}, u32[]{:S(2)}, u32[]{:S(2)}) collective-permute-start(bf16[2,96,1024]{2,1,0:T(8,128)(2,1)S(1)} %pad_maximum_fusion.2), channel_id=1, source_target_pairs={{0,4},{2,6},{4,0},{6,2},{8,12},{10,14},{12,8},{14,10},{16,20},{18,... | collective-permute-start | bytes 1179656 | tf_op jit(solution)/shard_map/ppermute | solution.py:358
  21.2 1.6 %collective-permute-start.4 = (bf16[2,96,1024]{2,1,0:T(8,128)(2,1)S(1)}, bf16[2,96,1024]{2,1,0:T(8,128)(2,1)S(1)}, u32[]{:S(2)}, u32[]{:S(2)}) collective-permute-start(bf16[2,96,1024]{2,1,0:T(8,128)(2,1)S(1)} %pad_maximum_fusion.3), channel_id=1, source_target_pairs={{0,8},{2,10},{4,12},{6,14},{8,0},{10,2},{12,4},{14,6},{16,24},{18,... | collective-permute-start | bytes 1179656 | tf_op jit(solution)/shard_map/ppermute | solution.py:358
  22.9 0.3 collective-permute-start.5
  23.2 7.4 %collective-permute-done.3.refs_2_ = bf16[2,96,1024]{2,1,0:T(8,128)(2,1)S(1)} collective-permute-done((bf16[2,96,1024]{2,1,0:T(8,128)(2,1)S(1)}, bf16[2,96,1024]{2,1,0:T(8,128)(2,1)S(1)}, u32[]{:S(2)}, u32[]{:S(2)}) %collective-permute-start.3) | collective-permute-done | bytes 393248 | tf_op jit(solution)/shard_map/ppermute | solution.py:358
  30.6 2.6 %collective-permute-done.4.refs_3_ = bf16[2,96,1024]{2,1,0:T(8,128)(2,1)S(1)} collective-permute-done((bf16[2,96,1024]{2,1,0:T(8,128)(2,1)S(1)}, bf16[2,96,1024]{2,1,0:T(8,128)(2,1)S(1)}, u32[]{:S(2)}, u32[]{:S(2)}) %collective-permute-start.4) | collective-permute-done | bytes 393248 | tf_op jit(solution)/shard_map/ppermute | solution.py:358
  33.2 7.1 %collective-permute-done.5.refs_4_ = bf16[2,96,1024]{2,1,0:T(8,128)(2,1)S(1)} collective-permute-done((bf16[2,96,1024]{2,1,0:T(8,128)(2,1)S(1)}, bf16[2,96,1024]{2,1,0:T(8,128)(2,1)S(1)}, u32[]{:S(2)}, u32[]{:S(2)}) %collective-permute-start.5) | collective-permute-done | bytes 393248 | tf_op jit(solution)/shard_map/ppermute | solution.py:358
  40.4 5.1 %shard_map.116 = (bf16[2,96,1024]{2,1,0:T(8,128)(2,1)S(1)}, bf16[2,96,1024]{2,1,0:T(8,128)(2,1)S(1)}, bf16[2,96,1024]{2,1,0:T(8,128)(2,1)S(1)}, bf16[2,96,1024]{2,1,0:T(8,128)(2,1)S(1)}) custom-call(s32[2]{0:T(128)S(1)} %pad_add_fusion.refs_0_, bf16[2,96,1024]{2,1,0:T(8,128)(2,1)S(1)} %pad_maximum_fusion.1.refs_1_, ...), custom_call_target="tpu_custom_call" | custom-call | flops 3321888768 | bytes 11796480 | tf_op jit(solution)/shard_map/pallas_call | solution.py:55
  45.5 2.7 %collective-permute-start.9 = (bf16[2,96,1024]{2,1,0:T(8,128)(2,1)S(1)}, bf16[2,96,1024]{2,1,0:T(8,128)(2,1)S(1)}, u32[]{:S(2)}, u32[]{:S(2)}) collective-permute-start(bf16[2,96,1024]{2,1,0:T(8,128)(2,1)S(1)} %get-tuple-element.41), channel_id=1, source_target_pairs={{0,12},{2,14},{4,8},{6,10},{8,4},{10,6},{12,0},{14,2},{16,28},{18,... | collective-permute-start | bytes 1179656 | tf_op jit(solution)/shard_map/ppermute | solution.py:358
  48.2 0.4 collective-permute-start.8
  48.7 0.4 collective-permute-start.7
  49.1 2.8 %collective-permute-start.13 = (bf16[96,1024]{1,0:T(8,128)(2,1)S(1)}, bf16[96,1024]{1,0:T(8,128)(2,1)S(1)}, u32[]{:S(2)}, u32[]{:S(2)}) collective-permute-start(bf16[96,1024]{1,0:T(8,128)(2,1)S(1)} %pad_maximum_fusion.6), channel_id=1, source_target_pairs={{0,16},{2,18},{4,20},{6,22},{8,24},{10,26},{12,28},{14,30},{16,0},... | collective-permute-start | bytes 589832 | tf_op jit(solution)/shard_map/ppermute | solution.py:358
  51.9 1.3 collective-permute-start.14
  53.3 13.7 %collective-permute-done.9.refs_9_ = bf16[2,96,1024]{2,1,0:T(8,128)(2,1)S(1)} collective-permute-done((bf16[2,96,1024]{2,1,0:T(8,128)(2,1)S(1)}, bf16[2,96,1024]{2,1,0:T(8,128)(2,1)S(1)}, u32[]{:S(2)}, u32[]{:S(2)}) %collective-permute-start.9) | collective-permute-done | bytes 393248 | tf_op jit(solution)/shard_map/ppermute | solution.py:358
  67.0 3.8 %collective-permute-start.19 = (bf16[96,1024]{1,0:T(8,128)(2,1)S(1)}, bf16[96,1024]{1,0:T(8,128)(2,1)S(1)}, u32[]{:S(2)}, u32[]{:S(2)}) collective-permute-start(bf16[96,1024]{1,0:T(8,128)(2,1)S(1)} %pad_maximum_fusion.8), channel_id=1, source_target_pairs={{0,24},{2,26},{4,28},{6,30},{8,16},{10,18},{12,20},{14,22},{16,8},... | collective-permute-start | bytes 589832 | tf_op jit(solution)/shard_map/ppermute | solution.py:358
  70.8 2.9 %collective-permute-done.8.refs_8_ = bf16[2,96,1024]{2,1,0:T(8,128)(2,1)S(1)} collective-permute-done((bf16[2,96,1024]{2,1,0:T(8,128)(2,1)S(1)}, bf16[2,96,1024]{2,1,0:T(8,128)(2,1)S(1)}, u32[]{:S(2)}, u32[]{:S(2)}) %collective-permute-start.8) | collective-permute-done | bytes 393248 | tf_op jit(solution)/shard_map/ppermute | solution.py:358
  73.6 9.9 %collective-permute-start.23 = (bf16[96,1024]{1,0:T(8,128)(2,1)S(1)}, bf16[96,1024]{1,0:T(8,128)(2,1)S(1)}, u32[]{:S(2)}, u32[]{:S(2)}) collective-permute-start(bf16[96,1024]{1,0:T(8,128)(2,1)S(1)} %pad_maximum_fusion.9), channel_id=1, source_target_pairs={{0,28},{2,30},{4,24},{6,26},{8,20},{10,22},{12,16},{14,18},{16,12}... | collective-permute-start | bytes 589832 | tf_op jit(solution)/shard_map/ppermute | solution.py:358
  83.5 0.1 pad_maximum_fusion
  83.8 1.6 %collective-permute-start.15 = (bf16[2,96,1024]{2,1,0:T(8,128)(2,1)S(1)}, bf16[2,96,1024]{2,1,0:T(8,128)(2,1)S(1)}, u32[]{:S(2)}, u32[]{:S(2)}) collective-permute-start(bf16[2,96,1024]{2,1,0:T(8,128)(2,1)S(1)} %pad_maximum_fusion.5), channel_id=1, source_target_pairs={{0,1},{1,0},{2,3},{3,2},{4,5},{5,4},{6,7},{7,6},{8,9},{9,8},{10,11... | collective-permute-start | bytes 1179656 | tf_op jit(solution)/shard_map/ppermute | solution.py:355
  85.4 0.8 shard_map.114
  86.2 0.6 collective-permute-start.20
  86.8 0.5 collective-permute-done.23.refs_1_
  87.3 1.5 collective-permute-start.24
  88.8 4.6 %shard_map.117 = (f32[2,128,1024]{2,1,0:T(8,128)S(1)}, f32[2,128,1024]{2,1,0:T(8,128)S(1)}) custom-call(s32[2]{0:T(128)S(1)} %pad_add_fusion.refs_0_, bf16[128,1024]{1,0:T(8,128)(2,1)S(1)} %get-tuple-element.34.refs_1_, bf16[128,1024]{1,0:T(8,128)(2,1)S(1)} %get-tuple-element.35.refs_2_, bf16[128,1024]{1,0:T(8,128)(2,1)S(1)} %collective-permute-done.refs_5_.refs_3_, ...), custom_call_target="tpu_custom_call" | custom-call | flops 2214592512 | bytes 11796480 | tf_op jit(solution)/shard_map/pallas_call | solution.py:55
  93.4 6.7 %collective-permute-done.20.refs_2_ = bf16[1,96,1024]{2,1,0:T(8,128)(2,1)S(1)} collective-permute-done((bf16[1,96,1024]{2,1,0:T(8,128)(2,1)S(1)}, bf16[1,96,1024]{2,1,0:T(8,128)(2,1)S(1)}, u32[]{:S(2)}, u32[]{:S(2)}) %collective-permute-start.20) | collective-permute-done | bytes 196640 | tf_op jit(solution)/shard_map/ppermute | solution.py:355
  100.1 4.5 %shard_map.120 = (bf16[96,1024]{1,0:T(8,128)(2,1)S(1)}, bf16[1,96,1024]{2,1,0:T(8,128)(2,1)S(1)}) custom-call(s32[2]{0:T(128)S(1)} %pad_add_fusion.refs_0_, bf16[96,1024]{1,0:T(8,128)(2,1)S(1)} %collective-permute-done.19.refs_1_, bf16[1,96,1024]{2,1,0:T(8,128)(2,1)S(1)} %collective-permute-done.20.refs_2_, bf16[704,2048]{1,0:T(8,128)(2,1)S(1)} %bitcast.47, ...), custom_call_target="tpu_custom_call" | custom-call | flops 830472192 | bytes 9437184 | tf_op jit(solution)/shard_map/pallas_call | solution.py:55
  104.5 1.6 %collective-permute-start.21 = (bf16[1,96,1024]{2,1,0:T(8,128)(2,1)S(1)}, bf16[1,96,1024]{2,1,0:T(8,128)(2,1)S(1)}, u32[]{:S(2)}, u32[]{:S(2)}) collective-permute-start(bf16[1,96,1024]{2,1,0:T(8,128)(2,1)S(1)} %get-tuple-element.54), channel_id=1, source_target_pairs={{0,1},{1,0},{2,3},{3,2},{4,5},{5,4},{6,7},{7,6},{8,9},{9,8},{10,11... | collective-permute-start | bytes 589832 | tf_op jit(solution)/shard_map/ppermute | solution.py:355
  106.1 4.3 %shard_map.121 = (bf16[96,1024]{1,0:T(8,128)(2,1)S(1)}, bf16[1,96,1024]{2,1,0:T(8,128)(2,1)S(1)}) custom-call(s32[2]{0:T(128)S(1)} %pad_add_fusion.refs_0_, bf16[96,1024]{1,0:T(8,128)(2,1)S(1)} %collective-permute-done.23.refs_1_, bf16[1,96,1024]{2,1,0:T(8,128)(2,1)S(1)} %collective-permute-done.24.refs_2_, bf16[704,2048]{1,0:T(8,128)(2,1)S(1)} %bitcast.48, ...), custom_call_target="tpu_custom_call" | custom-call | flops 830472192 | bytes 9437184 | tf_op jit(solution)/shard_map/pallas_call | solution.py:55
  110.4 0.6 collective-permute-start.25
  111.0 4.6 %shard_map.119 = (bf16[96,1024]{1,0:T(8,128)(2,1)S(1)}, bf16[96,1024]{1,0:T(8,128)(2,1)S(1)}, bf16[2,96,1024]{2,1,0:T(8,128)(2,1)S(1)}) custom-call(s32[2]{0:T(128)S(1)} %pad_add_fusion.refs_0_, bf16[96,1024]{1,0:T(8,128)(2,1)S(1)} %collective-permute-done.13.refs_1_, bf16[96,1024]{1,0:T(8,128)(2,1)S(1)} %collective-permute-done.14.refs_2_, ...), custom_call_target="tpu_custom_call" | custom-call | flops 1660944384 | bytes 10223616 | tf_op jit(solution)/shard_map/pallas_call | solution.py:55
  115.6 1.6 %collective-permute-start.16 = (bf16[2,96,1024]{2,1,0:T(8,128)(2,1)S(1)}, bf16[2,96,1024]{2,1,0:T(8,128)(2,1)S(1)}, u32[]{:S(2)}, u32[]{:S(2)}) collective-permute-start(bf16[2,96,1024]{2,1,0:T(8,128)(2,1)S(1)} %get-tuple-element.50), channel_id=1, source_target_pairs={{0,1},{1,0},{2,3},{3,2},{4,5},{5,4},{6,7},{7,6},{8,9},{9,8},{10,11... | collective-permute-start | bytes 1179656 | tf_op jit(solution)/shard_map/ppermute | solution.py:355
  117.4 4.8 %collective-permute-start.26 = (bf16[96,1024]{1,0:T(8,128)(2,1)S(1)}, bf16[96,1024]{1,0:T(8,128)(2,1)S(1)}, u32[]{:S(2)}, u32[]{:S(2)}) collective-permute-start(bf16[96,1024]{1,0:T(8,128)(2,1)S(1)} %fusion), channel_id=1, source_target_pairs={{0,28},{2,30},{4,24},{6,26},{8,20},{10,22},{12,16},{14,18},{16,12}... | collective-permute-start | bytes 589832 | tf_op jit(solution)/shard_map/ppermute | solution.py:358
  122.2 1.8 %shard_map.118 = (f32[2,128,1024]{2,1,0:T(8,128)S(1)}, bf16[2,128,1024]{2,1,0:T(8,128)(2,1)S(1)}) custom-call(s32[2]{0:T(128)S(1)} %pad_add_fusion.refs_0_, bf16[512,384]{1,0:T(8,128)(2,1)S(1)} %get-tuple-element.33.refs_1_, bf16[2,96,1024]{2,1,0:T(8,128)(2,1)S(1)} %collective-permute-done.6.refs_2_, ...), custom_call_target="tpu_custom_call" | custom-call | flops 805306368 | bytes 7208960 | tf_op jit(solution)/shard_map/pallas_call | solution.py:55
  124.0 0.6 collective-permute-start.11
  124.6 0.7 collective-permute-done.16
  125.3 0.1 fusion.2
  125.5 3.8 %collective-permute-start.18 = (bf16[96,1024]{1,0:T(8,128)(2,1)S(1)}, bf16[96,1024]{1,0:T(8,128)(2,1)S(1)}, u32[]{:S(2)}, u32[]{:S(2)}) collective-permute-start(bf16[96,1024]{1,0:T(8,128)(2,1)S(1)} %get-tuple-element.70), channel_id=1, source_target_pairs={{0,20},{2,22},{4,16},{6,18},{8,28},{10,30},{12,24},{14,26},{16,4},... | collective-permute-start | bytes 589832 | tf_op jit(solution)/shard_map/ppermute | solution.py:358
  129.3 2.8 %collective-permute-done.26.refs_7_ = bf16[96,1024]{1,0:T(8,128)(2,1)S(1)} collective-permute-done((bf16[96,1024]{1,0:T(8,128)(2,1)S(1)}, bf16[96,1024]{1,0:T(8,128)(2,1)S(1)}, u32[]{:S(2)}, u32[]{:S(2)}) %collective-permute-start.26) | collective-permute-done | bytes 196640 | tf_op jit(solution)/shard_map/ppermute | solution.py:358
  132.1 14.1 %collective-permute-done.17.refs_4_ = bf16[96,1024]{1,0:T(8,128)(2,1)S(1)} collective-permute-done((bf16[96,1024]{1,0:T(8,128)(2,1)S(1)}, bf16[96,1024]{1,0:T(8,128)(2,1)S(1)}, u32[]{:S(2)}, u32[]{:S(2)}) %collective-permute-start.17) | collective-permute-done | bytes 196640 | tf_op jit(solution)/shard_map/ppermute | solution.py:358
  146.3 4.6 %collective-permute-done.18.refs_5_ = bf16[96,1024]{1,0:T(8,128)(2,1)S(1)} collective-permute-done((bf16[96,1024]{1,0:T(8,128)(2,1)S(1)}, bf16[96,1024]{1,0:T(8,128)(2,1)S(1)}, u32[]{:S(2)}, u32[]{:S(2)}) %collective-permute-start.18) | collective-permute-done | bytes 196640 | tf_op jit(solution)/shard_map/ppermute | solution.py:358
  150.9 1.4 collective-permute-done.28.refs_9_
  152.4 2.0 %shard_map.122 = (bf16[128,1024]{1,0:T(8,128)(2,1)}, bf16[128,1024]{1,0:T(8,128)(2,1)}) custom-call(s32[2]{0:T(128)S(1)} %pad_add_fusion.refs_0_, bf16[512,384]{1,0:T(8,128)(2,1)S(1)} %get-tuple-element.32.refs_1_, f32[2,128,1024]{2,1,0:T(8,128)S(1)} %get-tuple-element.44.refs_2_, bf16[2,128,1024]{2,1,0:T(8,128)(2,1)S(1)} %collective-permute-done.11.refs_3_, ...), custom_call_target="tpu_custom_call" | custom-call | flops 402653184 | bytes 4063232 | tf_op jit(solution)/shard_map/pallas_call | solution.py:55
  (53 shorter events, 1.0 us)
Async XLA Ops:
  0.6 10.4 %collective-permute-start = (bf16[128,1024]{1,0:T(8,128)(2,1)}, bf16[128,1024]{1,0:T(8,128)(2,1)S(1)}, u32[]{:S(2)}, u32[]{:S(2)}) collective-permute-start(bf16[128,1024]{1,0:T(8,128)(2,1)} %refs_3_.1), channel_id=1, source_target_pairs={{0,1},{1,0},{2,3},{3,2},{4,5},{5,4},{6,7},{7,6},{8,9},{9,8},{10,11... | collective-permute-start | bytes 786440 | tf_op jit(solution)/shard_map/ppermute | solution.py:355
  3.7 12.1 %collective-permute-start.1 = (bf16[128,1024]{1,0:T(8,128)(2,1)}, bf16[128,1024]{1,0:T(8,128)(2,1)S(1)}, u32[]{:S(2)}, u32[]{:S(2)}) collective-permute-start(bf16[128,1024]{1,0:T(8,128)(2,1)} %refs_4_.1), channel_id=1, source_target_pairs={{0,1},{1,0},{2,3},{3,2},{4,5},{5,4},{6,7},{7,6},{8,9},{9,8},{10,11... | collective-permute-start | bytes 786440 | tf_op jit(solution)/shard_map/ppermute | solution.py:355
  3.8 36.5 %copy-start.2 = (bf16[1,704,2048]{2,1,0:T(8,128)(2,1)S(1)}, bf16[1,704,2048]{2,1,0:T(8,128)(2,1)}, u32[]{:S(2)}) copy-start(bf16[1,704,2048]{2,1,0:T(8,128)(2,1)} %param.19) | copy-start | bytes 8650756
  16.9 2.4 %collective-permute-start.2 = (bf16[4,2,48,1024]{3,2,1,0:T(8,128)(2,1)S(1)}, bf16[4,2,48,1024]{3,2,1,0:T(8,128)(2,1)S(1)}, u32[]{:S(2)}, u32[]{:S(2)}) collective-permute-start(bf16[4,2,48,1024]{3,2,1,0:T(8,128)(2,1)S(1)} %get-tuple-element.37), channel_id=1, source_target_pairs={{0,2},{2,0},{4,6},{6,4},{8,10},{10,8},{12,14},{14,12},{16,18},{18,... | collective-permute-start | bytes 2359304 | tf_op jit(solution)/shard_map/ppermute | solution.py:358
  17.0 6.1 %collective-permute-start.12 = (bf16[192,1024]{1,0:T(8,128)(2,1)S(1)}, bf16[192,1024]{1,0:T(8,128)(2,1)S(1)}, u32[]{:S(2)}, u32[]{:S(2)}) collective-permute-start(bf16[192,1024]{1,0:T(8,128)(2,1)S(1)} %get-tuple-element.47), channel_id=1, source_target_pairs={{0,2},{2,0},{4,6},{6,4},{8,10},{10,8},{12,14},{14,12},{16,18},{18,... | collective-permute-start | bytes 1179656 | tf_op jit(solution)/shard_map/ppermute | solution.py:358
  17.5 22.9 %copy-start.1 = (bf16[1,704,2048]{2,1,0:T(8,128)(2,1)S(1)}, bf16[1,704,2048]{2,1,0:T(8,128)(2,1)}, u32[]{:S(2)}) copy-start(bf16[1,704,2048]{2,1,0:T(8,128)(2,1)} %param.18) | copy-start | bytes 8650756
  19.4 11.2 %collective-permute-start.3 = (bf16[2,96,1024]{2,1,0:T(8,128)(2,1)S(1)}, bf16[2,96,1024]{2,1,0:T(8,128)(2,1)S(1)}, u32[]{:S(2)}, u32[]{:S(2)}) collective-permute-start(bf16[2,96,1024]{2,1,0:T(8,128)(2,1)S(1)} %pad_maximum_fusion.2), channel_id=1, source_target_pairs={{0,4},{2,6},{4,0},{6,2},{8,12},{10,14},{12,8},{14,10},{16,20},{18,... | collective-permute-start | bytes 1179656 | tf_op jit(solution)/shard_map/ppermute | solution.py:358
  21.2 19.2 %copy-start = (bf16[1,704,2048]{2,1,0:T(8,128)(2,1)S(1)}, bf16[1,704,2048]{2,1,0:T(8,128)(2,1)}, u32[]{:S(2)}) copy-start(bf16[1,704,2048]{2,1,0:T(8,128)(2,1)} %param.17) | copy-start | bytes 8650756
  21.2 12.1 %collective-permute-start.4 = (bf16[2,96,1024]{2,1,0:T(8,128)(2,1)S(1)}, bf16[2,96,1024]{2,1,0:T(8,128)(2,1)S(1)}, u32[]{:S(2)}, u32[]{:S(2)}) collective-permute-start(bf16[2,96,1024]{2,1,0:T(8,128)(2,1)S(1)} %pad_maximum_fusion.3), channel_id=1, source_target_pairs={{0,8},{2,10},{4,12},{6,14},{8,0},{10,2},{12,4},{14,6},{16,24},{18,... | collective-permute-start | bytes 1179656 | tf_op jit(solution)/shard_map/ppermute | solution.py:358
  22.9 17.5 %collective-permute-start.5 = (bf16[2,96,1024]{2,1,0:T(8,128)(2,1)S(1)}, bf16[2,96,1024]{2,1,0:T(8,128)(2,1)S(1)}, u32[]{:S(2)}, u32[]{:S(2)}) collective-permute-start(bf16[2,96,1024]{2,1,0:T(8,128)(2,1)S(1)} %pad_maximum_fusion.4), channel_id=1, source_target_pairs={{0,12},{2,14},{4,8},{6,10},{8,4},{10,6},{12,0},{14,2},{16,28},{18,... | collective-permute-start | bytes 1179656 | tf_op jit(solution)/shard_map/ppermute | solution.py:358
  40.4 48.4 %copy-start.4 = (bf16[704,2048]{1,0:T(8,128)(2,1)S(1)}, bf16[704,2048]{1,0:T(8,128)(2,1)}, u32[]{:S(2)}) copy-start(bf16[704,2048]{1,0:T(8,128)(2,1)} %refs_6_.1) | copy-start | bytes 8650756
  40.4 48.4 %copy-start.5 = (bf16[704,2048]{1,0:T(8,128)(2,1)S(1)}, bf16[704,2048]{1,0:T(8,128)(2,1)}, u32[]{:S(2)}) copy-start(bf16[704,2048]{1,0:T(8,128)(2,1)} %refs_7_.1) | copy-start | bytes 8650756
  45.5 21.5 %collective-permute-start.9 = (bf16[2,96,1024]{2,1,0:T(8,128)(2,1)S(1)}, bf16[2,96,1024]{2,1,0:T(8,128)(2,1)S(1)}, u32[]{:S(2)}, u32[]{:S(2)}) collective-permute-start(bf16[2,96,1024]{2,1,0:T(8,128)(2,1)S(1)} %get-tuple-element.41), channel_id=1, source_target_pairs={{0,12},{2,14},{4,8},{6,10},{8,4},{10,6},{12,0},{14,2},{16,28},{18,... | collective-permute-start | bytes 1179656 | tf_op jit(solution)/shard_map/ppermute | solution.py:358
  48.2 25.4 %collective-permute-start.8 = (bf16[2,96,1024]{2,1,0:T(8,128)(2,1)S(1)}, bf16[2,96,1024]{2,1,0:T(8,128)(2,1)S(1)}, u32[]{:S(2)}, u32[]{:S(2)}) collective-permute-start(bf16[2,96,1024]{2,1,0:T(8,128)(2,1)S(1)} %get-tuple-element.40), channel_id=1, source_target_pairs={{0,8},{2,10},{4,12},{6,14},{8,0},{10,2},{12,4},{14,6},{16,24},{18,... | collective-permute-start | bytes 1179656 | tf_op jit(solution)/shard_map/ppermute | solution.py:358
  48.7 34.8 %collective-permute-start.7 = (bf16[2,96,1024]{2,1,0:T(8,128)(2,1)S(1)}, bf16[2,96,1024]{2,1,0:T(8,128)(2,1)S(1)}, u32[]{:S(2)}, u32[]{:S(2)}) collective-permute-start(bf16[2,96,1024]{2,1,0:T(8,128)(2,1)S(1)} %get-tuple-element.39), channel_id=1, source_target_pairs={{0,4},{2,6},{4,0},{6,2},{8,12},{10,14},{12,8},{14,10},{16,20},{18,... | collective-permute-start | bytes 1179656 | tf_op jit(solution)/shard_map/ppermute | solution.py:358
  49.1 34.7 %collective-permute-start.13 = (bf16[96,1024]{1,0:T(8,128)(2,1)S(1)}, bf16[96,1024]{1,0:T(8,128)(2,1)S(1)}, u32[]{:S(2)}, u32[]{:S(2)}) collective-permute-start(bf16[96,1024]{1,0:T(8,128)(2,1)S(1)} %pad_maximum_fusion.6), channel_id=1, source_target_pairs={{0,16},{2,18},{4,20},{6,22},{8,24},{10,26},{12,28},{14,30},{16,0},... | collective-permute-start | bytes 589832 | tf_op jit(solution)/shard_map/ppermute | solution.py:358
  51.9 31.8 %collective-permute-start.14 = (bf16[96,1024]{1,0:T(8,128)(2,1)S(1)}, bf16[96,1024]{1,0:T(8,128)(2,1)S(1)}, u32[]{:S(2)}, u32[]{:S(2)}) collective-permute-start(bf16[96,1024]{1,0:T(8,128)(2,1)S(1)} %pad_maximum_fusion.7), channel_id=1, source_target_pairs={{0,20},{2,22},{4,16},{6,18},{8,28},{10,30},{12,24},{14,26},{16,4},... | collective-permute-start | bytes 589832 | tf_op jit(solution)/shard_map/ppermute | solution.py:358
  67.0 19.2 %collective-permute-start.19 = (bf16[96,1024]{1,0:T(8,128)(2,1)S(1)}, bf16[96,1024]{1,0:T(8,128)(2,1)S(1)}, u32[]{:S(2)}, u32[]{:S(2)}) collective-permute-start(bf16[96,1024]{1,0:T(8,128)(2,1)S(1)} %pad_maximum_fusion.8), channel_id=1, source_target_pairs={{0,24},{2,26},{4,28},{6,30},{8,16},{10,18},{12,20},{14,22},{16,8},... | collective-permute-start | bytes 589832 | tf_op jit(solution)/shard_map/ppermute | solution.py:358
  73.6 13.7 %collective-permute-start.23 = (bf16[96,1024]{1,0:T(8,128)(2,1)S(1)}, bf16[96,1024]{1,0:T(8,128)(2,1)S(1)}, u32[]{:S(2)}, u32[]{:S(2)}) collective-permute-start(bf16[96,1024]{1,0:T(8,128)(2,1)S(1)} %pad_maximum_fusion.9), channel_id=1, source_target_pairs={{0,28},{2,30},{4,24},{6,26},{8,20},{10,22},{12,16},{14,18},{16,12}... | collective-permute-start | bytes 589832 | tf_op jit(solution)/shard_map/ppermute | solution.py:358
  83.5 5.3 %copy-start.3 = (bf16[704,2048]{1,0:T(8,128)(2,1)S(1)}, bf16[704,2048]{1,0:T(8,128)(2,1)}, u32[]{:S(2)}) copy-start(bf16[704,2048]{1,0:T(8,128)(2,1)} %refs_5_.1) | copy-start | bytes 8650756
  83.7 38.5 %collective-permute-start.10 = (bf16[3,2,96,1024]{3,2,1,0:T(8,128)(2,1)S(1)}, bf16[3,2,96,1024]{3,2,1,0:T(8,128)(2,1)S(1)}, u32[]{:S(2)}, u32[]{:S(2)}) collective-permute-start(bf16[3,2,96,1024]{3,2,1,0:T(8,128)(2,1)S(1)} %pad_maximum_fusion), channel_id=1, source_target_pairs={{0,2},{2,0},{4,6},{6,4},{8,10},{10,8},{12,14},{14,12},{16,18},{18,... | collective-permute-start | bytes 3538952 | tf_op jit(solution)/shard_map/ppermute | solution.py:358
  83.8 27.2 %collective-permute-start.15 = (bf16[2,96,1024]{2,1,0:T(8,128)(2,1)S(1)}, bf16[2,96,1024]{2,1,0:T(8,128)(2,1)S(1)}, u32[]{:S(2)}, u32[]{:S(2)}) collective-permute-start(bf16[2,96,1024]{2,1,0:T(8,128)(2,1)S(1)} %pad_maximum_fusion.5), channel_id=1, source_target_pairs={{0,1},{1,0},{2,3},{3,2},{4,5},{5,4},{6,7},{7,6},{8,9},{9,8},{10,11... | collective-permute-start | bytes 1179656 | tf_op jit(solution)/shard_map/ppermute | solution.py:355
  86.2 13.9 %collective-permute-start.20 = (bf16[1,96,1024]{2,1,0:T(8,128)(2,1)S(1)}, bf16[1,96,1024]{2,1,0:T(8,128)(2,1)S(1)}, u32[]{:S(2)}, u32[]{:S(2)}) collective-permute-start(bf16[1,96,1024]{2,1,0:T(8,128)(2,1)S(1)} %bitcast.64), channel_id=1, source_target_pairs={{0,1},{1,0},{2,3},{3,2},{4,5},{5,4},{6,7},{7,6},{8,9},{9,8},{10,11... | collective-permute-start | bytes 589832 | tf_op jit(solution)/shard_map/ppermute | solution.py:355
  87.3 18.9 %collective-permute-start.24 = (bf16[1,96,1024]{2,1,0:T(8,128)(2,1)S(1)}, bf16[1,96,1024]{2,1,0:T(8,128)(2,1)S(1)}, u32[]{:S(2)}, u32[]{:S(2)}) collective-permute-start(bf16[1,96,1024]{2,1,0:T(8,128)(2,1)S(1)} %bitcast.63), channel_id=1, source_target_pairs={{0,1},{1,0},{2,3},{3,2},{4,5},{5,4},{6,7},{7,6},{8,9},{9,8},{10,11... | collective-permute-start | bytes 589832 | tf_op jit(solution)/shard_map/ppermute | solution.py:355
  104.5 12.7 %collective-permute-start.21 = (bf16[1,96,1024]{2,1,0:T(8,128)(2,1)S(1)}, bf16[1,96,1024]{2,1,0:T(8,128)(2,1)S(1)}, u32[]{:S(2)}, u32[]{:S(2)}) collective-permute-start(bf16[1,96,1024]{2,1,0:T(8,128)(2,1)S(1)} %get-tuple-element.54), channel_id=1, source_target_pairs={{0,1},{1,0},{2,3},{3,2},{4,5},{5,4},{6,7},{7,6},{8,9},{9,8},{10,11... | collective-permute-start | bytes 589832 | tf_op jit(solution)/shard_map/ppermute | solution.py:355
  110.4 6.9 %collective-permute-start.25 = (bf16[1,96,1024]{2,1,0:T(8,128)(2,1)S(1)}, bf16[1,96,1024]{2,1,0:T(8,128)(2,1)S(1)}, u32[]{:S(2)}, u32[]{:S(2)}) collective-permute-start(bf16[1,96,1024]{2,1,0:T(8,128)(2,1)S(1)} %get-tuple-element.57), channel_id=1, source_target_pairs={{0,1},{1,0},{2,3},{3,2},{4,5},{5,4},{6,7},{7,6},{8,9},{9,8},{10,11... | collective-permute-start | bytes 589832 | tf_op jit(solution)/shard_map/ppermute | solution.py:355
  115.6 9.7 %collective-permute-start.16 = (bf16[2,96,1024]{2,1,0:T(8,128)(2,1)S(1)}, bf16[2,96,1024]{2,1,0:T(8,128)(2,1)S(1)}, u32[]{:S(2)}, u32[]{:S(2)}) collective-permute-start(bf16[2,96,1024]{2,1,0:T(8,128)(2,1)S(1)} %get-tuple-element.50), channel_id=1, source_target_pairs={{0,1},{1,0},{2,3},{3,2},{4,5},{5,4},{6,7},{7,6},{8,9},{9,8},{10,11... | collective-permute-start | bytes 1179656 | tf_op jit(solution)/shard_map/ppermute | solution.py:355
  117.2 5.0 %collective-permute-start.6 = (bf16[2,96,1024]{2,1,0:T(8,128)(2,1)S(1)}, bf16[2,96,1024]{2,1,0:T(8,128)(2,1)S(1)}, u32[]{:S(2)}, u32[]{:S(2)}) collective-permute-start(bf16[2,96,1024]{2,1,0:T(8,128)(2,1)S(1)} %get-tuple-element.38.refs_6_), channel_id=1, source_target_pairs={{0,2},{2,0},{4,6},{6,4},{8,10},{10,8},{12,14},{14,12},{16,18},{18,... | collective-permute-start | bytes 1179656 | tf_op jit(solution)/shard_map/ppermute | solution.py:358
  117.3 12.1 %collective-permute-start.22 = (bf16[96,1024]{1,0:T(8,128)(2,1)S(1)}, bf16[96,1024]{1,0:T(8,128)(2,1)S(1)}, u32[]{:S(2)}, u32[]{:S(2)}) collective-permute-start(bf16[96,1024]{1,0:T(8,128)(2,1)S(1)} %fusion.1), channel_id=1, source_target_pairs={{0,24},{2,26},{4,28},{6,30},{8,16},{10,18},{12,20},{14,22},{16,8},... | collective-permute-start | bytes 589832 | tf_op jit(solution)/shard_map/ppermute | solution.py:358
  117.4 14.7 %collective-permute-start.26 = (bf16[96,1024]{1,0:T(8,128)(2,1)S(1)}, bf16[96,1024]{1,0:T(8,128)(2,1)S(1)}, u32[]{:S(2)}, u32[]{:S(2)}) collective-permute-start(bf16[96,1024]{1,0:T(8,128)(2,1)S(1)} %fusion), channel_id=1, source_target_pairs={{0,28},{2,30},{4,24},{6,26},{8,20},{10,22},{12,16},{14,18},{16,12}... | collective-permute-start | bytes 589832 | tf_op jit(solution)/shard_map/ppermute | solution.py:358
  124.0 28.4 %collective-permute-start.11 = (bf16[2,128,1024]{2,1,0:T(8,128)(2,1)S(1)}, bf16[2,128,1024]{2,1,0:T(8,128)(2,1)S(1)}, u32[]{:S(2)}, u32[]{:S(2)}) collective-permute-start(bf16[2,128,1024]{2,1,0:T(8,128)(2,1)S(1)} %get-tuple-element.45), channel_id=1, source_target_pairs={{0,1},{1,0},{2,3},{3,2},{4,5},{5,4},{6,7},{7,6},{8,9},{9,8},{10,11... | collective-permute-start | bytes 1572872 | tf_op jit(solution)/shard_map/ppermute | solution.py:355
  125.4 20.9 %collective-permute-start.17 = (bf16[96,1024]{1,0:T(8,128)(2,1)S(1)}, bf16[96,1024]{1,0:T(8,128)(2,1)S(1)}, u32[]{:S(2)}, u32[]{:S(2)}) collective-permute-start(bf16[96,1024]{1,0:T(8,128)(2,1)S(1)} %get-tuple-element.71), channel_id=1, source_target_pairs={{0,16},{2,18},{4,20},{6,22},{8,24},{10,26},{12,28},{14,30},{16,0},... | collective-permute-start | bytes 589832 | tf_op jit(solution)/shard_map/ppermute | solution.py:358
  125.5 25.4 %collective-permute-start.18 = (bf16[96,1024]{1,0:T(8,128)(2,1)S(1)}, bf16[96,1024]{1,0:T(8,128)(2,1)S(1)}, u32[]{:S(2)}, u32[]{:S(2)}) collective-permute-start(bf16[96,1024]{1,0:T(8,128)(2,1)S(1)} %get-tuple-element.70), channel_id=1, source_target_pairs={{0,20},{2,22},{4,16},{6,18},{8,28},{10,30},{12,24},{14,26},{16,4},... | collective-permute-start | bytes 589832 | tf_op jit(solution)/shard_map/ppermute | solution.py:358
  129.3 21.6 %collective-permute-start.29 = (bf16[96,1024]{1,0:T(8,128)(2,1)S(1)}, bf16[96,1024]{1,0:T(8,128)(2,1)S(1)}, u32[]{:S(2)}, u32[]{:S(2)}) collective-permute-start(bf16[96,1024]{1,0:T(8,128)(2,1)S(1)} %collective-permute-done.22.refs_6_), channel_id=1, source_target_pairs={{0,2},{2,0},{4,6},{6,4},{8,10},{10,8},{12,14},{14,12},{16,18},{18,... | collective-permute-start | bytes 589832 | tf_op jit(solution)/shard_map/ppermute | solution.py:358
  132.1 18.8 %collective-permute-start.30 = (bf16[96,1024]{1,0:T(8,128)(2,1)S(1)}, bf16[96,1024]{1,0:T(8,128)(2,1)S(1)}, u32[]{:S(2)}, u32[]{:S(2)}) collective-permute-start(bf16[96,1024]{1,0:T(8,128)(2,1)S(1)} %collective-permute-done.26.refs_7_), channel_id=1, source_target_pairs={{0,2},{2,0},{4,6},{6,4},{8,10},{10,8},{12,14},{14,12},{16,18},{18,... | collective-permute-start | bytes 589832 | tf_op jit(solution)/shard_map/ppermute | solution.py:358
  146.3 4.7 %collective-permute-start.27 = (bf16[96,1024]{1,0:T(8,128)(2,1)S(1)}, bf16[96,1024]{1,0:T(8,128)(2,1)S(1)}, u32[]{:S(2)}, u32[]{:S(2)}) collective-permute-start(bf16[96,1024]{1,0:T(8,128)(2,1)S(1)} %collective-permute-done.17.refs_4_), channel_id=1, source_target_pairs={{0,2},{2,0},{4,6},{6,4},{8,10},{10,8},{12,14},{14,12},{16,18},{18,... | collective-permute-start | bytes 589832 | tf_op jit(solution)/shard_map/ppermute | solution.py:358
  150.9 1.4 collective-permute-start.28

commit v2 on v1

--- a/solution.py
+++ b/solution.py
@@ -6,6 +6,11 @@
 from jax.experimental import pallas as pl
 from jax.experimental.pallas import tpu as pltpu
 from jax.sharding import PartitionSpec as P
+
+
+WHOLE_OUT = (1, 3,)
+WHOLE_BACK = (1, 3,)
+GROUPS = ((4,), (5,), (0, 1, 2, 3, 6,), (7,))
 
 
 BF = jnp.bfloat16
@@ -70,11 +75,11 @@
     return jax.ShapeDtypeStruct(shape, dtype)
 
 
-def prep(scalars, ids_t, wts_t, tokens, cotangent, experts, cap, near_chips):
+def prep(scalars, ids_t, wts_t, tokens, cotangent, experts, cap, chips):
     tok_rows, half = tokens.shape
     top_count = ids_t.shape[0]
     slots = experts * cap
-    far = experts // 2 - near_chips
+    far = len(chips)
 
     def body(scalar_ref, bufs, outs, ready):
         ids_ref, wts_ref, tok_ref, cot_ref = bufs
@@ -101,14 +106,14 @@
         slot_gate = jnp.sum(gm, axis=1, keepdims=True)
         dm_out[...] = dm
         gm_out[...] = gm
-        first = 2 * near_chips * cap
+        first = 2 * min(chips) * cap
         ready(2)
         x_rows = mm(dmb[first:], tok_ref[...])
         ready(3)
         g_rows = slot_gate[first:] * mm(dmb[first:], cot_ref[...])
         for q in range(far):
             for b in range(2):
-                low = (2 * q + b) * cap
+                low = (2 * chips[q] + b) * cap - first
                 both = jnp.concatenate((x_rows[low : low + cap], g_rows[low : low + cap]), 0)
                 if b:
                     core_out[2 * cap * q : 2 * cap * (q + 1), :] = both.astype(BF)
@@ -135,17 +140,17 @@
     return outs[:far], outs[far:]
 
 
-def gate_tables(scalars, dm, gm, cap, near_chips):
-    slots, tok_rows = dm.shape
-    near = 2 * near_chips * cap
+def gate_tables(scalars, dm, gm, cap, near, far):
+    _, tok_rows = dm.shape
 
     def body(_, bufs, outs, ready):
         blank = jnp.zeros((cap, tok_rows), F32)
-        for out, low, high in ((outs[0], 0, near), (outs[1], near, slots)):
+        for out, chips in zip(outs, (near, far)):
             gates, picks = [], []
-            for k in range(low, high, cap):
-                gates += [bufs[1][k : k + cap, :], blank]
-                picks += [blank, bufs[0][k : k + cap, :]]
+            for k in [2 * q + b for q in chips for b in range(2)]:
+                rows = slice(k * cap, (k + 1) * cap)
+                gates += [bufs[1][rows, :], blank]
+                picks += [blank, bufs[0][rows, :]]
             gate = jnp.transpose(jnp.concatenate(gates, 0))
             one = gate.astype(BF)
             left = gate - one.astype(F32)
@@ -159,33 +164,34 @@
         body,
         scalars,
         (dm, gm),
-        (shaped((4 * tok_rows, 2 * near)), shaped((4 * tok_rows, 2 * (slots - near)))),
+        [shaped((4 * tok_rows, 4 * cap * len(chips))) for chips in (near, far)],
     )
 
 
 def near_rows(scalars, dm, gm, tokens, tokens_other, cotangent, cotangent_other, cap, chips):
     tok_rows, half = tokens.shape
-    near = 2 * chips * cap
 
     def body(_, bufs, outs, ready):
         t_own, c_own, dm_ref, gm_ref, t_oth, c_oth = bufs
-        dmb = dm_ref[0:near, :].astype(BF)
-        slot_gate = jnp.sum(gm_ref[0:near, :], axis=1, keepdims=True)
+        rows = [slice(2 * q * cap, 2 * (q + 1) * cap) for q in chips]
+        dmb = jnp.concatenate([dm_ref[r, :] for r in rows], 0).astype(BF)
+        gates = jnp.concatenate([gm_ref[r, :] for r in rows], 0)
+        slot_gate = jnp.sum(gates, axis=1, keepdims=True)
         for h, (t_ref, c_ref) in enumerate(((t_own, c_own), (t_oth, c_oth))):
             x_rows = mm(dmb, t_ref[...])
             g_rows = slot_gate * mm(dmb, c_ref[...])
-            for q in range(chips):
+            for n in range(len(chips)):
                 for b in range(2):
-                    low = (2 * q + b) * cap
+                    low = (2 * n + b) * cap
                     both = jnp.concatenate((x_rows[low : low + cap], g_rows[low : low + cap]), 0)
-                    outs[b][q, h] = both.astype(BF)
+                    outs[b][n, h] = both.astype(BF)
 
     return local_call(
         body,
         scalars,
         (tokens, cotangent, dm, gm, tokens_other, cotangent_other),
-        [shaped((chips, 2, 2 * cap, half))] * 2,
-        flops=8 * near * tok_rows * half,
+        [shaped((len(chips), 2, 2 * cap, half))] * 2,
+        flops=16 * len(chips) * cap * tok_rows * half,
     )
 
 
@@ -214,19 +220,29 @@
     return 12 * rows * weights[0].shape[0] * weights[0].shape[1]
 
 
-def routed_ffn(scalars, near, far, other, weights, cap):
-    arrays = list(near) + list(far) + ([other] if far else [])
-    count = len(near) + len(far)
+def routed_ffn(scalars, ins, other, whole, weights, cap):
+    half = weights[0].shape[1] // 2
+    extra = [] if other is None else [other]
+    arrays = list(ins) + extra
+    count = len(ins)
+    parted = count - sum(whole)
 
     def body(scalar_ref, bufs, outs, ready):
-        def views(refs):
-            pairs = [(r.at[0], r.at[1]) for r in refs[: len(near)]]
-            rest = refs[len(near) :]
-            return pairs + [(rest[i], rest[len(far)].at[i]) for i in range(len(far))]
+        def views(refs, entire):
+            pairs, used = [], 0
+            for i in range(count):
+                if entire[i]:
+                    pairs.append((refs[i].at[0], refs[i].at[1]))
+                else:
+                    pairs.append((refs[i], refs[count].at[used]))
+                    used += 1
+            return pairs
+
+        given = views(bufs, [len(a.shape) == 3 for a in ins])
 
         def pick(h, part):
             segments = []
-            for pair in views(bufs[: len(arrays)]):
+            for pair in given:
                 block = pair[h][...].astype(F32)
                 for b in range(2):
                     low = (2 * b + part) * cap
@@ -236,7 +252,7 @@
         xs = [pick(0, 0), pick(1, 0)]
         gs = [pick(0, 1), pick(1, 1)]
         values, inputs = ffn(scalar_ref, xs, gs, bufs[len(arrays) :])
-        for n, pair in enumerate(views(outs)):
+        for n, pair in enumerate(views(outs, whole)):
             for h in range(2):
                 segments = []
                 for b in range(2):
@@ -244,14 +260,12 @@
                     segments += [values[h][low : low + cap], inputs[h][low : low + cap]]
                 pair[h][...] = jnp.concatenate(segments, 0).astype(BF)
 
-    outs = local_call(
-        body,
-        scalars,
-        arrays + list(weights),
-        [shaped(a.shape) for a in arrays],
-        flops=ffn_flops(2 * cap * count, weights),
-    )
-    return outs if near else (outs[:-1], outs[-1])
+    results = [shaped((2, 4 * cap, half)) if w else shaped((4 * cap, half)) for w in whole]
+    if parted:
+        results.append(shaped((parted, 4 * cap, half)))
+    return local_call(
+        body, scalars, arrays + list(weights), results, flops=ffn_flops(2 * cap * count, weights)
+    )
 
 
 def shared_ffn(scalars, tokens, tokens_other, cotangent, cotangent_other, weights):
@@ -360,53 +374,62 @@
     def joined(own, core):
         return jnp.concatenate((own, core), axis=own.ndim - 2)
 
-    chips, near_chips = experts // 2, experts // 4
+    chips = range(1, experts // 2)
+    out_halves = [q for q in chips if q not in WHOLE_OUT]
+    back_halves = [q for q in chips if q not in WHOLE_BACK]
     own_far, rest = prep(
-        scalars, route_ids.T, route_weights.T, tokens, cotangent, experts, cap, near_chips
+        scalars, route_ids.T, route_weights.T, tokens, cotangent, experts, cap, out_halves
     )
     core_far, dm, gm, tokens_here, cotangent_here = rest
     tokens_other = across(tokens)
     cotangent_other = across(cotangent)
     core_back = exchange(core_far, 1)
     arrived = {}
-    for q in range(near_chips, chips):
-        rows = slice((q - near_chips) * 2 * cap, (q - near_chips + 1) * 2 * cap)
-        arrived[q] = exchange(joined(own_far[q - near_chips], core_back[rows]), 2 * q)
+    for n, q in enumerate(out_halves):
+        rows = joined(own_far[n], core_back[2 * cap * n : 2 * cap * (n + 1)])
+        arrived[q] = exchange(rows, 2 * q)
+    near = (0, *WHOLE_OUT)
     near_own, near_out = near_rows(
-        scalars, dm, gm, tokens_here, tokens_other, cotangent_here, cotangent_other, cap, near_chips
+        scalars, dm, gm, tokens_here, tokens_other, cotangent_here, cotangent_other, cap, near
     )
     near_back = exchange(near_out, 1)
-    near_table, far_table = gate_tables(scalars, dm, gm, cap, near_chips)
-    near = [joined(near_own[q], near_back[q]) for q in range(near_chips)]
-    near = near[:1] + [exchange(near[q], 2 * q) for q in range(1, near_chips)]
+    for n, q in enumerate(near):
+        rows = joined(near_own[n], near_back[n])
+        arrived[q] = exchange(rows, 2 * q) if q else rows
+    near_table, far_table = gate_tables(scalars, dm, gm, cap, (0, *WHOLE_BACK), back_halves)
     shared_own, shared_other = shared_ffn(
         scalars, tokens_here, tokens_other, cotangent_here, cotangent_other, shared
     )
-    out = routed_ffn(scalars, near, (), None, routed, cap)
-    home = list(out[:1]) + [exchange(out[q], 2 * q) for q in range(1, near_chips)]
+    home = {}
+    for group in GROUPS:
+        halves = [arrived[q] for q in group if q in out_halves]
+        other = None
+        if halves:
+            other = jnp.stack(halves)
+            other = across(other)
+        whole = [q not in back_halves for q in group]
+        ins = [arrived[q] for q in group]
+        results = routed_ffn(scalars, ins, other, whole, routed, cap)
+        rest = across(results[-1]) if not all(whole) else None
+        used = 0
+        for q, entire, result in zip(group, whole, results):
+            if entire:
+                home[q] = exchange(result, 2 * q) if q else result
+            else:
+                total = (result.astype(F32) + rest[used].astype(F32)).astype(BF)
+                home[q] = exchange(total, 2 * q)
+                used += 1
     core0 = exchange(home[0], 1)
-    joint = jnp.stack(home[1:])
+    joint = jnp.stack([home[q] for q in WHOLE_BACK])
     core1 = exchange(joint, 1)
+    near_home = [home[q] for q in (0, *WHOLE_BACK)]
     base, partial = near_combine(
-        scalars, near_table, home, core0, core1, shared_own, shared_other, cap
+        scalars, near_table, near_home, core0, core1, shared_own, shared_other, cap
     )
     partner = across(partial)
-    returned = {}
-    for group in FAR_GROUPS:
-        rows = [arrived[q] for q in group]
-        both = jnp.stack(rows)
-        other = across(both)
-        own, rest = routed_ffn(scalars, (), rows, other, routed, cap)
-        rest = across(rest)
-        for n, q in enumerate(group):
-            total = (own[n].astype(F32) + rest[n].astype(F32)).astype(BF)
-            returned[q] = exchange(total, 2 * q)
-    own = [returned[q] for q in range(near_chips, chips)]
-    core = [exchange(returned[q], 1) for q in range(near_chips, chips)]
+    own = [home[q] for q in back_halves]
+    core = [exchange(home[q], 1) for q in back_halves]
     return far_combine(scalars, far_table, base, partner, own, core, cap)
-
-
-FAR_GROUPS = ((6,), (7,), (4, 5,))
 
 
 def serves(mesh_shape, args):

time: 155 us -> 138 us (0.89)
  starting transfers between devices: 45.6 us -> 34.2 us
  waiting for transfers between devices: 75.9 us -> 69 us
    ppermute x22 -> x23, starting transfers between devices: 34.5 us -> 23.1 us  [exchange(): return lax.ppermute(values, 'expert', [(i, i ^ k) for i in range(experts)])]
    ppermute x22 -> x23, waiting for transfers between devices: 59 us -> 49.1 us  [exchange(): return lax.ppermute(values, 'expert', [(i, i ^ k) for i in range(experts)])]
    ppermute x9 -> x11, waiting for transfers between devices: 17 us -> 19.9 us  [across(): return lax.ppermute(values, 'tensor', [(0, 1), (1, 0)])]
    ppermute x9 -> x11, starting transfers between devices: 11.1 us -> 11.1 us  [across(): return lax.ppermute(values, 'tensor', [(0, 1), (1, 0)])]
  transfers between devices with their start and end apart: 31 -> 34, of which waited for: 15 -> 14; matrix products, arithmetic and copies ran while one was open for 0% -> 0% of each run, Pallas kernels for 15% -> 20%
where the time goes in v2:
time: 138 us; the launch traced here: 136 us
  waiting for transfers between devices  69 us (50%)
  starting transfers between devices  34.2 us (25%)
  Pallas kernels  31.1 us (23%)
    ppermute x23, waiting for transfers between devices, exchange(): return lax.ppermute(values, 'expert', [(i, i ^ k) for i in range(experts)])  49.1 us
    pallas_call x10, Pallas kernels, local_call(): pl.pallas_call(kernel, out_shape=list(outs), in_specs=[pl.BlockSpec(memor...  31.1 us
    ppermute x23, starting transfers between devices, exchange(): return lax.ppermute(values, 'expert', [(i, i ^ k) for i in range(experts)])  23.1 us
    ppermute x11, waiting for transfers between devices, across(): return lax.ppermute(values, 'tensor', [(0, 1), (1, 0)])  19.9 us
    ppermute x11, starting transfers between devices, across(): return lax.ppermute(values, 'tensor', [(0, 1), (1, 0)])  11.1 us
  transfers between devices with their start and end apart: 34, of which 14 were waited for; matrix products, arithmetic and copies ran while one was open for 0% of the time, Pallas kernels for 20%

profile of v2, /device:TPU:0, one launch (start us, length us, event | category | flops | bytes accessed | tf_op | source)
XLA Modules:
  0.0 136.3 jit_solution(2352029647697588059)
XLA Ops:
  0.7 2.3 %shard_map.113 = (bf16[48,1024]{1,0:T(8,128)(2,1)S(1)}, bf16[48,1024]{1,0:T(8,128)(2,1)S(1)}, bf16[48,1024]{1,0:T(8,128)(2,1)S(1)}, bf16[48,1024]{1,0:T(8,128)(2...) custom-call(s32[2]{0:T(128)S(1)} %pad_add_fusion.refs_0_, ...), custom_call_target="tpu_custom_call" | custom-call | flops 201326592 | bytes 2430976 | tf_op jit(solution)/shard_map/pallas_call | solution.py:60
  3.0 0.6 collective-permute-start.4
  3.6 2.6 %collective-permute-start = (bf16[128,1024]{1,0:T(8,128)(2,1)}, bf16[128,1024]{1,0:T(8,128)(2,1)S(1)}, u32[]{:S(2)}, u32[]{:S(2)}) collective-permute-start(bf16[128,1024]{1,0:T(8,128)(2,1)} %refs_3_.1), channel_id=1, source_target_pairs={{0,1},{1,0},{2,3},{3,2},{4,5},{5,4},{6,7},{7,6},{8,9},{9,8},{10,11... | collective-permute-start | bytes 786440 | tf_op jit(solution)/shard_map/ppermute | solution.py:369
  6.2 7.3 %collective-permute-done.refs_5_.refs_3_ = bf16[128,1024]{1,0:T(8,128)(2,1)S(1)} collective-permute-done((bf16[128,1024]{1,0:T(8,128)(2,1)}, bf16[128,1024]{1,0:T(8,128)(2,1)S(1)}, u32[]{:S(2)}, u32[]{:S(2)}) %collective-permute-start) | collective-permute-done | bytes 262176 | tf_op jit(solution)/shard_map/ppermute | solution.py:369
  13.5 5.4 %collective-permute-done.1.refs_6_.refs_4_ = bf16[128,1024]{1,0:T(8,128)(2,1)S(1)} collective-permute-done((bf16[128,1024]{1,0:T(8,128)(2,1)}, bf16[128,1024]{1,0:T(8,128)(2,1)S(1)}, u32[]{:S(2)}, u32[]{:S(2)}) %collective-permute-start.1) | collective-permute-done | bytes 262176 | tf_op jit(solution)/shard_map/ppermute | solution.py:369
  18.9 1.0 shard_map.115
  20.0 1.9 %collective-permute-start.5 = (bf16[96,1024]{1,0:T(8,128)(2,1)S(1)}, bf16[96,1024]{1,0:T(8,128)(2,1)S(1)}, u32[]{:S(2)}, u32[]{:S(2)}) collective-permute-start(bf16[96,1024]{1,0:T(8,128)(2,1)S(1)} %pad_maximum_fusion.5), channel_id=1, source_target_pairs={{0,8},{2,10},{4,12},{6,14},{8,0},{10,2},{12,4},{14,6},{16,24},{18,... | collective-permute-start | bytes 589832 | tf_op jit(solution)/shard_map/ppermute | solution.py:372
  21.9 2.5 %collective-permute-start.7 = (bf16[96,1024]{1,0:T(8,128)(2,1)S(1)}, bf16[96,1024]{1,0:T(8,128)(2,1)S(1)}, u32[]{:S(2)}, u32[]{:S(2)}) collective-permute-start(bf16[96,1024]{1,0:T(8,128)(2,1)S(1)} %pad_maximum_fusion.6), channel_id=1, source_target_pairs={{0,24},{2,26},{4,28},{6,30},{8,16},{10,18},{12,20},{14,22},{16,8},... | collective-permute-start | bytes 589832 | tf_op jit(solution)/shard_map/ppermute | solution.py:372
  24.5 2.9 %collective-permute-done.5.refs_3_ = bf16[96,1024]{1,0:T(8,128)(2,1)S(1)} collective-permute-done((bf16[96,1024]{1,0:T(8,128)(2,1)S(1)}, bf16[96,1024]{1,0:T(8,128)(2,1)S(1)}, u32[]{:S(2)}, u32[]{:S(2)}) %collective-permute-start.5) | collective-permute-done | bytes 196640 | tf_op jit(solution)/shard_map/ppermute | solution.py:372
  27.5 6.5 %collective-permute-done.7.refs_5_ = bf16[96,1024]{1,0:T(8,128)(2,1)S(1)} collective-permute-done((bf16[96,1024]{1,0:T(8,128)(2,1)S(1)}, bf16[96,1024]{1,0:T(8,128)(2,1)S(1)}, u32[]{:S(2)}, u32[]{:S(2)}) %collective-permute-start.7) | collective-permute-done | bytes 196640 | tf_op jit(solution)/shard_map/ppermute | solution.py:372
  34.0 1.6 %collective-permute-start.8 = (bf16[2,96,1024]{2,1,0:T(8,128)(2,1)S(1)}, bf16[2,96,1024]{2,1,0:T(8,128)(2,1)S(1)}, u32[]{:S(2)}, u32[]{:S(2)}) collective-permute-start(bf16[2,96,1024]{2,1,0:T(8,128)(2,1)S(1)} %pad_maximum_fusion.4), channel_id=1, source_target_pairs={{0,1},{1,0},{2,3},{3,2},{4,5},{5,4},{6,7},{7,6},{8,9},{9,8},{10,11... | collective-permute-start | bytes 1179656 | tf_op jit(solution)/shard_map/ppermute | solution.py:369
  35.7 1.5 %collective-permute-start.3 = (bf16[2,96,1024]{2,1,0:T(8,128)(2,1)S(1)}, bf16[2,96,1024]{2,1,0:T(8,128)(2,1)S(1)}, u32[]{:S(2)}, u32[]{:S(2)}) collective-permute-start(bf16[2,96,1024]{2,1,0:T(8,128)(2,1)S(1)} %pad_maximum_fusion.2), channel_id=1, source_target_pairs={{0,4},{2,6},{4,0},{6,2},{8,12},{10,14},{12,8},{14,10},{16,20},{18,... | collective-permute-start | bytes 1179656 | tf_op jit(solution)/shard_map/ppermute | solution.py:372
  37.3 0.7 collective-permute-start.6
  38.0 0.8 shard_map.114
  38.8 1.4 %collective-permute-start.16 = (bf16[96,1024]{1,0:T(8,128)(2,1)S(1)}, bf16[96,1024]{1,0:T(8,128)(2,1)S(1)}, u32[]{:S(2)}, u32[]{:S(2)}) collective-permute-start(bf16[96,1024]{1,0:T(8,128)(2,1)S(1)} %pad_maximum_fusion.7), channel_id=1, source_target_pairs={{0,16},{2,18},{4,20},{6,22},{8,24},{10,26},{12,28},{14,30},{16,0},... | collective-permute-start | bytes 589832 | tf_op jit(solution)/shard_map/ppermute | solution.py:372
  40.3 2.5 %collective-permute-start.20 = (bf16[96,1024]{1,0:T(8,128)(2,1)S(1)}, bf16[96,1024]{1,0:T(8,128)(2,1)S(1)}, u32[]{:S(2)}, u32[]{:S(2)}) collective-permute-start(bf16[96,1024]{1,0:T(8,128)(2,1)S(1)} %pad_maximum_fusion.8), channel_id=1, source_target_pairs={{0,20},{2,22},{4,16},{6,18},{8,28},{10,30},{12,24},{14,26},{16,4},... | collective-permute-start | bytes 589832 | tf_op jit(solution)/shard_map/ppermute | solution.py:372
  42.9 1.8 %collective-permute-done.8.refs_6_ = bf16[2,96,1024]{2,1,0:T(8,128)(2,1)S(1)} collective-permute-done((bf16[2,96,1024]{2,1,0:T(8,128)(2,1)S(1)}, bf16[2,96,1024]{2,1,0:T(8,128)(2,1)S(1)}, u32[]{:S(2)}, u32[]{:S(2)}) %collective-permute-start.8) | collective-permute-done | bytes 393248 | tf_op jit(solution)/shard_map/ppermute | solution.py:369
  44.7 14.0 %collective-permute-done.3.refs_2_ = bf16[2,96,1024]{2,1,0:T(8,128)(2,1)S(1)} collective-permute-done((bf16[2,96,1024]{2,1,0:T(8,128)(2,1)S(1)}, bf16[2,96,1024]{2,1,0:T(8,128)(2,1)S(1)}, u32[]{:S(2)}, u32[]{:S(2)}) %collective-permute-start.3) | collective-permute-done | bytes 393248 | tf_op jit(solution)/shard_map/ppermute | solution.py:372
  58.8 5.5 %shard_map.116 = (bf16[2,96,1024]{2,1,0:T(8,128)(2,1)S(1)}, bf16[2,96,1024]{2,1,0:T(8,128)(2,1)S(1)}, bf16[96,1024]{1,0:T(8,128)(2,1)S(1)}, bf16[2,96,1024]{2,1,...) custom-call(s32[2]{0:T(128)S(1)} %pad_add_fusion.refs_0_, ...), custom_call_target="tpu_custom_call" | custom-call | flops 4152360960 | bytes 12582912 | tf_op jit(solution)/shard_map/pallas_call | solution.py:60
  64.3 0.5 collective-permute-start.11
  64.9 1.1 collective-permute-start.10
  66.0 4.0 %collective-permute-start.25 = (bf16[96,1024]{1,0:T(8,128)(2,1)S(1)}, bf16[96,1024]{1,0:T(8,128)(2,1)S(1)}, u32[]{:S(2)}, u32[]{:S(2)}) collective-permute-start(bf16[96,1024]{1,0:T(8,128)(2,1)S(1)} %pad_maximum_fusion.9), channel_id=1, source_target_pairs={{0,28},{2,30},{4,24},{6,26},{8,20},{10,22},{12,16},{14,18},{16,12}... | collective-permute-start | bytes 589832 | tf_op jit(solution)/shard_map/ppermute | solution.py:372
  69.9 0.5 collective-permute-start.17
  70.4 1.5 %collective-permute-start.21 = (bf16[1,96,1024]{2,1,0:T(8,128)(2,1)S(1)}, bf16[1,96,1024]{2,1,0:T(8,128)(2,1)S(1)}, u32[]{:S(2)}, u32[]{:S(2)}) collective-permute-start(bf16[1,96,1024]{2,1,0:T(8,128)(2,1)S(1)} %bitcast.61), channel_id=1, source_target_pairs={{0,1},{1,0},{2,3},{3,2},{4,5},{5,4},{6,7},{7,6},{8,9},{9,8},{10,11... | collective-permute-start | bytes 589832 | tf_op jit(solution)/shard_map/ppermute | solution.py:369
  72.0 4.6 %shard_map.117 = (f32[2,128,1024]{2,1,0:T(8,128)S(1)}, f32[2,128,1024]{2,1,0:T(8,128)S(1)}) custom-call(s32[2]{0:T(128)S(1)} %pad_add_fusion.refs_0_, bf16[128,1024]{1,0:T(8,128)(2,1)S(1)} %get-tuple-element.36.refs_1_, bf16[128,1024]{1,0:T(8,128)(2,1)S(1)} %get-tuple-element.37.refs_2_, bf16[128,1024]{1,0:T(8,128)(2,1)S(1)} %collective-permute-done.refs_5_.refs_3_, ...), custom_call_target="tpu_custom_call" | custom-call | flops 2214592512 | bytes 11796480 | tf_op jit(solution)/shard_map/pallas_call | solution.py:60
  76.6 6.2 %collective-permute-done.25.refs_1_ = bf16[96,1024]{1,0:T(8,128)(2,1)S(1)} collective-permute-done((bf16[96,1024]{1,0:T(8,128)(2,1)S(1)}, bf16[96,1024]{1,0:T(8,128)(2,1)S(1)}, u32[]{:S(2)}, u32[]{:S(2)}) %collective-permute-start.25) | collective-permute-done | bytes 196640 | tf_op jit(solution)/shard_map/ppermute | solution.py:372
  82.8 0.5 collective-permute-start.26
  83.3 4.5 %shard_map.119 = (bf16[96,1024]{1,0:T(8,128)(2,1)S(1)}, bf16[1,96,1024]{2,1,0:T(8,128)(2,1)S(1)}) custom-call(s32[2]{0:T(128)S(1)} %pad_add_fusion.refs_0_, bf16[96,1024]{1,0:T(8,128)(2,1)S(1)} %collective-permute-done.16.refs_1_, bf16[1,96,1024]{2,1,0:T(8,128)(2,1)S(1)} %collective-permute-done.17.refs_2_, bf16[704,2048]{1,0:T(8,128)(2,1)S(1)} %bitcast.46, ...), custom_call_target="tpu_custom_call" | custom-call | flops 830472192 | bytes 9437184 | tf_op jit(solution)/shard_map/pallas_call | solution.py:60
  87.8 1.6 %collective-permute-start.18 = (bf16[1,96,1024]{2,1,0:T(8,128)(2,1)S(1)}, bf16[1,96,1024]{2,1,0:T(8,128)(2,1)S(1)}, u32[]{:S(2)}, u32[]{:S(2)}) collective-permute-start(bf16[1,96,1024]{2,1,0:T(8,128)(2,1)S(1)} %get-tuple-element.54), channel_id=1, source_target_pairs={{0,1},{1,0},{2,3},{3,2},{4,5},{5,4},{6,7},{7,6},{8,9},{9,8},{10,11... | collective-permute-start | bytes 589832 | tf_op jit(solution)/shard_map/ppermute | solution.py:369
  89.4 4.3 %shard_map.120 = (bf16[96,1024]{1,0:T(8,128)(2,1)S(1)}, bf16[1,96,1024]{2,1,0:T(8,128)(2,1)S(1)}) custom-call(s32[2]{0:T(128)S(1)} %pad_add_fusion.refs_0_, bf16[96,1024]{1,0:T(8,128)(2,1)S(1)} %collective-permute-done.20.refs_1_, bf16[1,96,1024]{2,1,0:T(8,128)(2,1)S(1)} %collective-permute-done.21.refs_2_, bf16[704,2048]{1,0:T(8,128)(2,1)S(1)} %bitcast.47, ...), custom_call_target="tpu_custom_call" | custom-call | flops 830472192 | bytes 9437184 | tf_op jit(solution)/shard_map/pallas_call | solution.py:60
  93.7 0.6 collective-permute-start.22
  94.4 4.3 %shard_map.121 = (bf16[96,1024]{1,0:T(8,128)(2,1)S(1)}, bf16[1,96,1024]{2,1,0:T(8,128)(2,1)S(1)}) custom-call(s32[2]{0:T(128)S(1)} %pad_add_fusion.refs_0_, bf16[96,1024]{1,0:T(8,128)(2,1)S(1)} %collective-permute-done.25.refs_1_, bf16[1,96,1024]{2,1,0:T(8,128)(2,1)S(1)} %collective-permute-done.26.refs_2_, bf16[704,2048]{1,0:T(8,128)(2,1)S(1)} %bitcast.48, ...), custom_call_target="tpu_custom_call" | custom-call | flops 830472192 | bytes 9437184 | tf_op jit(solution)/shard_map/pallas_call | solution.py:60
  98.8 1.6 %collective-permute-start.27 = (bf16[1,96,1024]{2,1,0:T(8,128)(2,1)S(1)}, bf16[1,96,1024]{2,1,0:T(8,128)(2,1)S(1)}, u32[]{:S(2)}, u32[]{:S(2)}) collective-permute-start(bf16[1,96,1024]{2,1,0:T(8,128)(2,1)S(1)} %get-tuple-element.61), channel_id=1, source_target_pairs={{0,1},{1,0},{2,3},{3,2},{4,5},{5,4},{6,7},{7,6},{8,9},{9,8},{10,11... | collective-permute-start | bytes 589832 | tf_op jit(solution)/shard_map/ppermute | solution.py:369
  100.5 0.3 collective-permute-start.9
  100.7 0.5 collective-permute-start.14
  101.3 5.3 %collective-permute-done.27 = bf16[1,96,1024]{2,1,0:T(8,128)(2,1)S(1)} collective-permute-done((bf16[1,96,1024]{2,1,0:T(8,128)(2,1)S(1)}, bf16[1,96,1024]{2,1,0:T(8,128)(2,1)S(1)}, u32[]{:S(2)}, u32[]{:S(2)}) %collective-permute-start.27) | collective-permute-done | bytes 196640 | tf_op jit(solution)/shard_map/ppermute | solution.py:369
  106.6 0.2 collective-permute-start.23
  106.9 8.7 %collective-permute-done.19.refs_5_ = bf16[96,1024]{1,0:T(8,128)(2,1)S(1)} collective-permute-done((bf16[96,1024]{1,0:T(8,128)(2,1)S(1)}, bf16[96,1024]{1,0:T(8,128)(2,1)S(1)}, u32[]{:S(2)}, u32[]{:S(2)}) %collective-permute-start.19) | collective-permute-done | bytes 196640 | tf_op jit(solution)/shard_map/ppermute | solution.py:372
  115.6 2.3 %collective-permute-start.28 = (bf16[96,1024]{1,0:T(8,128)(2,1)S(1)}, bf16[96,1024]{1,0:T(8,128)(2,1)S(1)}, u32[]{:S(2)}, u32[]{:S(2)}) collective-permute-start(bf16[96,1024]{1,0:T(8,128)(2,1)S(1)} %fusion), channel_id=1, source_target_pairs={{0,28},{2,30},{4,24},{6,26},{8,20},{10,22},{12,16},{14,18},{16,12}... | collective-permute-start | bytes 589832 | tf_op jit(solution)/shard_map/ppermute | solution.py:372
  117.9 1.8 %shard_map.118 = (f32[2,128,1024]{2,1,0:T(8,128)S(1)}, bf16[2,128,1024]{2,1,0:T(8,128)(2,1)S(1)}) custom-call(s32[2]{0:T(128)S(1)} %pad_add_fusion.refs_0_, bf16[512,288]{1,0:T(8,128)(2,1)S(1)} %get-tuple-element.35.refs_1_, bf16[2,96,1024]{2,1,0:T(8,128)(2,1)S(1)} %collective-permute-done.9.refs_2_, ...), custom_call_target="tpu_custom_call" | custom-call | flops 603979776 | bytes 6324224 | tf_op jit(solution)/shard_map/pallas_call | solution.py:60
  120.0 2.6 %collective-permute-start.24 = (bf16[96,1024]{1,0:T(8,128)(2,1)S(1)}, bf16[96,1024]{1,0:T(8,128)(2,1)S(1)}, u32[]{:S(2)}, u32[]{:S(2)}) collective-permute-start(bf16[96,1024]{1,0:T(8,128)(2,1)S(1)} %get-tuple-element.73), channel_id=1, source_target_pairs={{0,24},{2,26},{4,28},{6,30},{8,16},{10,18},{12,20},{14,22},{16,8},... | collective-permute-start | bytes 589832 | tf_op jit(solution)/shard_map/ppermute | solution.py:372
  122.7 3.4 %collective-permute-done.28.refs_8_ = bf16[96,1024]{1,0:T(8,128)(2,1)S(1)} collective-permute-done((bf16[96,1024]{1,0:T(8,128)(2,1)S(1)}, bf16[96,1024]{1,0:T(8,128)(2,1)S(1)}, u32[]{:S(2)}, u32[]{:S(2)}) %collective-permute-start.28) | collective-permute-done | bytes 196640 | tf_op jit(solution)/shard_map/ppermute | solution.py:372
  126.1 0.5 collective-permute-start.33
  126.6 1.9 %collective-permute-done.15.refs_4_ = bf16[96,1024]{1,0:T(8,128)(2,1)S(1)} collective-permute-done((bf16[96,1024]{1,0:T(8,128)(2,1)S(1)}, bf16[96,1024]{1,0:T(8,128)(2,1)S(1)}, u32[]{:S(2)}, u32[]{:S(2)}) %collective-permute-start.15) | collective-permute-done | bytes 196640 | tf_op jit(solution)/shard_map/ppermute | solution.py:372
  128.6 3.9 %collective-permute-done.24.refs_7_ = bf16[96,1024]{1,0:T(8,128)(2,1)S(1)} collective-permute-done((bf16[96,1024]{1,0:T(8,128)(2,1)S(1)}, bf16[96,1024]{1,0:T(8,128)(2,1)S(1)}, u32[]{:S(2)}, u32[]{:S(2)}) %collective-permute-start.24) | collective-permute-done | bytes 196640 | tf_op jit(solution)/shard_map/ppermute | solution.py:372
  132.5 1.4 %collective-permute-done.32.refs_12_ = bf16[96,1024]{1,0:T(8,128)(2,1)S(1)} collective-permute-done((bf16[96,1024]{1,0:T(8,128)(2,1)S(1)}, bf16[96,1024]{1,0:T(8,128)(2,1)S(1)}, u32[]{:S(2)}, u32[]{:S(2)}) %collective-permute-start.32) | collective-permute-done | bytes 196640 | tf_op jit(solution)/shard_map/ppermute | solution.py:372
  133.9 0.2 collective-permute-done.13.refs_3_
  134.1 2.0 %shard_map.122 = (bf16[128,1024]{1,0:T(8,128)(2,1)}, bf16[128,1024]{1,0:T(8,128)(2,1)}) custom-call(s32[2]{0:T(128)S(1)} %pad_add_fusion.refs_0_, bf16[512,480]{1,0:T(8,128)(2,1)S(1)} %get-tuple-element.34.refs_1_, f32[2,128,1024]{2,1,0:T(8,128)S(1)} %get-tuple-element.48.refs_2_, bf16[2,128,1024]{2,1,0:T(8,128)(2,1)S(1)} %collective-permute-done.13.refs_3_, ...), custom_call_target="tpu_custom_call" | custom-call | flops 503316480 | bytes 4554752 | tf_op jit(solution)/shard_map/pallas_call | solution.py:60
  (60 shorter events, 1.4 us)
Async XLA Ops:
  3.0 17.0 %collective-permute-start.4 = (bf16[240,1024]{1,0:T(8,128)(2,1)S(1)}, bf16[240,1024]{1,0:T(8,128)(2,1)S(1)}, u32[]{:S(2)}, u32[]{:S(2)}) collective-permute-start(bf16[240,1024]{1,0:T(8,128)(2,1)S(1)} %get-tuple-element.41), channel_id=1, source_target_pairs={{0,2},{2,0},{4,6},{6,4},{8,10},{10,8},{12,14},{14,12},{16,18},{18,... | collective-permute-start | bytes 1474568 | tf_op jit(solution)/shard_map/ppermute | solution.py:372
  3.6 10.0 %collective-permute-start = (bf16[128,1024]{1,0:T(8,128)(2,1)}, bf16[128,1024]{1,0:T(8,128)(2,1)S(1)}, u32[]{:S(2)}, u32[]{:S(2)}) collective-permute-start(bf16[128,1024]{1,0:T(8,128)(2,1)} %refs_3_.1), channel_id=1, source_target_pairs={{0,1},{1,0},{2,3},{3,2},{4,5},{5,4},{6,7},{7,6},{8,9},{9,8},{10,11... | collective-permute-start | bytes 786440 | tf_op jit(solution)/shard_map/ppermute | solution.py:369
  6.1 12.7 %collective-permute-start.1 = (bf16[128,1024]{1,0:T(8,128)(2,1)}, bf16[128,1024]{1,0:T(8,128)(2,1)S(1)}, u32[]{:S(2)}, u32[]{:S(2)}) collective-permute-start(bf16[128,1024]{1,0:T(8,128)(2,1)} %refs_4_.1), channel_id=1, source_target_pairs={{0,1},{1,0},{2,3},{3,2},{4,5},{5,4},{6,7},{7,6},{8,9},{9,8},{10,11... | collective-permute-start | bytes 786440 | tf_op jit(solution)/shard_map/ppermute | solution.py:369
  18.9 39.9 %copy-start.2 = (bf16[1,704,2048]{2,1,0:T(8,128)(2,1)S(1)}, bf16[1,704,2048]{2,1,0:T(8,128)(2,1)}, u32[]{:S(2)}) copy-start(bf16[1,704,2048]{2,1,0:T(8,128)(2,1)} %param.19) | copy-start | bytes 8650756
  19.9 15.7 %collective-permute-start.2 = (bf16[3,2,48,1024]{3,2,1,0:T(8,128)(2,1)S(1)}, bf16[3,2,48,1024]{3,2,1,0:T(8,128)(2,1)S(1)}, u32[]{:S(2)}, u32[]{:S(2)}) collective-permute-start(bf16[3,2,48,1024]{3,2,1,0:T(8,128)(2,1)S(1)} %get-tuple-element.39), channel_id=1, source_target_pairs={{0,2},{2,0},{4,6},{6,4},{8,10},{10,8},{12,14},{14,12},{16,18},{18,... | collective-permute-start | bytes 1769480 | tf_op jit(solution)/shard_map/ppermute | solution.py:372
  20.0 7.4 %collective-permute-start.5 = (bf16[96,1024]{1,0:T(8,128)(2,1)S(1)}, bf16[96,1024]{1,0:T(8,128)(2,1)S(1)}, u32[]{:S(2)}, u32[]{:S(2)}) collective-permute-start(bf16[96,1024]{1,0:T(8,128)(2,1)S(1)} %pad_maximum_fusion.5), channel_id=1, source_target_pairs={{0,8},{2,10},{4,12},{6,14},{8,0},{10,2},{12,4},{14,6},{16,24},{18,... | collective-permute-start | bytes 589832 | tf_op jit(solution)/shard_map/ppermute | solution.py:372
  21.9 12.0 %collective-permute-start.7 = (bf16[96,1024]{1,0:T(8,128)(2,1)S(1)}, bf16[96,1024]{1,0:T(8,128)(2,1)S(1)}, u32[]{:S(2)}, u32[]{:S(2)}) collective-permute-start(bf16[96,1024]{1,0:T(8,128)(2,1)S(1)} %pad_maximum_fusion.6), channel_id=1, source_target_pairs={{0,24},{2,26},{4,28},{6,30},{8,16},{10,18},{12,20},{14,22},{16,8},... | collective-permute-start | bytes 589832 | tf_op jit(solution)/shard_map/ppermute | solution.py:372
  24.5 34.3 %copy-start.1 = (bf16[1,704,2048]{2,1,0:T(8,128)(2,1)S(1)}, bf16[1,704,2048]{2,1,0:T(8,128)(2,1)}, u32[]{:S(2)}) copy-start(bf16[1,704,2048]{2,1,0:T(8,128)(2,1)} %param.18) | copy-start | bytes 8650756
  24.5 34.2 %copy-start = (bf16[1,704,2048]{2,1,0:T(8,128)(2,1)S(1)}, bf16[1,704,2048]{2,1,0:T(8,128)(2,1)}, u32[]{:S(2)}) copy-start(bf16[1,704,2048]{2,1,0:T(8,128)(2,1)} %param.17) | copy-start | bytes 8650756
  34.0 10.7 %collective-permute-start.8 = (bf16[2,96,1024]{2,1,0:T(8,128)(2,1)S(1)}, bf16[2,96,1024]{2,1,0:T(8,128)(2,1)S(1)}, u32[]{:S(2)}, u32[]{:S(2)}) collective-permute-start(bf16[2,96,1024]{2,1,0:T(8,128)(2,1)S(1)} %pad_maximum_fusion.4), channel_id=1, source_target_pairs={{0,1},{1,0},{2,3},{3,2},{4,5},{5,4},{6,7},{7,6},{8,9},{9,8},{10,11... | collective-permute-start | bytes 1179656 | tf_op jit(solution)/shard_map/ppermute | solution.py:369
  35.7 23.0 %collective-permute-start.3 = (bf16[2,96,1024]{2,1,0:T(8,128)(2,1)S(1)}, bf16[2,96,1024]{2,1,0:T(8,128)(2,1)S(1)}, u32[]{:S(2)}, u32[]{:S(2)}) collective-permute-start(bf16[2,96,1024]{2,1,0:T(8,128)(2,1)S(1)} %pad_maximum_fusion.2), channel_id=1, source_target_pairs={{0,4},{2,6},{4,0},{6,2},{8,12},{10,14},{12,8},{14,10},{16,20},{18,... | collective-permute-start | bytes 1179656 | tf_op jit(solution)/shard_map/ppermute | solution.py:372
  37.3 21.4 %collective-permute-start.6 = (bf16[2,96,1024]{2,1,0:T(8,128)(2,1)S(1)}, bf16[2,96,1024]{2,1,0:T(8,128)(2,1)S(1)}, u32[]{:S(2)}, u32[]{:S(2)}) collective-permute-start(bf16[2,96,1024]{2,1,0:T(8,128)(2,1)S(1)} %pad_maximum_fusion.3), channel_id=1, source_target_pairs={{0,12},{2,14},{4,8},{6,10},{8,4},{10,6},{12,0},{14,2},{16,28},{18,... | collective-permute-start | bytes 1179656 | tf_op jit(solution)/shard_map/ppermute | solution.py:372
  38.8 31.1 %collective-permute-start.16 = (bf16[96,1024]{1,0:T(8,128)(2,1)S(1)}, bf16[96,1024]{1,0:T(8,128)(2,1)S(1)}, u32[]{:S(2)}, u32[]{:S(2)}) collective-permute-start(bf16[96,1024]{1,0:T(8,128)(2,1)S(1)} %pad_maximum_fusion.7), channel_id=1, source_target_pairs={{0,16},{2,18},{4,20},{6,22},{8,24},{10,26},{12,28},{14,30},{16,0},... | collective-permute-start | bytes 589832 | tf_op jit(solution)/shard_map/ppermute | solution.py:372
  40.3 30.2 %collective-permute-start.20 = (bf16[96,1024]{1,0:T(8,128)(2,1)S(1)}, bf16[96,1024]{1,0:T(8,128)(2,1)S(1)}, u32[]{:S(2)}, u32[]{:S(2)}) collective-permute-start(bf16[96,1024]{1,0:T(8,128)(2,1)S(1)} %pad_maximum_fusion.8), channel_id=1, source_target_pairs={{0,20},{2,22},{4,16},{6,18},{8,28},{10,30},{12,24},{14,26},{16,4},... | collective-permute-start | bytes 589832 | tf_op jit(solution)/shard_map/ppermute | solution.py:372
  58.7 13.2 %copy-start.3 = (bf16[704,2048]{1,0:T(8,128)(2,1)S(1)}, bf16[704,2048]{1,0:T(8,128)(2,1)}, u32[]{:S(2)}) copy-start(bf16[704,2048]{1,0:T(8,128)(2,1)} %refs_5_.1) | copy-start | bytes 8650756
  58.7 13.2 %copy-start.4 = (bf16[704,2048]{1,0:T(8,128)(2,1)S(1)}, bf16[704,2048]{1,0:T(8,128)(2,1)}, u32[]{:S(2)}) copy-start(bf16[704,2048]{1,0:T(8,128)(2,1)} %refs_6_.1) | copy-start | bytes 8650756
  58.7 13.2 %copy-start.5 = (bf16[704,2048]{1,0:T(8,128)(2,1)S(1)}, bf16[704,2048]{1,0:T(8,128)(2,1)}, u32[]{:S(2)}) copy-start(bf16[704,2048]{1,0:T(8,128)(2,1)} %refs_7_.1) | copy-start | bytes 8650756
  64.3 30.0 %collective-permute-start.11 = (bf16[2,96,1024]{2,1,0:T(8,128)(2,1)S(1)}, bf16[2,96,1024]{2,1,0:T(8,128)(2,1)S(1)}, u32[]{:S(2)}, u32[]{:S(2)}) collective-permute-start(bf16[2,96,1024]{2,1,0:T(8,128)(2,1)S(1)} %get-tuple-element.45), channel_id=1, source_target_pairs={{0,12},{2,14},{4,8},{6,10},{8,4},{10,6},{12,0},{14,2},{16,28},{18,... | collective-permute-start | bytes 1179656 | tf_op jit(solution)/shard_map/ppermute | solution.py:372
  64.9 29.4 %collective-permute-start.10 = (bf16[2,96,1024]{2,1,0:T(8,128)(2,1)S(1)}, bf16[2,96,1024]{2,1,0:T(8,128)(2,1)S(1)}, u32[]{:S(2)}, u32[]{:S(2)}) collective-permute-start(bf16[2,96,1024]{2,1,0:T(8,128)(2,1)S(1)} %get-tuple-element.44), channel_id=1, source_target_pairs={{0,4},{2,6},{4,0},{6,2},{8,12},{10,14},{12,8},{14,10},{16,20},{18,... | collective-permute-start | bytes 1179656 | tf_op jit(solution)/shard_map/ppermute | solution.py:372
  66.0 16.9 %collective-permute-start.25 = (bf16[96,1024]{1,0:T(8,128)(2,1)S(1)}, bf16[96,1024]{1,0:T(8,128)(2,1)S(1)}, u32[]{:S(2)}, u32[]{:S(2)}) collective-permute-start(bf16[96,1024]{1,0:T(8,128)(2,1)S(1)} %pad_maximum_fusion.9), channel_id=1, source_target_pairs={{0,28},{2,30},{4,24},{6,26},{8,20},{10,22},{12,16},{14,18},{16,12}... | collective-permute-start | bytes 589832 | tf_op jit(solution)/shard_map/ppermute | solution.py:372
  69.9 13.4 %collective-permute-start.17 = (bf16[1,96,1024]{2,1,0:T(8,128)(2,1)S(1)}, bf16[1,96,1024]{2,1,0:T(8,128)(2,1)S(1)}, u32[]{:S(2)}, u32[]{:S(2)}) collective-permute-start(bf16[1,96,1024]{2,1,0:T(8,128)(2,1)S(1)} %bitcast.62), channel_id=1, source_target_pairs={{0,1},{1,0},{2,3},{3,2},{4,5},{5,4},{6,7},{7,6},{8,9},{9,8},{10,11... | collective-permute-start | bytes 589832 | tf_op jit(solution)/shard_map/ppermute | solution.py:369
  70.4 19.0 %collective-permute-start.21 = (bf16[1,96,1024]{2,1,0:T(8,128)(2,1)S(1)}, bf16[1,96,1024]{2,1,0:T(8,128)(2,1)S(1)}, u32[]{:S(2)}, u32[]{:S(2)}) collective-permute-start(bf16[1,96,1024]{2,1,0:T(8,128)(2,1)S(1)} %bitcast.61), channel_id=1, source_target_pairs={{0,1},{1,0},{2,3},{3,2},{4,5},{5,4},{6,7},{7,6},{8,9},{9,8},{10,11... | collective-permute-start | bytes 589832 | tf_op jit(solution)/shard_map/ppermute | solution.py:369
  82.8 11.6 %collective-permute-start.26 = (bf16[1,96,1024]{2,1,0:T(8,128)(2,1)S(1)}, bf16[1,96,1024]{2,1,0:T(8,128)(2,1)S(1)}, u32[]{:S(2)}, u32[]{:S(2)}) collective-permute-start(bf16[1,96,1024]{2,1,0:T(8,128)(2,1)S(1)} %bitcast.63), channel_id=1, source_target_pairs={{0,1},{1,0},{2,3},{3,2},{4,5},{5,4},{6,7},{7,6},{8,9},{9,8},{10,11... | collective-permute-start | bytes 589832 | tf_op jit(solution)/shard_map/ppermute | solution.py:369
  87.8 12.5 %collective-permute-start.18 = (bf16[1,96,1024]{2,1,0:T(8,128)(2,1)S(1)}, bf16[1,96,1024]{2,1,0:T(8,128)(2,1)S(1)}, u32[]{:S(2)}, u32[]{:S(2)}) collective-permute-start(bf16[1,96,1024]{2,1,0:T(8,128)(2,1)S(1)} %get-tuple-element.54), channel_id=1, source_target_pairs={{0,1},{1,0},{2,3},{3,2},{4,5},{5,4},{6,7},{7,6},{8,9},{9,8},{10,11... | collective-permute-start | bytes 589832 | tf_op jit(solution)/shard_map/ppermute | solution.py:369
  93.7 7.0 %collective-permute-start.22 = (bf16[1,96,1024]{2,1,0:T(8,128)(2,1)S(1)}, bf16[1,96,1024]{2,1,0:T(8,128)(2,1)S(1)}, u32[]{:S(2)}, u32[]{:S(2)}) collective-permute-start(bf16[1,96,1024]{2,1,0:T(8,128)(2,1)S(1)} %get-tuple-element.57), channel_id=1, source_target_pairs={{0,1},{1,0},{2,3},{3,2},{4,5},{5,4},{6,7},{7,6},{8,9},{9,8},{10,11... | collective-permute-start | bytes 589832 | tf_op jit(solution)/shard_map/ppermute | solution.py:369
  94.4 23.5 %collective-permute-start.12 = (bf16[2,2,96,1024]{3,2,1,0:T(8,128)(2,1)S(1)}, bf16[2,2,96,1024]{3,2,1,0:T(8,128)(2,1)S(1)}, u32[]{:S(2)}, u32[]{:S(2)}) collective-permute-start(bf16[2,2,96,1024]{3,2,1,0:T(8,128)(2,1)S(1)} %pad_maximum_fusion), channel_id=1, source_target_pairs={{0,2},{2,0},{4,6},{6,4},{8,10},{10,8},{12,14},{14,12},{16,18},{18,... | collective-permute-start | bytes 2359304 | tf_op jit(solution)/shard_map/ppermute | solution.py:372
  98.8 7.8 %collective-permute-start.27 = (bf16[1,96,1024]{2,1,0:T(8,128)(2,1)S(1)}, bf16[1,96,1024]{2,1,0:T(8,128)(2,1)S(1)}, u32[]{:S(2)}, u32[]{:S(2)}) collective-permute-start(bf16[1,96,1024]{2,1,0:T(8,128)(2,1)S(1)} %get-tuple-element.61), channel_id=1, source_target_pairs={{0,1},{1,0},{2,3},{3,2},{4,5},{5,4},{6,7},{7,6},{8,9},{9,8},{10,11... | collective-permute-start | bytes 589832 | tf_op jit(solution)/shard_map/ppermute | solution.py:369
  100.4 15.2 %collective-permute-start.19 = (bf16[96,1024]{1,0:T(8,128)(2,1)S(1)}, bf16[96,1024]{1,0:T(8,128)(2,1)S(1)}, u32[]{:S(2)}, u32[]{:S(2)}) collective-permute-start(bf16[96,1024]{1,0:T(8,128)(2,1)S(1)} %fusion.3), channel_id=1, source_target_pairs={{0,16},{2,18},{4,20},{6,22},{8,24},{10,26},{12,28},{14,30},{16,0},... | collective-permute-start | bytes 589832 | tf_op jit(solution)/shard_map/ppermute | solution.py:372
  100.5 17.4 %collective-permute-start.9 = (bf16[2,96,1024]{2,1,0:T(8,128)(2,1)S(1)}, bf16[2,96,1024]{2,1,0:T(8,128)(2,1)S(1)}, u32[]{:S(2)}, u32[]{:S(2)}) collective-permute-start(bf16[2,96,1024]{2,1,0:T(8,128)(2,1)S(1)} %get-tuple-element.43.refs_6_), channel_id=1, source_target_pairs={{0,2},{2,0},{4,6},{6,4},{8,10},{10,8},{12,14},{14,12},{16,18},{18,... | collective-permute-start | bytes 1179656 | tf_op jit(solution)/shard_map/ppermute | solution.py:372
  100.7 19.0 %collective-permute-start.14 = (bf16[2,96,1024]{2,1,0:T(8,128)(2,1)S(1)}, bf16[2,96,1024]{2,1,0:T(8,128)(2,1)S(1)}, u32[]{:S(2)}, u32[]{:S(2)}) collective-permute-start(bf16[2,96,1024]{2,1,0:T(8,128)(2,1)S(1)} %get-tuple-element.51), channel_id=1, source_target_pairs={{0,1},{1,0},{2,3},{3,2},{4,5},{5,4},{6,7},{7,6},{8,9},{9,8},{10,11... | collective-permute-start | bytes 1179656 | tf_op jit(solution)/shard_map/ppermute | solution.py:369
  106.6 13.4 %collective-permute-start.23 = (bf16[96,1024]{1,0:T(8,128)(2,1)S(1)}, bf16[96,1024]{1,0:T(8,128)(2,1)S(1)}, u32[]{:S(2)}, u32[]{:S(2)}) collective-permute-start(bf16[96,1024]{1,0:T(8,128)(2,1)S(1)} %fusion.2), channel_id=1, source_target_pairs={{0,20},{2,22},{4,16},{6,18},{8,28},{10,30},{12,24},{14,26},{16,4},... | collective-permute-start | bytes 589832 | tf_op jit(solution)/shard_map/ppermute | solution.py:372
  115.6 10.5 %collective-permute-start.28 = (bf16[96,1024]{1,0:T(8,128)(2,1)S(1)}, bf16[96,1024]{1,0:T(8,128)(2,1)S(1)}, u32[]{:S(2)}, u32[]{:S(2)}) collective-permute-start(bf16[96,1024]{1,0:T(8,128)(2,1)S(1)} %fusion), channel_id=1, source_target_pairs={{0,28},{2,30},{4,24},{6,26},{8,20},{10,22},{12,16},{14,18},{16,12}... | collective-permute-start | bytes 589832 | tf_op jit(solution)/shard_map/ppermute | solution.py:372
  117.9 8.2 %collective-permute-start.30 = (bf16[96,1024]{1,0:T(8,128)(2,1)S(1)}, bf16[96,1024]{1,0:T(8,128)(2,1)S(1)}, u32[]{:S(2)}, u32[]{:S(2)}) collective-permute-start(bf16[96,1024]{1,0:T(8,128)(2,1)S(1)} %collective-permute-done.19.refs_5_), channel_id=1, source_target_pairs={{0,2},{2,0},{4,6},{6,4},{8,10},{10,8},{12,14},{14,12},{16,18},{18,... | collective-permute-start | bytes 589832 | tf_op jit(solution)/shard_map/ppermute | solution.py:372
  119.7 14.4 %collective-permute-start.13 = (bf16[2,128,1024]{2,1,0:T(8,128)(2,1)S(1)}, bf16[2,128,1024]{2,1,0:T(8,128)(2,1)S(1)}, u32[]{:S(2)}, u32[]{:S(2)}) collective-permute-start(bf16[2,128,1024]{2,1,0:T(8,128)(2,1)S(1)} %get-tuple-element.49), channel_id=1, source_target_pairs={{0,1},{1,0},{2,3},{3,2},{4,5},{5,4},{6,7},{7,6},{8,9},{9,8},{10,11... | collective-permute-start | bytes 1572872 | tf_op jit(solution)/shard_map/ppermute | solution.py:369
  119.9 8.6 %collective-permute-start.15 = (bf16[96,1024]{1,0:T(8,128)(2,1)S(1)}, bf16[96,1024]{1,0:T(8,128)(2,1)S(1)}, u32[]{:S(2)}, u32[]{:S(2)}) collective-permute-start(bf16[96,1024]{1,0:T(8,128)(2,1)S(1)} %get-tuple-element.74), channel_id=1, source_target_pairs={{0,8},{2,10},{4,12},{6,14},{8,0},{10,2},{12,4},{14,6},{16,24},{18,... | collective-permute-start | bytes 589832 | tf_op jit(solution)/shard_map/ppermute | solution.py:372
  120.0 12.4 %collective-permute-start.24 = (bf16[96,1024]{1,0:T(8,128)(2,1)S(1)}, bf16[96,1024]{1,0:T(8,128)(2,1)S(1)}, u32[]{:S(2)}, u32[]{:S(2)}) collective-permute-start(bf16[96,1024]{1,0:T(8,128)(2,1)S(1)} %get-tuple-element.73), channel_id=1, source_target_pairs={{0,24},{2,26},{4,28},{6,30},{8,16},{10,18},{12,20},{14,22},{16,8},... | collective-permute-start | bytes 589832 | tf_op jit(solution)/shard_map/ppermute | solution.py:372
  126.1 6.4 %collective-permute-start.31 = (bf16[96,1024]{1,0:T(8,128)(2,1)S(1)}, bf16[96,1024]{1,0:T(8,128)(2,1)S(1)}, u32[]{:S(2)}, u32[]{:S(2)}) collective-permute-start(bf16[96,1024]{1,0:T(8,128)(2,1)S(1)} %collective-permute-done.23.refs_6_), channel_id=1, source_target_pairs={{0,2},{2,0},{4,6},{6,4},{8,10},{10,8},{12,14},{14,12},{16,18},{18,... | collective-permute-start | bytes 589832 | tf_op jit(solution)/shard_map/ppermute | solution.py:372
  126.1 6.4 %collective-permute-start.33 = (bf16[96,1024]{1,0:T(8,128)(2,1)S(1)}, bf16[96,1024]{1,0:T(8,128)(2,1)S(1)}, u32[]{:S(2)}, u32[]{:S(2)}) collective-permute-start(bf16[96,1024]{1,0:T(8,128)(2,1)S(1)} %collective-permute-done.28.refs_8_), channel_id=1, source_target_pairs={{0,2},{2,0},{4,6},{6,4},{8,10},{10,8},{12,14},{14,12},{16,18},{18,... | collective-permute-start | bytes 589832 | tf_op jit(solution)/shard_map/ppermute | solution.py:372
  128.5 4.0 %collective-permute-start.29 = (bf16[96,1024]{1,0:T(8,128)(2,1)S(1)}, bf16[96,1024]{1,0:T(8,128)(2,1)S(1)}, u32[]{:S(2)}, u32[]{:S(2)}) collective-permute-start(bf16[96,1024]{1,0:T(8,128)(2,1)S(1)} %collective-permute-done.15.refs_4_), channel_id=1, source_target_pairs={{0,2},{2,0},{4,6},{6,4},{8,10},{10,8},{12,14},{14,12},{16,18},{18,... | collective-permute-start | bytes 589832 | tf_op jit(solution)/shard_map/ppermute | solution.py:372
  132.5 1.4 %collective-permute-start.32 = (bf16[96,1024]{1,0:T(8,128)(2,1)S(1)}, bf16[96,1024]{1,0:T(8,128)(2,1)S(1)}, u32[]{:S(2)}, u32[]{:S(2)}) collective-permute-start(bf16[96,1024]{1,0:T(8,128)(2,1)S(1)} %collective-permute-done.24.refs_7_), channel_id=1, source_target_pairs={{0,2},{2,0},{4,6},{6,4},{8,10},{10,8},{12,14},{14,12},{16,18},{18,... | collective-permute-start | bytes 589832 | tf_op jit(solution)/shard_map/ppermute | solution.py:372

commit v3 on v2

--- a/solution.py
+++ b/solution.py
@@ -8,9 +8,9 @@
 from jax.sharding import PartitionSpec as P
 
 
-WHOLE_OUT = (1, 3,)
+WHOLE_OUT = (1, 2,)
 WHOLE_BACK = (1, 3,)
-GROUPS = ((4,), (5,), (0, 1, 2, 3, 6,), (7,))
+GROUPS = ((4,), (2, 5,), (0, 1, 3, 6,), (7,))
 
 
 BF = jnp.bfloat16
@@ -195,20 +195,35 @@
     )
 
 
+def transposed(scalars, weights):
+    def body(_, bufs, outs, ready):
+        for i in range(len(weights)):
+            ready(i)
+            outs[i][...] = jnp.transpose(bufs[i][...])
+
+    return local_call(
+        body, scalars, weights, [shaped(w.shape[::-1]) for w in weights], staged=len(weights)
+    )
+
+
 def ffn(scalar_ref, xs, gs, weight_refs):
     half = xs[0].shape[1]
-    gate_w, up_w, down_w = (
-        [
-            w.at[:, pl.ds(pl.multiple_of(jnp.bitwise_xor(scalar_ref[1], i) * half, half), half)]
-            for i in range(2)
-        ]
-        for w in weight_refs
-    )
-    gate_pre = mmt(xs[0], gate_w[0][...]) + mmt(xs[1], gate_w[1][...])
-    up_pre = mmt(xs[0], up_w[0][...]) + mmt(xs[1], up_w[1][...])
+    parts = [
+        pl.ds(pl.multiple_of(jnp.bitwise_xor(scalar_ref[1], i) * half, half), half)
+        for i in range(2)
+    ]
+    gate_w, up_w, down_w = ([w.at[:, part] for part in parts] for w in weight_refs[:3])
+
+    def over_features(rows, w):
+        if len(weight_refs) > 3:
+            return sum(mm(rows[i], weight_refs[3 + w][parts[i], :]) for i in range(2))
+        return sum(mmt(rows[i], weight_refs[w][:, parts[i]]) for i in range(2))
+
+    gate_pre = over_features(xs, 0)
+    up_pre = over_features(xs, 1)
     act, slope = silu_parts(gate_pre)
     hidden = (act * up_pre).astype(BF)
-    grad_hidden = mmt(gs[0], down_w[0][...]) + mmt(gs[1], down_w[1][...])
+    grad_hidden = over_features(gs, 2)
     grad_gate = (grad_hidden * up_pre * slope).astype(BF)
     grad_up = (grad_hidden * act).astype(BF)
     values = [mm(hidden, down_w[i][...]) for i in range(2)]
@@ -400,6 +415,7 @@
     shared_own, shared_other = shared_ffn(
         scalars, tokens_here, tokens_other, cotangent_here, cotangent_other, shared
     )
+    routed_both = (*routed, *transposed(scalars, routed))
     home = {}
     for group in GROUPS:
         halves = [arrived[q] for q in group if q in out_halves]
@@ -409,7 +425,7 @@
             other = across(other)
         whole = [q not in back_halves for q in group]
         ins = [arrived[q] for q in group]
-        results = routed_ffn(scalars, ins, other, whole, routed, cap)
+        results = routed_ffn(scalars, ins, other, whole, routed_both, cap)
         rest = across(results[-1]) if not all(whole) else None
         used = 0
         for q, entire, result in zip(group, whole, results):

time: 138 us -> 127 us (0.920)
  waiting for transfers between devices: 69 us -> 45.7 us
  starting transfers between devices: 34.2 us -> 46.6 us
    ppermute x23, waiting for transfers between devices: 49.1 us -> 36.4 us  [exchange(): return lax.ppermute(values, 'expert', [(i, i ^ k) for i in range(experts)])]
    ppermute x23, starting transfers between devices: 23.1 us -> 34 us  [exchange(): return lax.ppermute(values, 'expert', [(i, i ^ k) for i in range(experts)])]
    ppermute x11, waiting for transfers between devices: 19.9 us -> 9.36 us  [across(): return lax.ppermute(values, 'tensor', [(0, 1), (1, 0)])]
    ppermute x11, starting transfers between devices: 11.1 us -> 12.6 us  [across(): return lax.ppermute(values, 'tensor', [(0, 1), (1, 0)])]
    pallas_call x10 -> x11, Pallas kernels: 31.1 us -> 32.4 us  [local_call(): pl.pallas_call(kernel, out_shape=list(outs), in_specs=[pl.BlockSpec(memor...]
  transfers between devices with their start and end apart: 34 -> 34, of which waited for: 14 -> 13; matrix products, arithmetic and copies ran while one was open for 0% -> 1% of each run, Pallas kernels for 20% -> 22%
where the time goes in v3:
time: 127 us
  starting transfers between devices  46.6 us (37%)
  waiting for transfers between devices  45.7 us (36%)
  Pallas kernels  32.4 us (26%)
    ppermute x23, waiting for transfers between devices, exchange(): return lax.ppermute(values, 'expert', [(i, i ^ k) for i in range(experts)])  36.4 us
    ppermute x23, starting transfers between devices, exchange(): return lax.ppermute(values, 'expert', [(i, i ^ k) for i in range(experts)])  34 us
    pallas_call x11, Pallas kernels, local_call(): pl.pallas_call(kernel, out_shape=list(outs), in_specs=[pl.BlockSpec(memor...  32.4 us
    ppermute x11, starting transfers between devices, across(): return lax.ppermute(values, 'tensor', [(0, 1), (1, 0)])  12.6 us
    ppermute x11, waiting for transfers between devices, across(): return lax.ppermute(values, 'tensor', [(0, 1), (1, 0)])  9.36 us
  transfers between devices with their start and end apart: 34, of which 13 were waited for; matrix products, arithmetic and copies ran while one was open for 1% of the time, Pallas kernels for 22%

profile of v3, /device:TPU:0, one launch (start us, length us, event | category | flops | bytes accessed | tf_op | source)
XLA Modules:
  0.0 126.6 jit_solution(11793068899529665148)
XLA Ops:
  0.7 2.2 %shard_map.113 = (bf16[48,1024]{1,0:T(8,128)(2,1)S(1)}, bf16[48,1024]{1,0:T(8,128)(2,1)S(1)}, bf16[48,1024]{1,0:T(8,128)(2,1)S(1)}, bf16[48,1024]{1,0:T(8,128)(2...) custom-call(s32[2]{0:T(128)S(1)} %pad_add_fusion.refs_0_, ...), custom_call_target="tpu_custom_call" | custom-call | flops 201326592 | bytes 2430976 | tf_op jit(solution)/shard_map/pallas_call | solution.py:60
  3.0 0.6 collective-permute-start.4
  3.5 2.6 %collective-permute-start = (bf16[128,1024]{1,0:T(8,128)(2,1)}, bf16[128,1024]{1,0:T(8,128)(2,1)S(1)}, u32[]{:S(2)}, u32[]{:S(2)}) collective-permute-start(bf16[128,1024]{1,0:T(8,128)(2,1)} %refs_3_.1), channel_id=1, source_target_pairs={{0,1},{1,0},{2,3},{3,2},{4,5},{5,4},{6,7},{7,6},{8,9},{9,8},{10,11... | collective-permute-start | bytes 786440 | tf_op jit(solution)/shard_map/ppermute | solution.py:384
  6.2 0.8 shard_map.114
  7.0 5.0 %shard_map.116 = (bf16[2048,704]{1,0:T(8,128)(2,1)S(1)}, bf16[2048,704]{1,0:T(8,128)(2,1)S(1)}, bf16[2048,704]{1,0:T(8,128)(2,1)S(1)}) custom-call(s32[2]{0:T(128)S(1)} %pad_add_fusion.refs_0_, bf16[704,2048]{1,0:T(8,128)(2,1)} %bitcast.45, bf16[704,2048]{1,0:T(8,128)(2,1)} %bitcast.50, bf16[704,2048]{1,0:T(8,128)(2,1)} %bitcast.55), custom_call_target="tpu_custom_call" | custom-call | bytes 17301504 | tf_op jit(solution)/shard_map/pallas_call | solution.py:60
  12.0 1.4 %collective-permute-done.refs_5_.refs_3_ = bf16[128,1024]{1,0:T(8,128)(2,1)S(1)} collective-permute-done((bf16[128,1024]{1,0:T(8,128)(2,1)}, bf16[128,1024]{1,0:T(8,128)(2,1)S(1)}, u32[]{:S(2)}, u32[]{:S(2)}) %collective-permute-start) | collective-permute-done | bytes 262176 | tf_op jit(solution)/shard_map/ppermute | solution.py:384
  13.5 5.4 %collective-permute-done.1.refs_6_.refs_4_ = bf16[128,1024]{1,0:T(8,128)(2,1)S(1)} collective-permute-done((bf16[128,1024]{1,0:T(8,128)(2,1)}, bf16[128,1024]{1,0:T(8,128)(2,1)S(1)}, u32[]{:S(2)}, u32[]{:S(2)}) %collective-permute-start.1) | collective-permute-done | bytes 262176 | tf_op jit(solution)/shard_map/ppermute | solution.py:384
  18.8 1.0 shard_map.115
  20.0 2.8 %collective-permute-start.5 = (bf16[96,1024]{1,0:T(8,128)(2,1)S(1)}, bf16[96,1024]{1,0:T(8,128)(2,1)S(1)}, u32[]{:S(2)}, u32[]{:S(2)}) collective-permute-start(bf16[96,1024]{1,0:T(8,128)(2,1)S(1)} %pad_maximum_fusion.5), channel_id=1, source_target_pairs={{0,12},{2,14},{4,8},{6,10},{8,4},{10,6},{12,0},{14,2},{16,28},{18,... | collective-permute-start | bytes 589832 | tf_op jit(solution)/shard_map/ppermute | solution.py:387
  22.8 2.5 %collective-permute-start.6 = (bf16[96,1024]{1,0:T(8,128)(2,1)S(1)}, bf16[96,1024]{1,0:T(8,128)(2,1)S(1)}, u32[]{:S(2)}, u32[]{:S(2)}) collective-permute-start(bf16[96,1024]{1,0:T(8,128)(2,1)S(1)} %pad_maximum_fusion.6), channel_id=1, source_target_pairs={{0,24},{2,26},{4,28},{6,30},{8,16},{10,18},{12,20},{14,22},{16,8},... | collective-permute-start | bytes 589832 | tf_op jit(solution)/shard_map/ppermute | solution.py:387
  25.4 2.9 %collective-permute-done.5.refs_3_ = bf16[96,1024]{1,0:T(8,128)(2,1)S(1)} collective-permute-done((bf16[96,1024]{1,0:T(8,128)(2,1)S(1)}, bf16[96,1024]{1,0:T(8,128)(2,1)S(1)}, u32[]{:S(2)}, u32[]{:S(2)}) %collective-permute-start.5) | collective-permute-done | bytes 196640 | tf_op jit(solution)/shard_map/ppermute | solution.py:387
  28.3 6.5 %collective-permute-done.6.refs_4_ = bf16[96,1024]{1,0:T(8,128)(2,1)S(1)} collective-permute-done((bf16[96,1024]{1,0:T(8,128)(2,1)S(1)}, bf16[96,1024]{1,0:T(8,128)(2,1)S(1)}, u32[]{:S(2)}, u32[]{:S(2)}) %collective-permute-start.6) | collective-permute-done | bytes 196640 | tf_op jit(solution)/shard_map/ppermute | solution.py:387
  34.9 1.6 %collective-permute-start.7 = (bf16[2,96,1024]{2,1,0:T(8,128)(2,1)S(1)}, bf16[2,96,1024]{2,1,0:T(8,128)(2,1)S(1)}, u32[]{:S(2)}, u32[]{:S(2)}) collective-permute-start(bf16[2,96,1024]{2,1,0:T(8,128)(2,1)S(1)} %pad_maximum_fusion.3), channel_id=1, source_target_pairs={{0,1},{1,0},{2,3},{3,2},{4,5},{5,4},{6,7},{7,6},{8,9},{9,8},{10,11... | collective-permute-start | bytes 1179656 | tf_op jit(solution)/shard_map/ppermute | solution.py:384
  36.6 0.6 collective-permute-start.3
  37.2 2.4 %collective-permute-start.25 = (bf16[96,1024]{1,0:T(8,128)(2,1)S(1)}, bf16[96,1024]{1,0:T(8,128)(2,1)S(1)}, u32[]{:S(2)}, u32[]{:S(2)}) collective-permute-start(bf16[96,1024]{1,0:T(8,128)(2,1)S(1)} %pad_maximum_fusion.9), channel_id=1, source_target_pairs={{0,28},{2,30},{4,24},{6,26},{8,20},{10,22},{12,16},{14,18},{16,12}... | collective-permute-start | bytes 589832 | tf_op jit(solution)/shard_map/ppermute | solution.py:387
  39.6 0.7 collective-permute-start.18
  40.4 3.2 %collective-permute-start.14 = (bf16[96,1024]{1,0:T(8,128)(2,1)S(1)}, bf16[96,1024]{1,0:T(8,128)(2,1)S(1)}, u32[]{:S(2)}, u32[]{:S(2)}) collective-permute-start(bf16[96,1024]{1,0:T(8,128)(2,1)S(1)} %pad_maximum_fusion.7), channel_id=1, source_target_pairs={{0,20},{2,22},{4,16},{6,18},{8,28},{10,30},{12,24},{14,26},{16,4},... | collective-permute-start | bytes 589832 | tf_op jit(solution)/shard_map/ppermute | solution.py:387
  43.7 4.1 %collective-permute-done.25.refs_1_ = bf16[96,1024]{1,0:T(8,128)(2,1)S(1)} collective-permute-done((bf16[96,1024]{1,0:T(8,128)(2,1)S(1)}, bf16[96,1024]{1,0:T(8,128)(2,1)S(1)}, u32[]{:S(2)}, u32[]{:S(2)}) %collective-permute-start.25) | collective-permute-done | bytes 196640 | tf_op jit(solution)/shard_map/ppermute | solution.py:387
  47.8 0.5 collective-permute-start.26
  48.3 2.8 %collective-permute-done.3.refs_2_ = bf16[2,96,1024]{2,1,0:T(8,128)(2,1)S(1)} collective-permute-done((bf16[2,96,1024]{2,1,0:T(8,128)(2,1)S(1)}, bf16[2,96,1024]{2,1,0:T(8,128)(2,1)S(1)}, u32[]{:S(2)}, u32[]{:S(2)}) %collective-permute-start.3) | collective-permute-done | bytes 393248 | tf_op jit(solution)/shard_map/ppermute | solution.py:387
  51.2 4.5 %shard_map.117 = (bf16[2,96,1024]{2,1,0:T(8,128)(2,1)S(1)}, bf16[2,96,1024]{2,1,0:T(8,128)(2,1)S(1)}, bf16[2,96,1024]{2,1,0:T(8,128)(2,1)S(1)}, bf16[96,1024]{1,0:T(8,128)(2,1)S(1)}, bf16[1,96,1024]{2,1,0:T(8,128)(2,1)S(1)}) custom-call(s32[2]{0:T(128)S(1)} %pad_add_fusion.refs_0_, bf16[2,96,1024]{2,1,0:T(8,128)(2,1)S(1)} %pad_maximum_fusion.1.refs_1_, ...), custom_call_target="tpu_custom_call" | custom-call | flops 3321888768 | bytes 20447232 | tf_op jit(solution)/shard_map/pallas_call | solution.py:60
  55.8 0.6 collective-permute-start.9
  56.4 9.4 %collective-permute-start.10 = (bf16[2,96,1024]{2,1,0:T(8,128)(2,1)S(1)}, bf16[2,96,1024]{2,1,0:T(8,128)(2,1)S(1)}, u32[]{:S(2)}, u32[]{:S(2)}) collective-permute-start(bf16[2,96,1024]{2,1,0:T(8,128)(2,1)S(1)} %get-tuple-element.51), channel_id=1, source_target_pairs={{0,12},{2,14},{4,8},{6,10},{8,4},{10,6},{12,0},{14,2},{16,28},{18,... | collective-permute-start | bytes 1179656 | tf_op jit(solution)/shard_map/ppermute | solution.py:387
  65.8 4.6 %shard_map.118 = (f32[2,128,1024]{2,1,0:T(8,128)S(1)}, f32[2,128,1024]{2,1,0:T(8,128)S(1)}) custom-call(s32[2]{0:T(128)S(1)} %pad_add_fusion.refs_0_, bf16[128,1024]{1,0:T(8,128)(2,1)S(1)} %get-tuple-element.39.refs_1_, bf16[128,1024]{1,0:T(8,128)(2,1)S(1)} %get-tuple-element.40.refs_2_, bf16[128,1024]{1,0:T(8,128)(2,1)S(1)} %collective-permute-done.refs_5_.refs_3_, ...), custom_call_target="tpu_custom_call" | custom-call | flops 2214592512 | bytes 11796480 | tf_op jit(solution)/shard_map/pallas_call | solution.py:60
  70.4 1.6 %collective-permute-start.19 = (bf16[1,96,1024]{2,1,0:T(8,128)(2,1)S(1)}, bf16[1,96,1024]{2,1,0:T(8,128)(2,1)S(1)}, u32[]{:S(2)}, u32[]{:S(2)}) collective-permute-start(bf16[1,96,1024]{2,1,0:T(8,128)(2,1)S(1)} %bitcast.65), channel_id=1, source_target_pairs={{0,1},{1,0},{2,3},{3,2},{4,5},{5,4},{6,7},{7,6},{8,9},{9,8},{10,11... | collective-permute-start | bytes 589832 | tf_op jit(solution)/shard_map/ppermute | solution.py:384
  72.0 0.5 collective-permute-start.15
  72.8 3.5 %shard_map.122 = (bf16[96,1024]{1,0:T(8,128)(2,1)S(1)}, bf16[1,96,1024]{2,1,0:T(8,128)(2,1)S(1)}) custom-call(s32[2]{0:T(128)S(1)} %pad_add_fusion.refs_0_, bf16[96,1024]{1,0:T(8,128)(2,1)S(1)} %collective-permute-done.25.refs_1_, bf16[1,96,1024]{2,1,0:T(8,128)(2,1)S(1)} %collective-permute-done.26.refs_2_, bf16[704,2048]{1,0:T(8,128)(2,1)S(1)} %bitcast.47, ...), custom_call_target="tpu_custom_call" | custom-call | flops 830472192 | bytes 18087936 | tf_op jit(solution)/shard_map/pallas_call | solution.py:60
  76.3 1.8 %collective-permute-done.19.refs_2_ = bf16[1,96,1024]{2,1,0:T(8,128)(2,1)S(1)} collective-permute-done((bf16[1,96,1024]{2,1,0:T(8,128)(2,1)S(1)}, bf16[1,96,1024]{2,1,0:T(8,128)(2,1)S(1)}, u32[]{:S(2)}, u32[]{:S(2)}) %collective-permute-start.19) | collective-permute-done | bytes 196640 | tf_op jit(solution)/shard_map/ppermute | solution.py:384
  78.1 1.5 %collective-permute-start.27 = (bf16[1,96,1024]{2,1,0:T(8,128)(2,1)S(1)}, bf16[1,96,1024]{2,1,0:T(8,128)(2,1)S(1)}, u32[]{:S(2)}, u32[]{:S(2)}) collective-permute-start(bf16[1,96,1024]{2,1,0:T(8,128)(2,1)S(1)} %get-tuple-element.67), channel_id=1, source_target_pairs={{0,1},{1,0},{2,3},{3,2},{4,5},{5,4},{6,7},{7,6},{8,9},{9,8},{10,11... | collective-permute-start | bytes 589832 | tf_op jit(solution)/shard_map/ppermute | solution.py:384
  79.6 3.5 %shard_map.121 = (bf16[96,1024]{1,0:T(8,128)(2,1)S(1)}, bf16[1,96,1024]{2,1,0:T(8,128)(2,1)S(1)}) custom-call(s32[2]{0:T(128)S(1)} %pad_add_fusion.refs_0_, bf16[96,1024]{1,0:T(8,128)(2,1)S(1)} %collective-permute-done.18.refs_1_, bf16[1,96,1024]{2,1,0:T(8,128)(2,1)S(1)} %collective-permute-done.19.refs_2_, bf16[704,2048]{1,0:T(8,128)(2,1)S(1)} %bitcast.48, ...), custom_call_target="tpu_custom_call" | custom-call | flops 830472192 | bytes 18087936 | tf_op jit(solution)/shard_map/pallas_call | solution.py:60
  83.1 0.6 collective-permute-start.20
  83.8 0.7 collective-permute-done.27
  84.6 3.4 %collective-permute-start.28 = (bf16[96,1024]{1,0:T(8,128)(2,1)S(1)}, bf16[96,1024]{1,0:T(8,128)(2,1)S(1)}, u32[]{:S(2)}, u32[]{:S(2)}) collective-permute-start(bf16[96,1024]{1,0:T(8,128)(2,1)S(1)} %fusion), channel_id=1, source_target_pairs={{0,28},{2,30},{4,24},{6,26},{8,20},{10,22},{12,16},{14,18},{16,12}... | collective-permute-start | bytes 589832 | tf_op jit(solution)/shard_map/ppermute | solution.py:387
  88.0 1.5 %collective-permute-start.23 = (bf16[1,96,1024]{2,1,0:T(8,128)(2,1)S(1)}, bf16[1,96,1024]{2,1,0:T(8,128)(2,1)S(1)}, u32[]{:S(2)}, u32[]{:S(2)}) collective-permute-start(bf16[1,96,1024]{2,1,0:T(8,128)(2,1)S(1)} %get-tuple-element.64), channel_id=1, source_target_pairs={{0,1},{1,0},{2,3},{3,2},{4,5},{5,4},{6,7},{7,6},{8,9},{9,8},{10,11... | collective-permute-start | bytes 589832 | tf_op jit(solution)/shard_map/ppermute | solution.py:384
  89.5 3.4 %shard_map.120 = (bf16[96,1024]{1,0:T(8,128)(2,1)S(1)}, bf16[96,1024]{1,0:T(8,128)(2,1)S(1)}, bf16[2,96,1024]{2,1,0:T(8,128)(2,1)S(1)}) custom-call(s32[2]{0:T(128)S(1)} %pad_add_fusion.refs_0_, bf16[2,96,1024]{2,1,0:T(8,128)(2,1)S(1)} %collective-permute-done.13.refs_1_, bf16[96,1024]{1,0:T(8,128)(2,1)S(1)} %collective-permute-done.14.refs_2_, ...), custom_call_target="tpu_custom_call" | custom-call | flops 1660944384 | bytes 18874368 | tf_op jit(solution)/shard_map/pallas_call | solution.py:60
  93.0 0.6 collective-permute-start.16
  93.6 0.5 collective-permute-done.28.refs_8_
  94.0 2.5 %collective-permute-start.21 = (bf16[96,1024]{1,0:T(8,128)(2,1)S(1)}, bf16[96,1024]{1,0:T(8,128)(2,1)S(1)}, u32[]{:S(2)}, u32[]{:S(2)}) collective-permute-start(bf16[96,1024]{1,0:T(8,128)(2,1)S(1)} %fusion.3), channel_id=1, source_target_pairs={{0,16},{2,18},{4,20},{6,22},{8,24},{10,26},{12,28},{14,30},{16,0},... | collective-permute-start | bytes 589832 | tf_op jit(solution)/shard_map/ppermute | solution.py:387
  96.6 2.5 %collective-permute-start.24 = (bf16[96,1024]{1,0:T(8,128)(2,1)S(1)}, bf16[96,1024]{1,0:T(8,128)(2,1)S(1)}, u32[]{:S(2)}, u32[]{:S(2)}) collective-permute-start(bf16[96,1024]{1,0:T(8,128)(2,1)S(1)} %fusion.1), channel_id=1, source_target_pairs={{0,24},{2,26},{4,28},{6,30},{8,16},{10,18},{12,20},{14,22},{16,8},... | collective-permute-start | bytes 589832 | tf_op jit(solution)/shard_map/ppermute | solution.py:387
  99.1 1.8 %shard_map.119 = (f32[2,128,1024]{2,1,0:T(8,128)S(1)}, bf16[2,128,1024]{2,1,0:T(8,128)(2,1)S(1)}) custom-call(s32[2]{0:T(128)S(1)} %pad_add_fusion.refs_0_, bf16[512,288]{1,0:T(8,128)(2,1)S(1)} %get-tuple-element.38.refs_1_, bf16[2,96,1024]{2,1,0:T(8,128)(2,1)S(1)} %collective-permute-done.8.refs_2_, ...), custom_call_target="tpu_custom_call" | custom-call | flops 603979776 | bytes 6324224 | tf_op jit(solution)/shard_map/pallas_call | solution.py:60
  100.9 1.6 %collective-permute-start.12 = (bf16[2,128,1024]{2,1,0:T(8,128)(2,1)S(1)}, bf16[2,128,1024]{2,1,0:T(8,128)(2,1)S(1)}, u32[]{:S(2)}, u32[]{:S(2)}) collective-permute-start(bf16[2,128,1024]{2,1,0:T(8,128)(2,1)S(1)} %get-tuple-element.55), channel_id=1, source_target_pairs={{0,1},{1,0},{2,3},{3,2},{4,5},{5,4},{6,7},{7,6},{8,9},{9,8},{10,11... | collective-permute-start | bytes 1572872 | tf_op jit(solution)/shard_map/ppermute | solution.py:384
  102.7 6.8 %collective-permute-done.21.refs_5_ = bf16[96,1024]{1,0:T(8,128)(2,1)S(1)} collective-permute-done((bf16[96,1024]{1,0:T(8,128)(2,1)S(1)}, bf16[96,1024]{1,0:T(8,128)(2,1)S(1)}, u32[]{:S(2)}, u32[]{:S(2)}) %collective-permute-start.21) | collective-permute-done | bytes 196640 | tf_op jit(solution)/shard_map/ppermute | solution.py:387
  109.6 1.6 %collective-permute-start.22 = (bf16[96,1024]{1,0:T(8,128)(2,1)S(1)}, bf16[96,1024]{1,0:T(8,128)(2,1)S(1)}, u32[]{:S(2)}, u32[]{:S(2)}) collective-permute-start(bf16[96,1024]{1,0:T(8,128)(2,1)S(1)} %get-tuple-element.79), channel_id=1, source_target_pairs={{0,20},{2,22},{4,16},{6,18},{8,28},{10,30},{12,24},{14,26},{16,4},... | collective-permute-start | bytes 589832 | tf_op jit(solution)/shard_map/ppermute | solution.py:387
  111.2 0.5 collective-permute-start.32
  111.7 1.9 %collective-permute-done.17.refs_4_ = bf16[96,1024]{1,0:T(8,128)(2,1)S(1)} collective-permute-done((bf16[96,1024]{1,0:T(8,128)(2,1)S(1)}, bf16[96,1024]{1,0:T(8,128)(2,1)S(1)}, u32[]{:S(2)}, u32[]{:S(2)}) %collective-permute-start.17) | collective-permute-done | bytes 196640 | tf_op jit(solution)/shard_map/ppermute | solution.py:387
  113.7 9.3 %collective-permute-done.22.refs_6_ = bf16[96,1024]{1,0:T(8,128)(2,1)S(1)} collective-permute-done((bf16[96,1024]{1,0:T(8,128)(2,1)S(1)}, bf16[96,1024]{1,0:T(8,128)(2,1)S(1)}, u32[]{:S(2)}, u32[]{:S(2)}) %collective-permute-start.22) | collective-permute-done | bytes 196640 | tf_op jit(solution)/shard_map/ppermute | solution.py:387
  123.0 1.4 %collective-permute-done.31.refs_11_ = bf16[96,1024]{1,0:T(8,128)(2,1)S(1)} collective-permute-done((bf16[96,1024]{1,0:T(8,128)(2,1)S(1)}, bf16[96,1024]{1,0:T(8,128)(2,1)S(1)}, u32[]{:S(2)}, u32[]{:S(2)}) %collective-permute-start.31) | collective-permute-done | bytes 196640 | tf_op jit(solution)/shard_map/ppermute | solution.py:387
  124.4 2.0 %shard_map.123 = (bf16[128,1024]{1,0:T(8,128)(2,1)}, bf16[128,1024]{1,0:T(8,128)(2,1)}) custom-call(s32[2]{0:T(128)S(1)} %pad_add_fusion.refs_0_, bf16[512,480]{1,0:T(8,128)(2,1)S(1)} %get-tuple-element.37.refs_1_, f32[2,128,1024]{2,1,0:T(8,128)S(1)} %get-tuple-element.54.refs_2_, bf16[2,128,1024]{2,1,0:T(8,128)(2,1)S(1)} %collective-permute-done.12.refs_3_, ...), custom_call_target="tpu_custom_call" | custom-call | flops 503316480 | bytes 4554752 | tf_op jit(solution)/shard_map/pallas_call | solution.py:60
  (61 shorter events, 1.4 us)
Async XLA Ops:
  3.0 17.0 %collective-permute-start.4 = (bf16[240,1024]{1,0:T(8,128)(2,1)S(1)}, bf16[240,1024]{1,0:T(8,128)(2,1)S(1)}, u32[]{:S(2)}, u32[]{:S(2)}) collective-permute-start(bf16[240,1024]{1,0:T(8,128)(2,1)S(1)} %get-tuple-element.44), channel_id=1, source_target_pairs={{0,2},{2,0},{4,6},{6,4},{8,10},{10,8},{12,14},{14,12},{16,18},{18,... | collective-permute-start | bytes 1474568 | tf_op jit(solution)/shard_map/ppermute | solution.py:387
  3.5 10.0 %collective-permute-start = (bf16[128,1024]{1,0:T(8,128)(2,1)}, bf16[128,1024]{1,0:T(8,128)(2,1)S(1)}, u32[]{:S(2)}, u32[]{:S(2)}) collective-permute-start(bf16[128,1024]{1,0:T(8,128)(2,1)} %refs_3_.1), channel_id=1, source_target_pairs={{0,1},{1,0},{2,3},{3,2},{4,5},{5,4},{6,7},{7,6},{8,9},{9,8},{10,11... | collective-permute-start | bytes 786440 | tf_op jit(solution)/shard_map/ppermute | solution.py:384
  6.1 12.7 %collective-permute-start.1 = (bf16[128,1024]{1,0:T(8,128)(2,1)}, bf16[128,1024]{1,0:T(8,128)(2,1)S(1)}, u32[]{:S(2)}, u32[]{:S(2)}) collective-permute-start(bf16[128,1024]{1,0:T(8,128)(2,1)} %refs_4_.1), channel_id=1, source_target_pairs={{0,1},{1,0},{2,3},{3,2},{4,5},{5,4},{6,7},{7,6},{8,9},{9,8},{10,11... | collective-permute-start | bytes 786440 | tf_op jit(solution)/shard_map/ppermute | solution.py:384
  18.8 32.3 %copy-start.2 = (bf16[1,704,2048]{2,1,0:T(8,128)(2,1)S(1)}, bf16[1,704,2048]{2,1,0:T(8,128)(2,1)}, u32[]{:S(2)}) copy-start(bf16[1,704,2048]{2,1,0:T(8,128)(2,1)} %param.19) | copy-start | bytes 8650756
  19.8 16.6 %collective-permute-start.2 = (bf16[3,2,48,1024]{3,2,1,0:T(8,128)(2,1)S(1)}, bf16[3,2,48,1024]{3,2,1,0:T(8,128)(2,1)S(1)}, u32[]{:S(2)}, u32[]{:S(2)}) collective-permute-start(bf16[3,2,48,1024]{3,2,1,0:T(8,128)(2,1)S(1)} %get-tuple-element.42), channel_id=1, source_target_pairs={{0,2},{2,0},{4,6},{6,4},{8,10},{10,8},{12,14},{14,12},{16,18},{18,... | collective-permute-start | bytes 1769480 | tf_op jit(solution)/shard_map/ppermute | solution.py:387
  20.0 8.3 %collective-permute-start.5 = (bf16[96,1024]{1,0:T(8,128)(2,1)S(1)}, bf16[96,1024]{1,0:T(8,128)(2,1)S(1)}, u32[]{:S(2)}, u32[]{:S(2)}) collective-permute-start(bf16[96,1024]{1,0:T(8,128)(2,1)S(1)} %pad_maximum_fusion.5), channel_id=1, source_target_pairs={{0,12},{2,14},{4,8},{6,10},{8,4},{10,6},{12,0},{14,2},{16,28},{18,... | collective-permute-start | bytes 589832 | tf_op jit(solution)/shard_map/ppermute | solution.py:387
  22.8 12.0 %collective-permute-start.6 = (bf16[96,1024]{1,0:T(8,128)(2,1)S(1)}, bf16[96,1024]{1,0:T(8,128)(2,1)S(1)}, u32[]{:S(2)}, u32[]{:S(2)}) collective-permute-start(bf16[96,1024]{1,0:T(8,128)(2,1)S(1)} %pad_maximum_fusion.6), channel_id=1, source_target_pairs={{0,24},{2,26},{4,28},{6,30},{8,16},{10,18},{12,20},{14,22},{16,8},... | collective-permute-start | bytes 589832 | tf_op jit(solution)/shard_map/ppermute | solution.py:387
  25.4 25.8 %copy-start = (bf16[1,704,2048]{2,1,0:T(8,128)(2,1)S(1)}, bf16[1,704,2048]{2,1,0:T(8,128)(2,1)}, u32[]{:S(2)}) copy-start(bf16[1,704,2048]{2,1,0:T(8,128)(2,1)} %param.17) | copy-start | bytes 8650756
  25.4 25.8 %copy-start.1 = (bf16[1,704,2048]{2,1,0:T(8,128)(2,1)S(1)}, bf16[1,704,2048]{2,1,0:T(8,128)(2,1)}, u32[]{:S(2)}) copy-start(bf16[1,704,2048]{2,1,0:T(8,128)(2,1)} %param.18) | copy-start | bytes 8650756
  34.9 13.4 %collective-permute-start.7 = (bf16[2,96,1024]{2,1,0:T(8,128)(2,1)S(1)}, bf16[2,96,1024]{2,1,0:T(8,128)(2,1)S(1)}, u32[]{:S(2)}, u32[]{:S(2)}) collective-permute-start(bf16[2,96,1024]{2,1,0:T(8,128)(2,1)S(1)} %pad_maximum_fusion.3), channel_id=1, source_target_pairs={{0,1},{1,0},{2,3},{3,2},{4,5},{5,4},{6,7},{7,6},{8,9},{9,8},{10,11... | collective-permute-start | bytes 1179656 | tf_op jit(solution)/shard_map/ppermute | solution.py:384
  36.6 14.6 %collective-permute-start.3 = (bf16[2,96,1024]{2,1,0:T(8,128)(2,1)S(1)}, bf16[2,96,1024]{2,1,0:T(8,128)(2,1)S(1)}, u32[]{:S(2)}, u32[]{:S(2)}) collective-permute-start(bf16[2,96,1024]{2,1,0:T(8,128)(2,1)S(1)} %pad_maximum_fusion.2), channel_id=1, source_target_pairs={{0,4},{2,6},{4,0},{6,2},{8,12},{10,14},{12,8},{14,10},{16,20},{18,... | collective-permute-start | bytes 1179656 | tf_op jit(solution)/shard_map/ppermute | solution.py:387
  37.2 10.6 %collective-permute-start.25 = (bf16[96,1024]{1,0:T(8,128)(2,1)S(1)}, bf16[96,1024]{1,0:T(8,128)(2,1)S(1)}, u32[]{:S(2)}, u32[]{:S(2)}) collective-permute-start(bf16[96,1024]{1,0:T(8,128)(2,1)S(1)} %pad_maximum_fusion.9), channel_id=1, source_target_pairs={{0,28},{2,30},{4,24},{6,26},{8,20},{10,22},{12,16},{14,18},{16,12}... | collective-permute-start | bytes 589832 | tf_op jit(solution)/shard_map/ppermute | solution.py:387
  39.6 30.7 %collective-permute-start.18 = (bf16[96,1024]{1,0:T(8,128)(2,1)S(1)}, bf16[96,1024]{1,0:T(8,128)(2,1)S(1)}, u32[]{:S(2)}, u32[]{:S(2)}) collective-permute-start(bf16[96,1024]{1,0:T(8,128)(2,1)S(1)} %pad_maximum_fusion.8), channel_id=1, source_target_pairs={{0,16},{2,18},{4,20},{6,22},{8,24},{10,26},{12,28},{14,30},{16,0},... | collective-permute-start | bytes 589832 | tf_op jit(solution)/shard_map/ppermute | solution.py:387
  40.4 31.6 %collective-permute-start.14 = (bf16[96,1024]{1,0:T(8,128)(2,1)S(1)}, bf16[96,1024]{1,0:T(8,128)(2,1)S(1)}, u32[]{:S(2)}, u32[]{:S(2)}) collective-permute-start(bf16[96,1024]{1,0:T(8,128)(2,1)S(1)} %pad_maximum_fusion.7), channel_id=1, source_target_pairs={{0,20},{2,22},{4,16},{6,18},{8,28},{10,30},{12,24},{14,26},{16,4},... | collective-permute-start | bytes 589832 | tf_op jit(solution)/shard_map/ppermute | solution.py:387
  47.8 24.7 %collective-permute-start.26 = (bf16[1,96,1024]{2,1,0:T(8,128)(2,1)S(1)}, bf16[1,96,1024]{2,1,0:T(8,128)(2,1)S(1)}, u32[]{:S(2)}, u32[]{:S(2)}) collective-permute-start(bf16[1,96,1024]{2,1,0:T(8,128)(2,1)S(1)} %bitcast.66), channel_id=1, source_target_pairs={{0,1},{1,0},{2,3},{3,2},{4,5},{5,4},{6,7},{7,6},{8,9},{9,8},{10,11... | collective-permute-start | bytes 589832 | tf_op jit(solution)/shard_map/ppermute | solution.py:384
  51.2 14.6 %copy-start.3 = (bf16[704,2048]{1,0:T(8,128)(2,1)S(1)}, bf16[704,2048]{1,0:T(8,128)(2,1)}, u32[]{:S(2)}) copy-start(bf16[704,2048]{1,0:T(8,128)(2,1)} %refs_5_.1) | copy-start | bytes 8650756
  51.2 14.6 %copy-start.4 = (bf16[704,2048]{1,0:T(8,128)(2,1)S(1)}, bf16[704,2048]{1,0:T(8,128)(2,1)}, u32[]{:S(2)}) copy-start(bf16[704,2048]{1,0:T(8,128)(2,1)} %refs_6_.1) | copy-start | bytes 8650756
  51.2 14.6 %copy-start.5 = (bf16[704,2048]{1,0:T(8,128)(2,1)S(1)}, bf16[704,2048]{1,0:T(8,128)(2,1)}, u32[]{:S(2)}) copy-start(bf16[704,2048]{1,0:T(8,128)(2,1)} %refs_7_.1) | copy-start | bytes 8650756
  55.8 27.3 %collective-permute-start.9 = (bf16[2,96,1024]{2,1,0:T(8,128)(2,1)S(1)}, bf16[2,96,1024]{2,1,0:T(8,128)(2,1)S(1)}, u32[]{:S(2)}, u32[]{:S(2)}) collective-permute-start(bf16[2,96,1024]{2,1,0:T(8,128)(2,1)S(1)} %get-tuple-element.50), channel_id=1, source_target_pairs={{0,4},{2,6},{4,0},{6,2},{8,12},{10,14},{12,8},{14,10},{16,20},{18,... | collective-permute-start | bytes 1179656 | tf_op jit(solution)/shard_map/ppermute | solution.py:387
  56.4 27.3 %collective-permute-start.10 = (bf16[2,96,1024]{2,1,0:T(8,128)(2,1)S(1)}, bf16[2,96,1024]{2,1,0:T(8,128)(2,1)S(1)}, u32[]{:S(2)}, u32[]{:S(2)}) collective-permute-start(bf16[2,96,1024]{2,1,0:T(8,128)(2,1)S(1)} %get-tuple-element.51), channel_id=1, source_target_pairs={{0,12},{2,14},{4,8},{6,10},{8,4},{10,6},{12,0},{14,2},{16,28},{18,... | collective-permute-start | bytes 1179656 | tf_op jit(solution)/shard_map/ppermute | solution.py:387
  70.4 7.7 %collective-permute-start.19 = (bf16[1,96,1024]{2,1,0:T(8,128)(2,1)S(1)}, bf16[1,96,1024]{2,1,0:T(8,128)(2,1)S(1)}, u32[]{:S(2)}, u32[]{:S(2)}) collective-permute-start(bf16[1,96,1024]{2,1,0:T(8,128)(2,1)S(1)} %bitcast.65), channel_id=1, source_target_pairs={{0,1},{1,0},{2,3},{3,2},{4,5},{5,4},{6,7},{7,6},{8,9},{9,8},{10,11... | collective-permute-start | bytes 589832 | tf_op jit(solution)/shard_map/ppermute | solution.py:384
  72.0 16.0 %collective-permute-start.15 = (bf16[1,96,1024]{2,1,0:T(8,128)(2,1)S(1)}, bf16[1,96,1024]{2,1,0:T(8,128)(2,1)S(1)}, u32[]{:S(2)}, u32[]{:S(2)}) collective-permute-start(bf16[1,96,1024]{2,1,0:T(8,128)(2,1)S(1)} %bitcast.64), channel_id=1, source_target_pairs={{0,1},{1,0},{2,3},{3,2},{4,5},{5,4},{6,7},{7,6},{8,9},{9,8},{10,11... | collective-permute-start | bytes 589832 | tf_op jit(solution)/shard_map/ppermute | solution.py:384
  72.5 17.0 %collective-permute-start.13 = (bf16[2,96,1024]{2,1,0:T(8,128)(2,1)S(1)}, bf16[2,96,1024]{2,1,0:T(8,128)(2,1)S(1)}, u32[]{:S(2)}, u32[]{:S(2)}) collective-permute-start(bf16[2,96,1024]{2,1,0:T(8,128)(2,1)S(1)} %pad_maximum_fusion.4), channel_id=1, source_target_pairs={{0,8},{2,10},{4,12},{6,14},{8,0},{10,2},{12,4},{14,6},{16,24},{18,... | collective-permute-start | bytes 1179656 | tf_op jit(solution)/shard_map/ppermute | solution.py:387
  78.1 6.5 %collective-permute-start.27 = (bf16[1,96,1024]{2,1,0:T(8,128)(2,1)S(1)}, bf16[1,96,1024]{2,1,0:T(8,128)(2,1)S(1)}, u32[]{:S(2)}, u32[]{:S(2)}) collective-permute-start(bf16[1,96,1024]{2,1,0:T(8,128)(2,1)S(1)} %get-tuple-element.67), channel_id=1, source_target_pairs={{0,1},{1,0},{2,3},{3,2},{4,5},{5,4},{6,7},{7,6},{8,9},{9,8},{10,11... | collective-permute-start | bytes 589832 | tf_op jit(solution)/shard_map/ppermute | solution.py:384
  83.1 10.4 %collective-permute-start.20 = (bf16[1,96,1024]{2,1,0:T(8,128)(2,1)S(1)}, bf16[1,96,1024]{2,1,0:T(8,128)(2,1)S(1)}, u32[]{:S(2)}, u32[]{:S(2)}) collective-permute-start(bf16[1,96,1024]{2,1,0:T(8,128)(2,1)S(1)} %get-tuple-element.61), channel_id=1, source_target_pairs={{0,1},{1,0},{2,3},{3,2},{4,5},{5,4},{6,7},{7,6},{8,9},{9,8},{10,11... | collective-permute-start | bytes 589832 | tf_op jit(solution)/shard_map/ppermute | solution.py:384
  83.7 15.4 %collective-permute-start.11 = (bf16[2,2,96,1024]{3,2,1,0:T(8,128)(2,1)S(1)}, bf16[2,2,96,1024]{3,2,1,0:T(8,128)(2,1)S(1)}, u32[]{:S(2)}, u32[]{:S(2)}) collective-permute-start(bf16[2,2,96,1024]{3,2,1,0:T(8,128)(2,1)S(1)} %pad_maximum_fusion), channel_id=1, source_target_pairs={{0,2},{2,0},{4,6},{6,4},{8,10},{10,8},{12,14},{14,12},{16,18},{18,... | collective-permute-start | bytes 2359304 | tf_op jit(solution)/shard_map/ppermute | solution.py:387
  84.6 9.4 %collective-permute-start.28 = (bf16[96,1024]{1,0:T(8,128)(2,1)S(1)}, bf16[96,1024]{1,0:T(8,128)(2,1)S(1)}, u32[]{:S(2)}, u32[]{:S(2)}) collective-permute-start(bf16[96,1024]{1,0:T(8,128)(2,1)S(1)} %fusion), channel_id=1, source_target_pairs={{0,28},{2,30},{4,24},{6,26},{8,20},{10,22},{12,16},{14,18},{16,12}... | collective-permute-start | bytes 589832 | tf_op jit(solution)/shard_map/ppermute | solution.py:387
  88.0 8.5 %collective-permute-start.23 = (bf16[1,96,1024]{2,1,0:T(8,128)(2,1)S(1)}, bf16[1,96,1024]{2,1,0:T(8,128)(2,1)S(1)}, u32[]{:S(2)}, u32[]{:S(2)}) collective-permute-start(bf16[1,96,1024]{2,1,0:T(8,128)(2,1)S(1)} %get-tuple-element.64), channel_id=1, source_target_pairs={{0,1},{1,0},{2,3},{3,2},{4,5},{5,4},{6,7},{7,6},{8,9},{9,8},{10,11... | collective-permute-start | bytes 589832 | tf_op jit(solution)/shard_map/ppermute | solution.py:384
  93.0 9.6 %collective-permute-start.16 = (bf16[2,96,1024]{2,1,0:T(8,128)(2,1)S(1)}, bf16[2,96,1024]{2,1,0:T(8,128)(2,1)S(1)}, u32[]{:S(2)}, u32[]{:S(2)}) collective-permute-start(bf16[2,96,1024]{2,1,0:T(8,128)(2,1)S(1)} %get-tuple-element.58), channel_id=1, source_target_pairs={{0,1},{1,0},{2,3},{3,2},{4,5},{5,4},{6,7},{7,6},{8,9},{9,8},{10,11... | collective-permute-start | bytes 1179656 | tf_op jit(solution)/shard_map/ppermute | solution.py:384
  93.5 3.1 %collective-permute-start.8 = (bf16[2,96,1024]{2,1,0:T(8,128)(2,1)S(1)}, bf16[2,96,1024]{2,1,0:T(8,128)(2,1)S(1)}, u32[]{:S(2)}, u32[]{:S(2)}) collective-permute-start(bf16[2,96,1024]{2,1,0:T(8,128)(2,1)S(1)} %get-tuple-element.49.refs_6_), channel_id=1, source_target_pairs={{0,2},{2,0},{4,6},{6,4},{8,10},{10,8},{12,14},{14,12},{16,18},{18,... | collective-permute-start | bytes 1179656 | tf_op jit(solution)/shard_map/ppermute | solution.py:387
  94.0 15.5 %collective-permute-start.21 = (bf16[96,1024]{1,0:T(8,128)(2,1)S(1)}, bf16[96,1024]{1,0:T(8,128)(2,1)S(1)}, u32[]{:S(2)}, u32[]{:S(2)}) collective-permute-start(bf16[96,1024]{1,0:T(8,128)(2,1)S(1)} %fusion.3), channel_id=1, source_target_pairs={{0,16},{2,18},{4,20},{6,22},{8,24},{10,26},{12,28},{14,30},{16,0},... | collective-permute-start | bytes 589832 | tf_op jit(solution)/shard_map/ppermute | solution.py:387
  96.5 14.7 %collective-permute-start.33 = (bf16[96,1024]{1,0:T(8,128)(2,1)S(1)}, bf16[96,1024]{1,0:T(8,128)(2,1)S(1)}, u32[]{:S(2)}, u32[]{:S(2)}) collective-permute-start(bf16[96,1024]{1,0:T(8,128)(2,1)S(1)} %collective-permute-done.28.refs_8_), channel_id=1, source_target_pairs={{0,2},{2,0},{4,6},{6,4},{8,10},{10,8},{12,14},{14,12},{16,18},{18,... | collective-permute-start | bytes 589832 | tf_op jit(solution)/shard_map/ppermute | solution.py:387
  96.6 14.6 %collective-permute-start.24 = (bf16[96,1024]{1,0:T(8,128)(2,1)S(1)}, bf16[96,1024]{1,0:T(8,128)(2,1)S(1)}, u32[]{:S(2)}, u32[]{:S(2)}) collective-permute-start(bf16[96,1024]{1,0:T(8,128)(2,1)S(1)} %fusion.1), channel_id=1, source_target_pairs={{0,24},{2,26},{4,28},{6,30},{8,16},{10,18},{12,20},{14,22},{16,8},... | collective-permute-start | bytes 589832 | tf_op jit(solution)/shard_map/ppermute | solution.py:387
  100.9 23.5 %collective-permute-start.12 = (bf16[2,128,1024]{2,1,0:T(8,128)(2,1)S(1)}, bf16[2,128,1024]{2,1,0:T(8,128)(2,1)S(1)}, u32[]{:S(2)}, u32[]{:S(2)}) collective-permute-start(bf16[2,128,1024]{2,1,0:T(8,128)(2,1)S(1)} %get-tuple-element.55), channel_id=1, source_target_pairs={{0,1},{1,0},{2,3},{3,2},{4,5},{5,4},{6,7},{7,6},{8,9},{9,8},{10,11... | collective-permute-start | bytes 1572872 | tf_op jit(solution)/shard_map/ppermute | solution.py:384
  102.7 11.0 %collective-permute-start.17 = (bf16[96,1024]{1,0:T(8,128)(2,1)S(1)}, bf16[96,1024]{1,0:T(8,128)(2,1)S(1)}, u32[]{:S(2)}, u32[]{:S(2)}) collective-permute-start(bf16[96,1024]{1,0:T(8,128)(2,1)S(1)} %get-tuple-element.80), channel_id=1, source_target_pairs={{0,8},{2,10},{4,12},{6,14},{8,0},{10,2},{12,4},{14,6},{16,24},{18,... | collective-permute-start | bytes 589832 | tf_op jit(solution)/shard_map/ppermute | solution.py:387
  109.6 13.4 %collective-permute-start.22 = (bf16[96,1024]{1,0:T(8,128)(2,1)S(1)}, bf16[96,1024]{1,0:T(8,128)(2,1)S(1)}, u32[]{:S(2)}, u32[]{:S(2)}) collective-permute-start(bf16[96,1024]{1,0:T(8,128)(2,1)S(1)} %get-tuple-element.79), channel_id=1, source_target_pairs={{0,20},{2,22},{4,16},{6,18},{8,28},{10,30},{12,24},{14,26},{16,4},... | collective-permute-start | bytes 589832 | tf_op jit(solution)/shard_map/ppermute | solution.py:387
  111.2 11.8 %collective-permute-start.30 = (bf16[96,1024]{1,0:T(8,128)(2,1)S(1)}, bf16[96,1024]{1,0:T(8,128)(2,1)S(1)}, u32[]{:S(2)}, u32[]{:S(2)}) collective-permute-start(bf16[96,1024]{1,0:T(8,128)(2,1)S(1)} %collective-permute-done.21.refs_5_), channel_id=1, source_target_pairs={{0,2},{2,0},{4,6},{6,4},{8,10},{10,8},{12,14},{14,12},{16,18},{18,... | collective-permute-start | bytes 589832 | tf_op jit(solution)/shard_map/ppermute | solution.py:387
  111.2 11.8 %collective-permute-start.32 = (bf16[96,1024]{1,0:T(8,128)(2,1)S(1)}, bf16[96,1024]{1,0:T(8,128)(2,1)S(1)}, u32[]{:S(2)}, u32[]{:S(2)}) collective-permute-start(bf16[96,1024]{1,0:T(8,128)(2,1)S(1)} %collective-permute-done.24.refs_7_), channel_id=1, source_target_pairs={{0,2},{2,0},{4,6},{6,4},{8,10},{10,8},{12,14},{14,12},{16,18},{18,... | collective-permute-start | bytes 589832 | tf_op jit(solution)/shard_map/ppermute | solution.py:387
  113.7 9.3 %collective-permute-start.29 = (bf16[96,1024]{1,0:T(8,128)(2,1)S(1)}, bf16[96,1024]{1,0:T(8,128)(2,1)S(1)}, u32[]{:S(2)}, u32[]{:S(2)}) collective-permute-start(bf16[96,1024]{1,0:T(8,128)(2,1)S(1)} %collective-permute-done.17.refs_4_), channel_id=1, source_target_pairs={{0,2},{2,0},{4,6},{6,4},{8,10},{10,8},{12,14},{14,12},{16,18},{18,... | collective-permute-start | bytes 589832 | tf_op jit(solution)/shard_map/ppermute | solution.py:387
  123.0 1.4 %collective-permute-start.31 = (bf16[96,1024]{1,0:T(8,128)(2,1)S(1)}, bf16[96,1024]{1,0:T(8,128)(2,1)S(1)}, u32[]{:S(2)}, u32[]{:S(2)}) collective-permute-start(bf16[96,1024]{1,0:T(8,128)(2,1)S(1)} %collective-permute-done.22.refs_6_), channel_id=1, source_target_pairs={{0,2},{2,0},{4,6},{6,4},{8,10},{10,8},{12,14},{14,12},{16,18},{18,... | collective-permute-start | bytes 589832 | tf_op jit(solution)/shard_map/ppermute | solution.py:387
